TPU v7x, 256 devices: a whole 4x4x8 slice. The times are simulated.
256 devices in a mesh: row: 32 (over z, x_lo, core), col: 8 (over y, x_hi).
Axes of the slice: x: 4 (x_hi: 2, x_lo: 2; x = x_hi * 2 + x_lo), y: 4, z: 8, core: 2. Of those that a mesh axis runs over, the one named last changes fastest.
Arguments:
- matrix: float32 [8192, 4096], P('row', 'col'), may hold values from -12 to 12
Outputs:
- rotated: float32 [8192, 4096], P('row', 'col')
- coupling: float32 [2], replicated
All inputs are finite; a program needn't handle non-finite values.
Results may differ from a plain program's by a relative error of at most 0.00027.
Values sent between devices are 32-bit elements; how exact they have to be, the bound alone decides.
No kernel may reach another device: no remote copies, remote signals or barrier semaphores. Data moves between devices by JAX's collectives and lax.ppermute only.
A program may use at most 64 MiB of HBM per device.

v0:
```python
import jax
import jax.numpy as jnp
from jax import lax
from jax.sharding import Mesh
from jax.sharding import PartitionSpec as P

STEPS = 2
ROW = ("row_0", "row_1", "row_2")


def padded_to(lines, count):
    spare = -len(lines) % count
    return jnp.pad(lines, [(0, spare)] + [(0, 0)] * (lines.ndim - 1))


def copy_for_each(value, axis):
    copies = jnp.broadcast_to(value, (lax.axis_size(axis), *value.shape))
    return lax.all_to_all(copies, axis, split_axis=0, concat_axis=0, tiled=True)


def in_order(parts, dim):
    parts = jnp.moveaxis(parts, 0, dim)
    shape = parts.shape
    return parts.reshape(*shape[:dim], shape[dim] * shape[dim + 1], *shape[dim + 2 :])


def gather_axes(value, axes, dim):
    far, near = axes
    parts = copy_for_each(copy_for_each(value, far), near)
    return in_order(parts.swapaxes(0, 1).reshape(-1, *value.shape), dim)


def cut_along(value, dim, count):
    before, after = (value.shape[:dim], value.shape[dim + 1 :])
    return jnp.moveaxis(value.reshape(*before, count, -1, *after), dim, 0)


def summed_on_arrival(value, axis, dim):
    count = lax.axis_size(axis)
    parts = lax.all_to_all(cut_along(value, dim, count), axis, 0, 0, tiled=True)
    return jnp.sum(parts, axis=0)


def sum_in_two_steps(value, axes, dim):
    far, near = axes
    own = summed_on_arrival(cut_along(value, dim, lax.axis_size(far)), near, dim + 1)
    return jnp.sum(lax.all_to_all(own, far, 0, 0, tiled=True), axis=0)


def total_of(value, axes):
    lines = value.reshape(-1, value.shape[-1])
    padded = padded_to(lines, lax.axis_size(axes[0]) * lax.axis_size(axes[1]))
    whole = gather_axes(sum_in_two_steps(padded, axes, 0), axes, 0)
    return lax.slice_in_dim(whole, 0, len(lines)).reshape(value.shape)


def from_behind(value, axis, steps):
    count = lax.axis_size(axis)
    first, last = (max(0, -steps), min(count, count - steps))
    return lax.ppermute(value, axis, [(source, source + steps) for source in range(first, last)])


def gathered_copies(value, axis, dim):
    return in_order(copy_for_each(value, axis), dim)


def nested_sum(value, axes):
    lines = value.reshape(-1, value.shape[-1])
    own = summed_on_arrival(padded_to(lines, lax.axis_size(axes)), axes, 0)
    whole = gathered_copies(own, axes, 0)
    return whole[: len(lines)].reshape(value.shape)


def over_copies(value, axis):
    return copy_for_each(value, axis).sum(axis=0)


def pair_grams(pair_blocks):
    return jnp.einsum(
        "prk,prl->pkl",
        pair_blocks,
        pair_blocks,
        precision=lax.Precision.HIGHEST,
        preferred_element_type=jnp.float32,
    )


def coupling_term(pair_gram, width):
    diagonal = jnp.diagonal(pair_gram, axis1=1, axis2=2)
    cross = pair_gram[:, :width, width:]
    return jnp.sum(cross * cross / (diagonal[:, :width, None] * diagonal[:, None, width:]))


def lower_solve(second, right_side):
    return jax.scipy.linalg.solve_triangular(second, right_side, lower=True)


def body(matrix):
    row_total = matrix.shape[0]
    width = matrix.shape[1] // 2
    col_place = lax.axis_index("col")
    col_last = lax.axis_size("col") - 1
    first_col = col_place == 0
    last_col = col_place == col_last
    top_block = matrix[:, :width]
    bottom_block = matrix[:, width:]
    pair_blocks = matrix[None]
    pair_gram = total_of(pair_grams(pair_blocks), (("row_0", "row_1"), "row_2"))
    coupling_terms = []
    for step_index in range(STEPS):
        local_term = coupling_term(pair_gram, width)
        coupling_terms.append(local_term)
        lower_factor = jnp.linalg.cholesky(pair_gram)
        inner_gram = jnp.einsum(
            "pik,pil->pkl",
            lower_factor,
            lower_factor,
            precision=lax.Precision.HIGHEST,
            preferred_element_type=jnp.float32,
        )
        second = jnp.linalg.cholesky(inner_gram)
        rotation = jnp.swapaxes(lower_solve(second, jnp.swapaxes(lower_factor, 1, 2)), 1, 2)
        turned = jnp.einsum(
            "prk,pkl->prl",
            pair_blocks,
            rotation,
            precision=lax.Precision.HIGHEST,
            preferred_element_type=jnp.float32,
        )
        new_top = turned[0, :, :width]
        new_bottom = turned[0, :, width:]
        own_top = jnp.einsum(
            "pik,pil->pkl",
            second[:, :, :width],
            second[:, :, :width],
            precision=lax.Precision.HIGHEST,
            preferred_element_type=jnp.float32,
        )
        own_bottom = jnp.einsum(
            "pik,pil->pkl",
            second[:, width:, width:],
            second[:, width:, width:],
            precision=lax.Precision.HIGHEST,
            preferred_element_type=jnp.float32,
        )
        carried_top = jnp.concatenate([new_top, own_top[0]], axis=0)
        carried_bottom = jnp.concatenate([new_bottom, own_bottom[0]], axis=0)
        outgoing = jnp.where(first_col, carried_bottom, carried_top)
        arrived_top = from_behind(outgoing, "col", 1)
        arrived_bottom = from_behind(carried_bottom, "col", -1)
        top_whole = jnp.where(first_col, carried_top, arrived_top)
        bottom_whole = jnp.where(last_col, carried_top, arrived_bottom)
        top_block = top_whole[:row_total]
        bottom_block = bottom_whole[:row_total]
        pair_blocks = jnp.concatenate([top_block, bottom_block], axis=1)[None]
        if step_index + 1 < STEPS:
            cross_part = jnp.einsum(
                "prk,prl->pkl",
                top_block[None],
                bottom_block[None],
                precision=lax.Precision.HIGHEST,
                preferred_element_type=jnp.float32,
            )
            cross_total = nested_sum(cross_part, ROW)
            top_own = top_whole[row_total:][None]
            bottom_own = bottom_whole[row_total:][None]
            upper_half = jnp.concatenate([top_own, cross_total], axis=2)
            lower_half = jnp.concatenate([jnp.swapaxes(cross_total, 1, 2), bottom_own], axis=2)
            pair_gram = jnp.concatenate([upper_half, lower_half], axis=1)
    totals = over_copies(jnp.stack(coupling_terms), "col")
    coupling = jnp.sqrt(totals / (1.0 * lax.axis_size("col") * width))
    rotated = jnp.concatenate([top_block, bottom_block], axis=1)
    return (rotated, coupling)


def solution(mesh):
    split = Mesh(
        mesh.devices.reshape(8, 2, 2, mesh.shape["col"]), ("row_0", "row_1", "row_2", "col")
    )
    placed = (P(ROW, "col"),)
    return jax.shard_map(
        body, mesh=split, in_specs=placed, out_specs=(P(ROW, "col"), P()), check_vma=False
    )
```

profile of v0, /device:TPU:6, one launch (start us, length us, event | category | flops | bytes accessed | tf_op | source)
XLA Modules:
  0.0 656.2 jit_solution(7298705477561527356)
XLA Ops:
  4.1 3.6 all-to-all-start
  7.7 2.1 all-to-all-done
  9.9 26.5 %all_to_all.37 = f32[16,16,512]{2,1,0:T(8,128)S(1)} all-to-all(f32[16,16,512]{2,1,0:T(8,128)S(1)} %reduce_sum.54), channel_id=1, replica_groups=mesh['row_0'=8,'row_1'=2,'row_2'=2,'col'=8] {'row_0','row_1'}, dimensions={0} | all-to-all | bytes 1048576 | tf_op jit(solution)/shard_map/all_to_all | solution.py:47
  37.2 4.7 all-to-all-start.2
  41.9 14.9 %all-to-all-done.2 = f32[16,16,512]{2,1,0:T(8,128)S(1)} async-done(((f32[16,16,512]{2,1,0:T(8,128)}), f32[16,16,512]{2,1,0:T(8,128)S(1)}, u32[]{:S(2)}, u32[]{:S(2)}) %all-to-all-start.2) | async-done | bytes 524320 | tf_op jit(solution)/shard_map/all_to_all | solution.py:18
  57.0 4.6 all_to_all.36
  62.2 11.7 %custom-call.53 = f32[1,128,128]{2,1,0:T(8,128)S(1)} custom-call(f32[1,128,128]{2,1,0:T(8,128)S(1)} %cholesky.741), custom_call_target="Cholesky" | custom-call | tf_op jit(solution)/shard_map/jit(cholesky)/cholesky | solution.py:113
  74.0 9.8 %custom-call.54 = f32[1,1,128,128]{2,3,1,0:T(8,128)S(1)} custom-call(f32[1,1,128,128]{3,2,1,0:T(8,128)S(1)} %get-tuple-element.113), custom_call_target="InvertDiagBlocksLowerTriangular" | custom-call | tf_op jit(solution)/shard_map/jit(cholesky)/cholesky | solution.py:113
  84.6 11.7 %custom-call.55 = f32[1,128,128]{2,1,0:T(8,128)S(1)} custom-call(f32[1,128,128]{2,1,0:T(8,128)S(1)} %cholesky.745), custom_call_target="Cholesky" | custom-call | tf_op jit(solution)/shard_map/jit(cholesky)/cholesky | solution.py:113
  96.3 9.9 %custom-call.56 = f32[1,1,128,128]{2,3,1,0:T(8,128)S(1)} custom-call(f32[1,1,128,128]{3,2,1,0:T(8,128)S(1)} %get-tuple-element.110), custom_call_target="InvertDiagBlocksLowerTriangular" | custom-call | tf_op jit(solution)/shard_map/jit(cholesky)/cholesky | solution.py:113
  106.9 11.7 %custom-call.57 = f32[1,128,128]{2,1,0:T(8,128)S(1)} custom-call(f32[1,128,128]{2,1,0:T(8,128)S(1)} %cholesky.750), custom_call_target="Cholesky" | custom-call | tf_op jit(solution)/shard_map/jit(cholesky)/cholesky | solution.py:113
  119.4 9.8 %custom-call.58 = f32[1,1,128,128]{2,3,1,0:T(8,128)S(1)} custom-call(f32[1,1,128,128]{3,2,1,0:T(8,128)S(1)} %get-tuple-element.107), custom_call_target="InvertDiagBlocksLowerTriangular" | custom-call | tf_op jit(solution)/shard_map/jit(cholesky)/cholesky | solution.py:113
  129.8 11.7 %custom-call.59 = f32[1,128,128]{2,1,0:T(8,128)S(1)} custom-call(f32[1,128,128]{2,1,0:T(8,128)S(1)} %fusion.16), custom_call_target="Cholesky" | custom-call | tf_op jit(solution)/shard_map/jit(cholesky)/cholesky | solution.py:113
  146.7 1.9 fusion.39
  150.1 11.7 %custom-call.60 = f32[1,128,128]{2,1,0:T(8,128)S(1)} custom-call(f32[1,128,128]{2,1,0:T(8,128)S(1)} %cholesky.754), custom_call_target="Cholesky" | custom-call | tf_op jit(solution)/shard_map/jit(cholesky)/cholesky | solution.py:121
  162.5 9.8 %custom-call.61 = f32[1,1,128,128]{2,3,1,0:T(8,128)S(1)} custom-call(f32[1,1,128,128]{3,2,1,0:T(8,128)S(1)} %get-tuple-element.103), custom_call_target="InvertDiagBlocksLowerTriangular" | custom-call | tf_op jit(solution)/shard_map/jit(cholesky)/cholesky | solution.py:121
  173.2 12.2 %custom-call.62 = f32[1,128,128]{2,1,0:T(8,128)S(1)} custom-call(f32[1,128,128]{2,1,0:T(8,128)S(1)} %cholesky.758), custom_call_target="Cholesky" | custom-call | tf_op jit(solution)/shard_map/jit(cholesky)/cholesky | solution.py:121
  186.0 9.8 %custom-call.63 = f32[1,1,128,128]{2,3,1,0:T(8,128)S(1)} custom-call(f32[1,1,128,128]{3,2,1,0:T(8,128)S(1)} %get-tuple-element.100), custom_call_target="InvertDiagBlocksLowerTriangular" | custom-call | tf_op jit(solution)/shard_map/jit(cholesky)/cholesky | solution.py:121
  196.5 11.7 %custom-call.64 = f32[1,128,128]{2,1,0:T(8,128)S(1)} custom-call(f32[1,128,128]{2,1,0:T(8,128)S(1)} %cholesky.763), custom_call_target="Cholesky" | custom-call | tf_op jit(solution)/shard_map/jit(cholesky)/cholesky | solution.py:121
  208.9 9.8 %custom-call.65 = f32[1,1,128,128]{2,3,1,0:T(8,128)S(1)} custom-call(f32[1,1,128,128]{3,2,1,0:T(8,128)S(1)} %get-tuple-element.97), custom_call_target="InvertDiagBlocksLowerTriangular" | custom-call | tf_op jit(solution)/shard_map/jit(cholesky)/cholesky | solution.py:121
  219.3 11.9 %custom-call.66 = f32[1,128,128]{2,1,0:T(8,128)S(1)} custom-call(f32[1,128,128]{2,1,0:T(8,128)S(1)} %fusion.17), custom_call_target="Cholesky" | custom-call | tf_op jit(solution)/shard_map/jit(cholesky)/cholesky | solution.py:121
  237.6 10.4 %while.4 = (s32[]{:T(128)}, f32[512,512]{1,0:T(8,128)S(1)}, s32[4,2]{0,1:T(2,128)S(1)}, f32[4,128,128]{2,1,0:T(8,128)}, s32[]{:T(128)}) while((s32[]{:T(128)}, f32[512,512]{1,0:T(8,128)S(1)}, s32[4,2]{0,1:T(2,128)S(1)}, f32[4,128,128]{2,1,0:T(8,128)}, s32[]{:T(128)}) %tuple.88), condition=%wide.while_cond, body=%wide.while_body.sunk | while | flops 2 | bytes 132205 | solution.py:95
  238.2 2.0 bitcast_dynamic-update-slice_fusion.4
  240.8 2.0 bitcast_dynamic-update-slice_fusion.4
  243.4 2.0 bitcast_dynamic-update-slice_fusion.4
  246.0 2.0 bitcast_dynamic-update-slice_fusion.4
  248.0 40.7 %custom-call.67 = f32[4,128,128]{1,2,0:T(8,128)} custom-call(f32[4,128,128]{2,1,0:T(8,128)} %get-tuple-element.18), custom_call_target="InvertDiagBlocksLowerTriangular" | custom-call | tf_op jit(solution)/shard_map/jit(_solve_triangular)/triangular_solve | solution.py:95
  297.4 4.3 collective-permute-start
  301.8 3.1 collective-permute-start.1
  304.8 10.0 %collective-permute-done = f32[512,256]{0,1:T(8,128)S(1)} collective-permute-done((f32[512,256]{0,1:T(8,128)S(1)}, f32[512,256]{0,1:T(8,128)S(1)}, u32[]{:S(2)}, u32[]{:S(2)}) %collective-permute-start) | collective-permute-done | bytes 524320 | tf_op jit(solution)/shard_map/ppermute | solution.py:60
  314.8 12.3 %collective-permute-done.1 = f32[512,256]{0,1:T(8,128)} collective-permute-done((f32[512,256]{0,1:T(8,128)S(1)}, f32[512,256]{0,1:T(8,128)}, u32[]{:S(2)}, u32[]{:S(2)}) %collective-permute-start.1) | collective-permute-done | bytes 524320 | tf_op jit(solution)/shard_map/ppermute | solution.py:60
  329.5 5.3 all-to-all-start.4
  334.7 4.5 gather_fusion
  339.3 7.6 %all-to-all-done.4 = f32[32,8,256]{2,1,0:T(8,128)S(1)} async-done(((f32[32,8,256]{2,1,0:T(8,128)}), f32[32,8,256]{2,1,0:T(8,128)S(1)}, u32[]{:S(2)}, u32[]{:S(2)}) %all-to-all-start.4) | async-done | bytes 262176 | tf_op jit(solution)/shard_map/all_to_all | solution.py:40
  347.6 4.5 all-to-all-start.5
  354.4 9.5 %all-to-all-done.5 = f32[32,8,256]{2,1,0:T(8,128)S(1)} async-done(((f32[32,8,256]{2,1,0:T(8,128)}), f32[32,8,256]{2,1,0:T(8,128)S(1)}, u32[]{:S(2)}, u32[]{:S(2)}) %all-to-all-start.5) | async-done | bytes 262176 | tf_op jit(solution)/shard_map/all_to_all | solution.py:18
  366.3 11.7 %custom-call.68 = f32[1,128,128]{2,1,0:T(8,128)S(1)} custom-call(f32[1,128,128]{2,1,0:T(8,128)S(1)} %cholesky.767), custom_call_target="Cholesky" | custom-call | tf_op jit(solution)/shard_map/jit(cholesky)/cholesky | solution.py:113
  378.7 9.8 %custom-call.69 = f32[1,1,128,128]{2,3,1,0:T(8,128)S(1)} custom-call(f32[1,1,128,128]{3,2,1,0:T(8,128)S(1)} %get-tuple-element.93), custom_call_target="InvertDiagBlocksLowerTriangular" | custom-call | tf_op jit(solution)/shard_map/jit(cholesky)/cholesky | solution.py:113
  390.0 11.7 %custom-call.70 = f32[1,128,128]{2,1,0:T(8,128)S(1)} custom-call(f32[1,128,128]{2,1,0:T(8,128)S(1)} %cholesky.771), custom_call_target="Cholesky" | custom-call | tf_op jit(solution)/shard_map/jit(cholesky)/cholesky | solution.py:113
  402.4 9.9 %custom-call.71 = f32[1,1,128,128]{2,3,1,0:T(8,128)S(1)} custom-call(f32[1,1,128,128]{3,2,1,0:T(8,128)S(1)} %get-tuple-element.90), custom_call_target="InvertDiagBlocksLowerTriangular" | custom-call | tf_op jit(solution)/shard_map/jit(cholesky)/cholesky | solution.py:113
  414.5 13.2 %custom-call.72 = f32[1,128,128]{2,1,0:T(8,128)} custom-call(f32[1,128,128]{2,1,0:T(8,128)} %cholesky.776), custom_call_target="Cholesky" | custom-call | tf_op jit(solution)/shard_map/jit(cholesky)/cholesky | solution.py:113
  429.8 11.3 %custom-call.73 = f32[1,1,128,128]{2,3,1,0:T(8,128)} custom-call(f32[1,1,128,128]{3,2,1,0:T(8,128)} %get-tuple-element.87), custom_call_target="InvertDiagBlocksLowerTriangular" | custom-call | tf_op jit(solution)/shard_map/jit(cholesky)/cholesky | solution.py:113
  442.5 11.9 %custom-call.74 = f32[1,128,128]{2,1,0:T(8,128)S(1)} custom-call(f32[1,128,128]{2,1,0:T(8,128)S(1)} %fusion.18), custom_call_target="Cholesky" | custom-call | tf_op jit(solution)/shard_map/jit(cholesky)/cholesky | solution.py:113
  458.8 1.9 fusion.36
  462.3 11.7 %custom-call.75 = f32[1,128,128]{2,1,0:T(8,128)S(1)} custom-call(f32[1,128,128]{2,1,0:T(8,128)S(1)} %cholesky.780), custom_call_target="Cholesky" | custom-call | tf_op jit(solution)/shard_map/jit(cholesky)/cholesky | solution.py:121
  474.7 9.8 %custom-call.76 = f32[1,1,128,128]{2,3,1,0:T(8,128)S(1)} custom-call(f32[1,1,128,128]{3,2,1,0:T(8,128)S(1)} %get-tuple-element.83), custom_call_target="InvertDiagBlocksLowerTriangular" | custom-call | tf_op jit(solution)/shard_map/jit(cholesky)/cholesky | solution.py:121
  486.0 12.1 %custom-call.77 = f32[1,128,128]{2,1,0:T(8,128)S(1)} custom-call(f32[1,128,128]{2,1,0:T(8,128)S(1)} %cholesky.784), custom_call_target="Cholesky" | custom-call | tf_op jit(solution)/shard_map/jit(cholesky)/cholesky | solution.py:121
  498.8 9.8 %custom-call.78 = f32[1,1,128,128]{2,3,1,0:T(8,128)S(1)} custom-call(f32[1,1,128,128]{3,2,1,0:T(8,128)S(1)} %get-tuple-element.80), custom_call_target="InvertDiagBlocksLowerTriangular" | custom-call | tf_op jit(solution)/shard_map/jit(cholesky)/cholesky | solution.py:121
  510.8 13.2 %custom-call.79 = f32[1,128,128]{2,1,0:T(8,128)} custom-call(f32[1,128,128]{2,1,0:T(8,128)} %cholesky.789), custom_call_target="Cholesky" | custom-call | tf_op jit(solution)/shard_map/jit(cholesky)/cholesky | solution.py:121
  526.0 11.3 %custom-call.80 = f32[1,1,128,128]{2,3,1,0:T(8,128)} custom-call(f32[1,1,128,128]{3,2,1,0:T(8,128)} %get-tuple-element.77), custom_call_target="InvertDiagBlocksLowerTriangular" | custom-call | tf_op jit(solution)/shard_map/jit(cholesky)/cholesky | solution.py:121
  538.8 11.9 %custom-call.81 = f32[1,128,128]{2,1,0:T(8,128)S(1)} custom-call(f32[1,128,128]{2,1,0:T(8,128)S(1)} %fusion.19), custom_call_target="Cholesky" | custom-call | tf_op jit(solution)/shard_map/jit(cholesky)/cholesky | solution.py:121
  555.1 1.7 fusion.57
  558.1 4.5 gather_fusion.1
  562.7 11.7 %while.5 = (s32[]{:T(128)}, f32[512,512]{1,0:T(8,128)}, s32[4,2]{0,1:T(2,128)S(1)}, f32[4,128,128]{2,1,0:T(8,128)S(1)}, s32[]{:T(128)}) while((s32[]{:T(128)}, f32[512,512]{1,0:T(8,128)}, s32[4,2]{0,1:T(2,128)S(1)}, f32[4,128,128]{2,1,0:T(8,128)S(1)}, s32[]{:T(128)}) %tuple.94), condition=%wide.while_cond.clone, body=%wide.while_body.clone.sunk | while | flops 2 | bytes 131189 | solution.py:95
  563.3 2.3 bitcast_dynamic-update-slice_fusion.5
  566.3 2.3 bitcast_dynamic-update-slice_fusion.5
  569.2 2.3 bitcast_dynamic-update-slice_fusion.5
  572.1 2.2 bitcast_dynamic-update-slice_fusion.5
  574.4 39.5 %custom-call.82 = f32[4,128,128]{1,2,0:T(8,128)S(1)} custom-call(f32[4,128,128]{2,1,0:T(8,128)S(1)} %get-tuple-element.19), custom_call_target="InvertDiagBlocksLowerTriangular" | custom-call | tf_op jit(solution)/shard_map/jit(_solve_triangular)/triangular_solve | solution.py:95
  616.2 1.9 convolution_subtract_fusion
  618.5 2.4 convolution_subtract_fusion.4
  624.2 4.3 collective-permute-start.2
  628.5 3.0 collective-permute-start.3
  633.7 20.6 %all_to_all.38 = f32[8,1,2]{2,1,0:T(1,128)S(1)} all-to-all(f32[8,1,2]{2,1,0:T(1,128)S(1)} %broadcast_in_dim.42), channel_id=1, replica_groups=mesh['row_0'=8,'row_1'=2,'row_2'=2,'col'=8] {'col'}, dimensions={0} | all-to-all | bytes 128 | tf_op jit(solution)/shard_map/all_to_all | solution.py:18
  (193 shorter events, 74.9 us)
Async XLA Ops:
  0.6 1.3 copy-start.10
  4.1 5.7 all-to-all-start
  37.2 19.6 %all-to-all-start.2 = ((f32[16,16,512]{2,1,0:T(8,128)}), f32[16,16,512]{2,1,0:T(8,128)S(1)}, u32[]{:S(2)}, u32[]{:S(2)}) async-start(f32[16,16,512]{2,1,0:T(8,128)} %broadcast_in_dim.23), calls=%async_computation.2 | async-start | bytes 1048576 | tf_op jit(solution)/shard_map/all_to_all | solution.py:18
  149.1 1.0 copy-start.2
  150.1 22.3 %copy-start.3 = (f32[1,512,512]{2,1,0:T(8,128)S(1)}, f32[1,512,512]{2,1,0:T(8,128)}, u32[]{:S(2)}) copy-start(f32[1,512,512]{2,1,0:T(8,128)} %copy-done.2) | copy-start | bytes 3145732
  234.6 54.2 %copy-start.1 = (f32[1,512,512]{1,2,0:T(8,128)S(1)}, f32[1,512,512]{1,2,0:T(8,128)}, u32[]{:S(2)}) copy-start(f32[1,512,512]{1,2,0:T(8,128)} %fusion.43) | copy-start | bytes 3145732
  290.0 1.0 copy-start.16
  294.3 1.0 copy-start.11
  296.4 1.0 copy-start.13
  297.4 17.4 %collective-permute-start = (f32[512,256]{0,1:T(8,128)S(1)}, f32[512,256]{0,1:T(8,128)S(1)}, u32[]{:S(2)}, u32[]{:S(2)}) collective-permute-start(f32[512,256]{0,1:T(8,128)S(1)} %get-tuple-element.70), channel_id=1, source_target_pairs={{0,1},{1,2},{2,3},{3,4},{4,5},{5,6},{6,7},{8,9},{9,10},{10,11},{11... | collective-permute-start | bytes 1572872 | tf_op jit(solution)/shard_map/ppermute | solution.py:60
  301.8 25.4 %collective-permute-start.1 = (f32[512,256]{0,1:T(8,128)S(1)}, f32[512,256]{0,1:T(8,128)}, u32[]{:S(2)}, u32[]{:S(2)}) collective-permute-start(f32[512,256]{0,1:T(8,128)S(1)} %get-tuple-element.71), channel_id=1, source_target_pairs={{1,0},{2,1},{3,2},{4,3},{5,4},{6,5},{7,6},{9,8},{10,9},{11,10},{12... | collective-permute-start | bytes 1572872 | tf_op jit(solution)/shard_map/ppermute | solution.py:60
  329.5 17.4 %all-to-all-start.4 = ((f32[32,8,256]{2,1,0:T(8,128)}), f32[32,8,256]{2,1,0:T(8,128)S(1)}, u32[]{:S(2)}, u32[]{:S(2)}) async-start(f32[32,8,256]{2,1,0:T(8,128)} %fusion.84), calls=%async_computation.4 | async-start | bytes 524288 | tf_op jit(solution)/shard_map/all_to_all | solution.py:40
  347.6 16.2 %all-to-all-start.5 = ((f32[32,8,256]{2,1,0:T(8,128)}), f32[32,8,256]{2,1,0:T(8,128)S(1)}, u32[]{:S(2)}, u32[]{:S(2)}) async-start(f32[32,8,256]{2,1,0:T(8,128)} %broadcast_in_dim.40), calls=%async_computation.5 | async-start | bytes 524288 | tf_op jit(solution)/shard_map/all_to_all | solution.py:18
  353.6 10.4 %copy-start.8 = (f32[1,256,256]{1,2,0:T(8,128)}, f32[1,256,256]{1,2,0:T(8,128)S(1)}, u32[]{:S(2)}) copy-start(f32[1,256,256]{1,2,0:T(8,128)S(1)} %get-tuple-element.65) | copy-start | bytes 786436
  354.4 9.9 %copy-start.9 = (f32[1,256,256]{1,2,0:T(8,128)}, f32[1,256,256]{1,2,0:T(8,128)S(1)}, u32[]{:S(2)}) copy-start(f32[1,256,256]{1,2,0:T(8,128)S(1)} %get-tuple-element.67) | copy-start | bytes 786436
  364.0 0.7 copy-start.6
  389.3 0.7 copy-start.14
  461.2 1.0 copy-start.4
  462.3 22.3 %copy-start.5 = (f32[1,512,512]{2,1,0:T(8,128)S(1)}, f32[1,512,512]{2,1,0:T(8,128)}, u32[]{:S(2)}) copy-start(f32[1,512,512]{2,1,0:T(8,128)} %copy-done.4) | copy-start | bytes 3145732
  485.3 0.7 copy-start.15
  558.1 55.8 %copy-start = (f32[1,512,512]{1,2,0:T(8,128)S(1)}, f32[1,512,512]{1,2,0:T(8,128)}, u32[]{:S(2)}) copy-start(f32[1,512,512]{1,2,0:T(8,128)} %fusion.45) | copy-start | bytes 3145732
  621.0 1.0 copy-start.17
  621.0 1.0 copy-start.18
  623.0 1.0 copy-start.7
  623.0 1.0 copy-start.12
  624.2 30.7 %collective-permute-start.2 = (f32[512,256]{0,1:T(8,128)S(1)}, f32[512,256]{0,1:T(8,128)S(1)}, u32[]{:S(2)}, u32[]{:S(2)}) collective-permute-start(f32[512,256]{0,1:T(8,128)S(1)} %get-tuple-element.60), channel_id=1, source_target_pairs={{0,1},{1,2},{2,3},{3,4},{4,5},{5,6},{6,7},{8,9},{9,10},{10,11},{11... | collective-permute-start | bytes 1572872 | tf_op jit(solution)/shard_map/ppermute | solution.py:60
  628.5 26.4 %collective-permute-start.3 = (f32[512,256]{0,1:T(8,128)S(1)}, f32[512,256]{0,1:T(8,128)S(1)}, u32[]{:S(2)}, u32[]{:S(2)}) collective-permute-start(f32[512,256]{0,1:T(8,128)S(1)} %get-tuple-element.61), channel_id=1, source_target_pairs={{1,0},{2,1},{3,2},{4,3},{5,4},{6,5},{7,6},{9,8},{10,9},{11,10},{12... | collective-permute-start | bytes 1572872 | tf_op jit(solution)/shard_map/ppermute | solution.py:60
where the time goes:
time: 668 us; the launch traced here: 656 us
  other arithmetic  417 us (62%)
  waiting for transfers between devices  56.4 us (8%)
  blocking collectives  51.7 us (8%)
  local copies, waits for them, and re-layouts  49.1 us (7%)
  matrix products  37.2 us (6%)
  starting transfers between devices  32.8 us (5%)
  between operations  11.9 us (2%)
    another operation x30, other arithmetic, body(): second = jnp.linalg.cholesky(inner_gram)  164 us
    another operation x29, other arithmetic, body(): lower_factor = jnp.linalg.cholesky(pair_gram)  162 us
    another operation x5, other arithmetic, lower_solve(): return jax.scipy.linalg.solve_triangular(second, right_side, lower=True)  81.6 us
    all_to_all x1, blocking collectives, sum_in_two_steps(): return jnp.sum(lax.all_to_all(own, far, 0, 0, tiled=True), axis=0)  26.5 us
    all_to_all x2, blocking collectives, copy_for_each(): return lax.all_to_all(copies, axis, split_axis=0, concat_axis=0, tiled=True)  25.2 us
    all_to_all x2, waiting for transfers between devices, copy_for_each(): return lax.all_to_all(copies, axis, split_axis=0, concat_axis=0, tiled=True)  24.4 us
    another operation x27, local copies, waits for them, and re-layouts, lower_solve(): return jax.scipy.linalg.solve_triangular(second, right_side, lower=True)  22.7 us
    ppermute x4, waiting for transfers between devices, from_behind(): lax.ppermute(value, axis, [(source, source + steps) for source in range(f...  22.3 us
  transfers between devices with their start and end apart: 8, of which 6 were waited for; matrix products, arithmetic and copies ran while one was open for 1% of the time, Pallas kernels for 0%

commit v1 on v0

--- a/solution.py
+++ b/solution.py
@@ -1,8 +1,119 @@
 import jax
 import jax.numpy as jnp
 from jax import lax
+from jax.experimental import pallas as pl
+from jax.experimental.pallas import tpu as pltpu
 from jax.sharding import Mesh
 from jax.sharding import PartitionSpec as P
+
+HI=lax.Precision.HIGHEST
+F32=jnp.float32
+N=512; T=128
+def dot(a,b,ca,cb):
+    return lax.dot_general(a,b,(((ca,),(cb,)),((),())),precision=HI,preferred_element_type=F32)
+def spread(x): return jnp.broadcast_to(x,(8,T))
+def leaves(mats, B=4):
+    sub=lax.broadcasted_iota(jnp.int32,(8,T),0); lane=lax.broadcasted_iota(jnp.int32,(8,T),1)
+    n=len(mats); G8=T//8
+    As=[list(m) for m in mats]
+    Is=[[jnp.where(sub+8*q==lane,1.0,0.0).astype(F32) for q in range(G8)] for _ in range(n)]
+    for P in range(0,G8,B):
+        for p in range(P,P+B):
+            r0=8*p
+            qs=list(range(p,P+B))
+            C=[{q:[spread(A[q][:,r0+k:r0+k+1]) for k in range(8)] for q in qs} for A in As]
+            rd=[jnp.ones((8,T),F32) for _ in range(n)]
+            for j in range(8):
+                for a in range(n):
+                    A,I=As[a],Is[a]
+                    rinv=1.0/spread(C[a][p][j][j:j+1,:])
+                    rd[a]=jnp.where(sub==j,rinv,rd[a])
+                    rows=[spread(C[a][p][k][j:j+1,:]) for k in range(j+1,8)]
+                    ra=spread(A[p][j:j+1,:]); ri=spread(I[p][j:j+1,:])
+                    for q in qs:
+                        if q==p:
+                            if j==7: continue
+                            m=jnp.where(sub>j,C[a][q][j]*rinv,0.0)
+                        else:
+                            m=C[a][q][j]*rinv
+                        for k in range(j+1,8):
+                            C[a][q][k]=C[a][q][k]-m*rows[k-j-1]
+                        A[q]=A[q]-m*ra; I[q]=I[q]-m*ri
+            for a in range(n):
+                s=jnp.sqrt(rd[a])
+                As[a][p]=As[a][p]*s; Is[a][p]=Is[a][p]*s
+        if P+B<G8:
+            for a in range(n):
+                A,I=As[a],Is[a]
+                SA=jnp.concatenate(A[P:P+B],axis=0)
+                both=jnp.concatenate([SA,jnp.concatenate(I[P:P+B],axis=0)],axis=1)
+                upd=dot(SA[:,8*(P+B):],both,0,0)
+                for q in range(P+B,G8):
+                    o=8*(q-P-B)
+                    A[q]=A[q]-upd[o:o+8,:T]; I[q]=I[q]-upd[o:o+8,T:]
+    for a in range(n):
+        for p in range(G8):
+            As[a][p]=jnp.where(lane>=sub+8*p,As[a][p],0.0)
+    return As,Is
+def kern(g_ref,pair_ref,turned_ref,top_ref,bot_ref,cpl_ref,A,U,V,W,Bc,RT,d_ref,u_ref,i_ref):
+    A[...]=g_ref[...]
+    H=N//2
+    eye=lax.broadcasted_iota(jnp.int32,(H,H),0)==lax.broadcasted_iota(jnp.int32,(H,H),1)
+    dt=jnp.sum(jnp.where(eye,g_ref[:H,:H],0.0),axis=1,keepdims=True)
+    db=jnp.sum(jnp.where(eye,g_ref[H:,H:],0.0),axis=0,keepdims=True)
+    cr=g_ref[:H,H:]
+    cpl_ref[...]=jnp.broadcast_to(jnp.sum(jnp.sum(cr*cr/(dt*db),axis=0,keepdims=True),axis=1,keepdims=True),(8,T))
+    U[...]=jnp.zeros_like(U); V[...]=jnp.zeros_like(V)
+    d_ref[0]=g_ref[:T,:T]
+    sub=lax.broadcasted_iota(jnp.int32,(T,T),0); lane=lax.broadcasted_iota(jnp.int32,(T,T),1)
+    d_ref[1]=jnp.where(sub==lane,1.0,0.0).astype(F32)
+    def branch(t):
+        lo,hi=t*T,(t+1)*T
+        if t>=1:
+            s=t-1; sl,sh=s*T,t*T
+            V[sl:sh,sl:sh]=u_ref[1]
+            sinv=i_ref[1]
+            W[sl:sh,sl:sh]=sinv
+            if s:
+                t1=dot(V[:sl,sl:sh],W[:sl,:sl],0,0)
+                W[sl:sh,:sl]=-dot(sinv,t1,1,0)
+                W[:sl,sl:sh]=jnp.zeros((sl,T),F32)
+        if t<4:
+            U[lo:hi,lo:hi]=u_ref[0]
+            linv=i_ref[0]
+            if t<3:
+                U[lo:hi,hi:]=dot(linv,A[lo:hi,hi:],1,0)
+                d_ref[0]=A[hi:hi+T,hi:hi+T]-dot(U[lo:hi,hi:hi+T],U[lo:hi,hi:hi+T],0,0)
+            bcol=dot(U[:hi,lo:],U[lo:hi,lo:],1,1)
+            if t:
+                vcol=dot(W[:lo,:lo],bcol[:lo],1,0)
+                V[:lo,lo:hi]=vcol
+                d_ref[1]=bcol[lo:]-dot(vcol,vcol,0,0)
+            else:
+                d_ref[1]=bcol
+            for i in range(t+1,4):
+                a,b=i*T,(i+1)*T
+                A[a:b,a:]=A[a:b,a:]-dot(U[lo:hi,a:b],U[lo:hi,a:],0,0)
+        if t>=1:
+            RT[sl:sh,:]=dot(W[sl:sh,:sh],U[:sh,:],1,0)
+    def stage(t,c):
+        us,is_=leaves([[d_ref[a,8*q:8*q+8,:] for q in range(T//8)] for a in range(2)])
+        for a in range(2):
+            for q in range(T//8):
+                u_ref[a,8*q:8*q+8,:]=us[a][q]; i_ref[a,8*q:8*q+8,:]=is_[a][q]
+        for k in range(5):
+            pl.when(t==k)(lambda k=k: branch(k))
+        return c
+    lax.fori_loop(0,5,stage,0)
+    turned_ref[...]=dot(pair_ref[...],RT[...],1,1)
+    top_ref[...]=dot(V[:256,:],V[:256,:],1,1)
+    bot_ref[...]=dot(V[256:,256:],V[256:,256:],1,1)
+def step(g,pair):
+    vm=pl.BlockSpec(memory_space=pltpu.VMEM)
+    return pl.pallas_call(kern,out_shape=[jax.ShapeDtypeStruct((256,512),F32),jax.ShapeDtypeStruct((256,256),F32),jax.ShapeDtypeStruct((256,256),F32),jax.ShapeDtypeStruct((8,T),F32)],
+        in_specs=[vm,vm],out_specs=[vm]*4,
+        scratch_shapes=[pltpu.VMEM((N,N),F32)]*4+[pltpu.VMEM((N,T),F32),pltpu.VMEM((N,N),F32)]+[pltpu.VMEM((2,T,T),F32)]*3,
+        name="rotate")(g,pair)
 
 STEPS = 2
 ROW = ("row_0", "row_1", "row_2")
@@ -83,16 +194,6 @@
         precision=lax.Precision.HIGHEST,
         preferred_element_type=jnp.float32,
     )
-
-
-def coupling_term(pair_gram, width):
-    diagonal = jnp.diagonal(pair_gram, axis1=1, axis2=2)
-    cross = pair_gram[:, :width, width:]
-    return jnp.sum(cross * cross / (diagonal[:, :width, None] * diagonal[:, None, width:]))
-
-
-def lower_solve(second, right_side):
-    return jax.scipy.linalg.solve_triangular(second, right_side, lower=True)
 
 
 def body(matrix):
@@ -108,41 +209,11 @@
     pair_gram = total_of(pair_grams(pair_blocks), (("row_0", "row_1"), "row_2"))
     coupling_terms = []
     for step_index in range(STEPS):
-        local_term = coupling_term(pair_gram, width)
-        coupling_terms.append(local_term)
-        lower_factor = jnp.linalg.cholesky(pair_gram)
-        inner_gram = jnp.einsum(
-            "pik,pil->pkl",
-            lower_factor,
-            lower_factor,
-            precision=lax.Precision.HIGHEST,
-            preferred_element_type=jnp.float32,
-        )
-        second = jnp.linalg.cholesky(inner_gram)
-        rotation = jnp.swapaxes(lower_solve(second, jnp.swapaxes(lower_factor, 1, 2)), 1, 2)
-        turned = jnp.einsum(
-            "prk,pkl->prl",
-            pair_blocks,
-            rotation,
-            precision=lax.Precision.HIGHEST,
-            preferred_element_type=jnp.float32,
-        )
+        turned, own_top, own_bottom, term = step(pair_gram[0], pair_blocks[0])
+        turned, own_top, own_bottom = turned[None], own_top[None], own_bottom[None]
+        coupling_terms.append(term[0, 0])
         new_top = turned[0, :, :width]
         new_bottom = turned[0, :, width:]
-        own_top = jnp.einsum(
-            "pik,pil->pkl",
-            second[:, :, :width],
-            second[:, :, :width],
-            precision=lax.Precision.HIGHEST,
-            preferred_element_type=jnp.float32,
-        )
-        own_bottom = jnp.einsum(
-            "pik,pil->pkl",
-            second[:, width:, width:],
-            second[:, width:, width:],
-            precision=lax.Precision.HIGHEST,
-            preferred_element_type=jnp.float32,
-        )
         carried_top = jnp.concatenate([new_top, own_top[0]], axis=0)
         carried_bottom = jnp.concatenate([new_bottom, own_bottom[0]], axis=0)
         outgoing = jnp.where(first_col, carried_bottom, carried_top)

time: 668 us -> 235 us (0.35); the launches traced: 656 us -> 235 us
  other arithmetic: 417 us -> 5.28 us
  Pallas kernels: 0 us -> 74.6 us
  local copies, waits for them, and re-layouts: 49.1 us -> 9.27 us
  matrix products: 37.2 us -> 1.39 us
  blocking collectives: 51.7 us -> 71.3 us
  between operations: 11.9 us -> 0.84 us
  starting transfers between devices: 32.8 us -> 23.5 us
  waiting for transfers between devices: 56.4 us -> 48.4 us
    another operation x64 -> x0, other arithmetic: 407 us -> none  [the longest x30 164 us: body(): second = jnp.linalg.cholesky(inner_gram)]
    pallas_call x0 -> x2, Pallas kernels: none -> 74.6 us  [step(): pl.pallas_call(kern, out_shape=[jax.ShapeDtypeStruct((256, 512), F32), ja...]
    another operation x45 -> x0, local copies, waits for them, and re-layouts: 25 us -> none  [the longest x27 22.7 us: lower_solve(): return jax.scipy.linalg.solve_triangular(second, right_side, lower=True)]
    another operation x38 -> x0, matrix products: 23.9 us -> none  [the longest x14 13 us: lower_solve(): return jax.scipy.linalg.solve_triangular(second, right_side, lower=True)]
    all_to_all x0 -> x2, blocking collectives: none -> 21.2 us  [summed_on_arrival(): parts = lax.all_to_all(cut_along(value, dim, count), axis, 0, 0, tiled=True)]
    dot_general x8 -> x0, matrix products: 11.1 us -> none  [the longest x2 3.72 us: body(): jnp.einsum('pik,pil->pkl', lower_factor, lower_factor, precision=lax.Prec...]
    all_to_all x2 -> x0, waiting for transfers between devices: 9.69 us -> none  [summed_on_arrival(): parts = lax.all_to_all(cut_along(value, dim, count), axis, 0, 0, tiled=True)]
    gather x2 -> x0, local copies, waits for them, and re-layouts: 9.06 us -> none  [coupling_term(): diagonal = jnp.diagonal(pair_gram, axis1=1, axis2=2)]
  transfers between devices with their start and end apart: 8 -> 6, of which waited for: 6 -> 4; matrix products, arithmetic and copies ran while one was open for 1% -> 2% of each run, Pallas kernels for 0% -> 0%
where the time goes in v1:
time: 235 us
  Pallas kernels  74.6 us (32%)
  blocking collectives  71.3 us (30%)
  waiting for transfers between devices  48.4 us (21%)
  starting transfers between devices  23.5 us (10%)
  local copies, waits for them, and re-layouts  9.27 us (4%)
  other arithmetic  5.28 us (2%)
    pallas_call x2, Pallas kernels, step(): pl.pallas_call(kern, out_shape=[jax.ShapeDtypeStruct((256, 512), F32), ja...  74.6 us
    all_to_all x1, blocking collectives, sum_in_two_steps(): return jnp.sum(lax.all_to_all(own, far, 0, 0, tiled=True), axis=0)  26.5 us
    all_to_all x2, waiting for transfers between devices, copy_for_each(): return lax.all_to_all(copies, axis, split_axis=0, concat_axis=0, tiled=True)  26.1 us
    all_to_all x2, blocking collectives, copy_for_each(): return lax.all_to_all(copies, axis, split_axis=0, concat_axis=0, tiled=True)  23.6 us
    ppermute x4, waiting for transfers between devices, from_behind(): lax.ppermute(value, axis, [(source, source + steps) for source in range(f...  22.2 us
    all_to_all x2, blocking collectives, summed_on_arrival(): parts = lax.all_to_all(cut_along(value, dim, count), axis, 0, 0, tiled=True)  21.2 us
    ppermute x4, starting transfers between devices, from_behind(): lax.ppermute(value, axis, [(source, source + steps) for source in range(f...  14.8 us
    all_to_all x2, starting transfers between devices, copy_for_each(): return lax.all_to_all(copies, axis, split_axis=0, concat_axis=0, tiled=True)  8.78 us
  transfers between devices with their start and end apart: 6, of which 4 were waited for; matrix products, arithmetic and copies ran while one was open for 2% of the time, Pallas kernels for 0%

profile of v1, /device:TPU:6, one launch (start us, length us, event | category | flops | bytes accessed | tf_op | source)
XLA Modules:
  0.0 234.6 jit_solution(795794660490472722)
XLA Ops:
  0.6 0.0 copy-start
  0.6 1.3 copy.19
  1.9 0.0 copy-done
  2.0 1.0 convolution_bitcast_fusion
  3.0 0.1 copy.20
  3.1 4.6 %all_to_all.36 = f32[2,16,16,512]{3,2,1,0:T(8,128)S(1)} all-to-all(f32[2,16,16,512]{3,2,1,0:T(8,128)S(1)} %copy.20), channel_id=1, replica_groups=mesh['row_0'=8,'row_1'=2,'row_2'=2,'col'=8] {'row_2'}, dimensions={0} | all-to-all | bytes 2097152 | tf_op jit(solution)/shard_map/all_to_all | solution.py:151
  7.7 0.1 reduce_sum.36
  7.8 26.5 %all_to_all.37 = f32[16,16,512]{2,1,0:T(8,128)S(1)} all-to-all(f32[16,16,512]{2,1,0:T(8,128)S(1)} %reduce_sum.36), channel_id=1, replica_groups=mesh['row_0'=8,'row_1'=2,'row_2'=2,'col'=8] {'row_0','row_1'}, dimensions={0} | all-to-all | bytes 1048576 | tf_op jit(solution)/shard_map/all_to_all | solution.py:158
  34.3 0.9 broadcast_in_dim.27
  35.1 4.7 %all-to-all-start.2 = ((f32[16,16,512]{2,1,0:T(8,128)}), f32[16,16,512]{2,1,0:T(8,128)S(1)}, u32[]{:S(2)}, u32[]{:S(2)}) async-start(f32[16,16,512]{2,1,0:T(8,128)} %broadcast_in_dim.27), calls=%async_computation.2 | async-start | bytes 1048576 | tf_op jit(solution)/shard_map/all_to_all | solution.py:129
  39.8 14.9 %all-to-all-done.2 = f32[16,16,512]{2,1,0:T(8,128)S(1)} async-done(((f32[16,16,512]{2,1,0:T(8,128)}), f32[16,16,512]{2,1,0:T(8,128)S(1)}, u32[]{:S(2)}, u32[]{:S(2)}) %all-to-all-start.2) | async-done | bytes 524320 | tf_op jit(solution)/shard_map/all_to_all | solution.py:129
  54.7 0.1 broadcast_in_dim.28
  54.9 4.6 %all_to_all.38 = f32[2,16,16,512]{3,2,1,0:T(8,128)S(1)} all-to-all(f32[2,16,16,512]{3,2,1,0:T(8,128)S(1)} %broadcast_in_dim.28), channel_id=1, replica_groups=mesh['row_0'=8,'row_1'=2,'row_2'=2,'col'=8] {'row_2'}, dimensions={0} | all-to-all | bytes 2097152 | tf_op jit(solution)/shard_map/all_to_all | solution.py:129
  59.4 1.1 copy.21
  60.5 37.4 %rotate.2 = (f32[256,512]{1,0:T(8,128)}, f32[256,256]{1,0:T(8,128)}, f32[256,256]{1,0:T(8,128)}, f32[8,128]{1,0:T(8,128)}) custom-call(f32[512,512]{1,0:T(8,128)} %bitcast.42, f32[256,512]{1,0:T(8,128)} %pair_ref.1), custom_call_target="tpu_custom_call" | custom-call | tf_op jit(solution)/shard_map/rotate/pallas_call | solution.py:113
  97.9 0.0 copy-start.1
  97.9 0.0 copy-start.4
  97.9 1.1 slice_bitcast_fusion.5
  99.0 0.0 copy-done.1
  99.1 0.0 copy-done.4
  99.1 0.1 fusion.4
  99.2 4.3 %collective-permute-start = (f32[512,256]{1,0:T(8,128)S(1)}, f32[512,256]{1,0:T(8,128)S(1)}, u32[]{:S(2)}, u32[]{:S(2)}) collective-permute-start(f32[512,256]{1,0:T(8,128)S(1)} %get-tuple-element.31), channel_id=1, source_target_pairs={{0,1},{1,2},{2,3},{3,4},{4,5},{5,6},{6,7},{8,9},{9,10},{10,11},{11... | collective-permute-start | bytes 1572872 | tf_op jit(solution)/shard_map/ppermute | solution.py:171
  103.5 3.0 %collective-permute-start.1 = (f32[512,256]{1,0:T(8,128)S(1)}, f32[512,256]{1,0:T(8,128)S(1)}, u32[]{:S(2)}, u32[]{:S(2)}) collective-permute-start(f32[512,256]{1,0:T(8,128)S(1)} %get-tuple-element.32), channel_id=1, source_target_pairs={{1,0},{2,1},{3,2},{4,3},{5,4},{6,5},{7,6},{9,8},{10,9},{11,10},{12... | collective-permute-start | bytes 1572872 | tf_op jit(solution)/shard_map/ppermute | solution.py:171
  106.6 10.0 %collective-permute-done = f32[512,256]{1,0:T(8,128)S(1)} collective-permute-done((f32[512,256]{1,0:T(8,128)S(1)}, f32[512,256]{1,0:T(8,128)S(1)}, u32[]{:S(2)}, u32[]{:S(2)}) %collective-permute-start) | collective-permute-done | bytes 524320 | tf_op jit(solution)/shard_map/ppermute | solution.py:171
  116.6 12.2 %collective-permute-done.1 = f32[512,256]{1,0:T(8,128)S(1)} collective-permute-done((f32[512,256]{1,0:T(8,128)S(1)}, f32[512,256]{1,0:T(8,128)S(1)}, u32[]{:S(2)}, u32[]{:S(2)}) %collective-permute-start.1) | collective-permute-done | bytes 524320 | tf_op jit(solution)/shard_map/ppermute | solution.py:171
  128.8 0.1 fusion.3
  128.9 0.1 fusion.10
  129.0 0.1 copy.22
  129.1 0.4 fusion.6
  129.5 16.6 %all_to_all.39 = f32[32,8,256]{2,1,0:T(8,128)S(1)} all-to-all(f32[32,8,256]{2,1,0:T(8,128)S(1)} %fusion.6), channel_id=1, replica_groups=mesh['row_0'=8,'row_1'=2,'row_2'=2,'col'=8] {'row_0','row_1','row_2'}, dimensions={0} | all-to-all | bytes 524288 | tf_op jit(solution)/shard_map/all_to_all | solution.py:151
  146.2 0.7 broadcast_in_dim.31
  146.9 4.1 %all-to-all-start.5 = ((f32[32,8,256]{2,1,0:T(8,128)}), f32[32,8,256]{2,1,0:T(8,128)S(1)}, u32[]{:S(2)}, u32[]{:S(2)}) async-start(f32[32,8,256]{2,1,0:T(8,128)} %broadcast_in_dim.31), calls=%async_computation.5 | async-start | bytes 524288 | tf_op jit(solution)/shard_map/all_to_all | solution.py:129
  151.1 0.9 pad_maximum_fusion.3.pair_ref
  151.9 11.2 %all-to-all-done.5 = f32[32,8,256]{2,1,0:T(8,128)S(1)} async-done(((f32[32,8,256]{2,1,0:T(8,128)}), f32[32,8,256]{2,1,0:T(8,128)S(1)}, u32[]{:S(2)}, u32[]{:S(2)}) %all-to-all-start.5) | async-done | bytes 262176 | tf_op jit(solution)/shard_map/all_to_all | solution.py:129
  163.2 0.1 copy.23
  163.3 1.1 maximum_bitcast_fusion.g_ref
  164.4 37.2 %rotate.3 = (f32[256,512]{1,0:T(8,128)}, f32[256,256]{1,0:T(8,128)}, f32[256,256]{1,0:T(8,128)}, f32[8,128]{1,0:T(8,128)}) custom-call(f32[512,512]{1,0:T(8,128)} %maximum_bitcast_fusion.g_ref, f32[256,512]{1,0:T(8,128)} %pad_maximum_fusion.3.pair_ref), custom_call_target="tpu_custom_call" | custom-call | tf_op jit(solution)/shard_map/rotate/pallas_call | solution.py:113
  201.7 0.0 copy-start.2
  201.7 0.0 copy-start.3
  201.7 1.1 slice_bitcast_fusion.1
  202.8 0.0 copy-done.2
  202.8 0.0 copy-done.3
  202.8 0.1 fusion
  202.9 4.3 %collective-permute-start.2 = (f32[512,256]{1,0:T(8,128)S(1)}, f32[512,256]{1,0:T(8,128)S(1)}, u32[]{:S(2)}, u32[]{:S(2)}) collective-permute-start(f32[512,256]{1,0:T(8,128)S(1)} %get-tuple-element.20), channel_id=1, source_target_pairs={{0,1},{1,2},{2,3},{3,4},{4,5},{5,6},{6,7},{8,9},{9,10},{10,11},{11... | collective-permute-start | bytes 1572872 | tf_op jit(solution)/shard_map/ppermute | solution.py:171
  207.3 3.0 %collective-permute-start.3 = (f32[512,256]{1,0:T(8,128)S(1)}, f32[512,256]{1,0:T(8,128)S(1)}, u32[]{:S(2)}, u32[]{:S(2)}) collective-permute-start(f32[512,256]{1,0:T(8,128)S(1)} %get-tuple-element.21), channel_id=1, source_target_pairs={{1,0},{2,1},{3,2},{4,3},{5,4},{6,5},{7,6},{9,8},{10,9},{11,10},{12... | collective-permute-start | bytes 1572872 | tf_op jit(solution)/shard_map/ppermute | solution.py:171
  210.3 1.2 slice.46
  211.5 1.2 slice.47
  212.7 1.4 pad_maximum_fusion.6
  214.1 19.0 %all_to_all.40 = f32[8,1,2]{2,1,0:T(1,128)S(1)} all-to-all(f32[8,1,2]{2,1,0:T(1,128)S(1)} %broadcast_in_dim.34), channel_id=1, replica_groups=mesh['row_0'=8,'row_1'=2,'row_2'=2,'col'=8] {'col'}, dimensions={0} | all-to-all | bytes 128 | tf_op jit(solution)/shard_map/all_to_all | solution.py:129
  233.1 0.5 multiply_sqrt_fusion
  233.6 0.0 collective-permute-done.2
  233.7 0.0 collective-permute-done.3
  233.7 0.1 slice_select_fusion.1
  233.7 0.9 pad_maximum_fusion.5
  (5 shorter events, 0.1 us)
Async XLA Ops:
  0.6 1.3 copy-start
  35.1 19.6 %all-to-all-start.2 = ((f32[16,16,512]{2,1,0:T(8,128)}), f32[16,16,512]{2,1,0:T(8,128)S(1)}, u32[]{:S(2)}, u32[]{:S(2)}) async-start(f32[16,16,512]{2,1,0:T(8,128)} %broadcast_in_dim.27), calls=%async_computation.2 | async-start | bytes 1048576 | tf_op jit(solution)/shard_map/all_to_all | solution.py:129
  97.9 1.1 copy-start.1
  97.9 1.2 copy-start.4
  99.2 17.4 %collective-permute-start = (f32[512,256]{1,0:T(8,128)S(1)}, f32[512,256]{1,0:T(8,128)S(1)}, u32[]{:S(2)}, u32[]{:S(2)}) collective-permute-start(f32[512,256]{1,0:T(8,128)S(1)} %get-tuple-element.31), channel_id=1, source_target_pairs={{0,1},{1,2},{2,3},{3,4},{4,5},{5,6},{6,7},{8,9},{9,10},{10,11},{11... | collective-permute-start | bytes 1572872 | tf_op jit(solution)/shard_map/ppermute | solution.py:171
  103.5 25.3 %collective-permute-start.1 = (f32[512,256]{1,0:T(8,128)S(1)}, f32[512,256]{1,0:T(8,128)S(1)}, u32[]{:S(2)}, u32[]{:S(2)}) collective-permute-start(f32[512,256]{1,0:T(8,128)S(1)} %get-tuple-element.32), channel_id=1, source_target_pairs={{1,0},{2,1},{3,2},{4,3},{5,4},{6,5},{7,6},{9,8},{10,9},{11,10},{12... | collective-permute-start | bytes 1572872 | tf_op jit(solution)/shard_map/ppermute | solution.py:171
  146.9 16.2 %all-to-all-start.5 = ((f32[32,8,256]{2,1,0:T(8,128)}), f32[32,8,256]{2,1,0:T(8,128)S(1)}, u32[]{:S(2)}, u32[]{:S(2)}) async-start(f32[32,8,256]{2,1,0:T(8,128)} %broadcast_in_dim.31), calls=%async_computation.5 | async-start | bytes 524288 | tf_op jit(solution)/shard_map/all_to_all | solution.py:129
  201.7 1.1 copy-start.2
  201.7 1.2 copy-start.3
  202.9 30.7 %collective-permute-start.2 = (f32[512,256]{1,0:T(8,128)S(1)}, f32[512,256]{1,0:T(8,128)S(1)}, u32[]{:S(2)}, u32[]{:S(2)}) collective-permute-start(f32[512,256]{1,0:T(8,128)S(1)} %get-tuple-element.20), channel_id=1, source_target_pairs={{0,1},{1,2},{2,3},{3,4},{4,5},{5,6},{6,7},{8,9},{9,10},{10,11},{11... | collective-permute-start | bytes 1572872 | tf_op jit(solution)/shard_map/ppermute | solution.py:171
  207.3 26.4 %collective-permute-start.3 = (f32[512,256]{1,0:T(8,128)S(1)}, f32[512,256]{1,0:T(8,128)S(1)}, u32[]{:S(2)}, u32[]{:S(2)}) collective-permute-start(f32[512,256]{1,0:T(8,128)S(1)} %get-tuple-element.21), channel_id=1, source_target_pairs={{1,0},{2,1},{3,2},{4,3},{5,4},{6,5},{7,6},{9,8},{10,9},{11,10},{12... | collective-permute-start | bytes 1572872 | tf_op jit(solution)/shard_map/ppermute | solution.py:171

commit v2 on v1

v2 whole, which is shorter than its diff:
```python
import functools

import jax
import jax.numpy as jnp
from jax import lax
from jax.experimental import pallas as pl
from jax.experimental.pallas import tpu as pltpu
from jax.sharding import Mesh
from jax.sharding import PartitionSpec as P

STEPS = 2
ROW = ("row_0", "row_1", "row_2")
CHIPS = ("row_0", "row_1")
H = 256
TOP = ((0, 0), (0, 1), (1, 1))
CROSS = ((0, 2), (0, 3), (1, 2), (1, 3))
BOTTOM = ((2, 2), (2, 3), (3, 3))
VM = pl.BlockSpec(memory_space=pltpu.VMEM)
SM = pl.BlockSpec(memory_space=pltpu.SMEM)

HI=lax.Precision.HIGHEST
F32=jnp.float32
N=512
T=128
def dot(a,b,ca,cb):
    return lax.dot_general(a,b,(((ca,),(cb,)),((),())),precision=HI,preferred_element_type=F32)
def spread(x): return jnp.broadcast_to(x,(8,T))
def leaves(mats, B=4):
    sub=lax.broadcasted_iota(jnp.int32,(8,T),0); lane=lax.broadcasted_iota(jnp.int32,(8,T),1)
    n=len(mats); G8=T//8
    As=[list(m) for m in mats]
    Is=[[jnp.where(sub+8*q==lane,1.0,0.0).astype(F32) for q in range(G8)] for _ in range(n)]
    for P in range(0,G8,B):
        for p in range(P,P+B):
            r0=8*p
            qs=list(range(p,P+B))
            C=[{q:[spread(A[q][:,r0+k:r0+k+1]) for k in range(8)] for q in qs} for A in As]
            rd=[jnp.ones((8,T),F32) for _ in range(n)]
            for j in range(8):
                for a in range(n):
                    A,I=As[a],Is[a]
                    rinv=1.0/spread(C[a][p][j][j:j+1,:])
                    rd[a]=jnp.where(sub==j,rinv,rd[a])
                    rows=[spread(C[a][p][k][j:j+1,:]) for k in range(j+1,8)]
                    ra=spread(A[p][j:j+1,:]); ri=spread(I[p][j:j+1,:])
                    for q in qs:
                        if q==p:
                            if j==7: continue
                            m=jnp.where(sub>j,C[a][q][j]*rinv,0.0)
                        else:
                            m=C[a][q][j]*rinv
                        for k in range(j+1,8):
                            C[a][q][k]=C[a][q][k]-m*rows[k-j-1]
                        A[q]=A[q]-m*ra; I[q]=I[q]-m*ri
            for a in range(n):
                s=jnp.sqrt(rd[a])
                As[a][p]=As[a][p]*s; Is[a][p]=Is[a][p]*s
        if P+B<G8:
            for a in range(n):
                A,I=As[a],Is[a]
                SA=jnp.concatenate(A[P:P+B],axis=0)
                both=jnp.concatenate([SA,jnp.concatenate(I[P:P+B],axis=0)],axis=1)
                upd=dot(SA[:,8*(P+B):],both,0,0)
                for q in range(P+B,G8):
                    o=8*(q-P-B)
                    A[q]=A[q]-upd[o:o+8,:T]; I[q]=I[q]-upd[o:o+8,T:]
    for a in range(n):
        for p in range(G8):
            As[a][p]=jnp.where(lane>=sub+8*p,As[a][p],0.0)
    return As,Is

def tile(ij):
    i,j=ij
    return slice(i*T,(i+1)*T),slice(j*T,(j+1)*T)
def gram_kernel(pair_ref,g_ref):
    where={ij:n for n,ij in enumerate(TOP+CROSS+BOTTOM)}
    for i in range(4):
        rows=dot(pair_ref[:,i*T:(i+1)*T],pair_ref[:,i*T:],0,0)
        for j in range(i,4):
            n=where[(i,j)]
            g_ref[n*T:(n+1)*T,:]=rows[:,(j-i)*T:(j-i+1)*T]
def local_gram(pair):
    return pl.pallas_call(gram_kernel,out_shape=jax.ShapeDtypeStruct((10*T,T),F32),in_specs=[VM],out_specs=VM,name="gram")(pair)
def cross_kernel(ends_ref,top_ref,from_left_ref,from_right_ref,pair_ref,c_ref):
    own=top_ref[...]
    top=jnp.where(ends_ref[0]==1,own,from_left_ref[...])
    bottom=jnp.where(ends_ref[1]==1,own,from_right_ref[...])
    pair_ref[:,:H]=top
    pair_ref[:,H:]=bottom
    for i in range(2):
        rows=dot(top[:,i*T:(i+1)*T],bottom,0,0)
        c_ref[2*i*T:(2*i+1)*T,:]=rows[:,:T]
        c_ref[(2*i+1)*T:(2*i+2)*T,:]=rows[:,T:]
def local_cross(ends,top,from_left,from_right):
    return pl.pallas_call(cross_kernel,out_shape=[jax.ShapeDtypeStruct((256,512),F32),jax.ShapeDtypeStruct((4*T,T),F32)],
        in_specs=[SM,VM,VM,VM],out_specs=[VM]*2,name="cross")(ends,top,from_left,from_right)
def diagonals(A,sub,lane):
    eye=sub==lane
    down=[jnp.sum(jnp.where(eye,A[tile((i,i))],0.0),axis=1,keepdims=True) for i in (0,1)]
    along=[jnp.sum(jnp.where(eye,A[tile((i,i))],0.0),axis=0,keepdims=True) for i in (2,3)]
    return down,along
def rotate_kernel(first,*refs):
    if first:
        ends_ref,g_ref,pair_ref,top_ref,bottom_ref,right_ref,own_top_ref,own_bottom_ref,own_right_ref,cpl_ref=refs[:10]
        refs=refs[10:]
    else:
        ends_ref,own_ref,own_left_ref,own_from_right_ref,g_ref,pair_ref,top_ref,bottom_ref,right_ref,cpl_ref=refs[:10]
        refs=refs[10:]
    A,U,V,W,RT,d_ref,u_ref,i_ref=refs
    sub=lax.broadcasted_iota(jnp.int32,(T,T),0); lane=lax.broadcasted_iota(jnp.int32,(T,T),1)
    if first:
        for n,ij in enumerate(TOP+CROSS+BOTTOM):
            A[tile(ij)]=g_ref[n*T:(n+1)*T,:]
    else:
        own=own_ref[...]
        own_top=jnp.where(ends_ref[0]==1,own,own_left_ref[...])
        own_bottom=jnp.where(ends_ref[1]==1,own,own_from_right_ref[...])
        for n in range(3):
            A[tile(TOP[n])]=own_top[n*T:(n+1)*T]
            A[tile(BOTTOM[n])]=own_bottom[n*T:(n+1)*T]
        for n,ij in enumerate(CROSS):
            A[tile(ij)]=g_ref[n*T:(n+1)*T,:]
    U[...]=jnp.zeros_like(U); V[...]=jnp.zeros_like(V)
    d_ref[0]=A[:T,:T]
    d_ref[1]=jnp.where(sub==lane,1.0,0.0).astype(F32)
    down,along=diagonals(A,sub,lane)
    cpl=jnp.zeros((1,T),F32)
    for i in (0,1):
        for j in (2,3):
            c=A[tile((i,j))]
            cpl=cpl+jnp.sum(c*c/(down[i]*along[j-2]),axis=0,keepdims=True)
    cpl_ref[...]=jnp.broadcast_to(jnp.sum(cpl,axis=1,keepdims=True),(8,T))
    def branch(t):
        lo,hi=t*T,(t+1)*T
        if t>=1:
            s=t-1; sl,sh=s*T,t*T
            V[sl:sh,sl:sh]=u_ref[1]
            sinv=i_ref[1]
            W[sl:sh,sl:sh]=sinv
            if s:
                t1=dot(V[:sl,sl:sh],W[:sl,:sl],0,0)
                W[sl:sh,:sl]=-dot(sinv,t1,1,0)
                W[:sl,sl:sh]=jnp.zeros((sl,T),F32)
        if t<4:
            U[lo:hi,lo:hi]=u_ref[0]
            linv=i_ref[0]
            if t<3:
                U[lo:hi,hi:]=dot(linv,A[lo:hi,hi:],1,0)
                d_ref[0]=A[hi:hi+T,hi:hi+T]-dot(U[lo:hi,hi:hi+T],U[lo:hi,hi:hi+T],0,0)
            bcol=dot(U[:hi,lo:],U[lo:hi,lo:],1,1)
            if t:
                vcol=dot(W[:lo,:lo],bcol[:lo],1,0)
                V[:lo,lo:hi]=vcol
                d_ref[1]=bcol[lo:]-dot(vcol,vcol,0,0)
            else:
                d_ref[1]=bcol
            for i in range(t+1,4):
                a,b=i*T,(i+1)*T
                A[a:b,a:]=A[a:b,a:]-dot(U[lo:hi,a:b],U[lo:hi,a:],0,0)
        if t>=1:
            RT[sl:sh,:]=dot(W[sl:sh,:sh],U[:sh,:],1,0)
    def stage(t,c):
        us,is_=leaves([[d_ref[a,8*q:8*q+8,:] for q in range(T//8)] for a in range(2)])
        for a in range(2):
            for q in range(T//8):
                u_ref[a,8*q:8*q+8,:]=us[a][q]; i_ref[a,8*q:8*q+8,:]=is_[a][q]
        for k in range(5):
            pl.when(t==k)(functools.partial(branch,k))
        return c
    lax.fori_loop(0,5,stage,0)
    turned=dot(pair_ref[...],RT[...],1,1)
    top,bottom=turned[:,:H],turned[:,H:]
    top_ref[...]=top
    bottom_ref[...]=bottom
    at_start=ends_ref[0]==1
    right_ref[...]=jnp.where(at_start,bottom,top)
    if first:
        def packed(ref,lo):
            a=dot(V[lo:lo+T,lo:],V[lo:lo+H,lo:],1,1)
            b=dot(V[lo+T:lo+H,lo:],V[lo+T:lo+H,lo:],1,1)
            ref[:T,:]=a[:,:T]
            ref[T:2*T,:]=a[:,T:]
            ref[2*T:,:]=b
        packed(own_top_ref,0)
        packed(own_bottom_ref,H)
        own_right_ref[...]=jnp.where(at_start,own_bottom_ref[...],own_top_ref[...])
def rotate(first,*operands):
    block=jax.ShapeDtypeStruct((256,H),F32)
    own=jax.ShapeDtypeStruct((3*T,T),F32)
    outs=[block]*3+([own]*3 if first else [])+[jax.ShapeDtypeStruct((8,T),F32)]
    return pl.pallas_call(functools.partial(rotate_kernel,first),out_shape=outs,
        in_specs=[SM]+[VM]*(len(operands)-1),out_specs=[VM]*len(outs),
        scratch_shapes=[pltpu.VMEM((N,N),F32)]*5+[pltpu.VMEM((2,T,T),F32)]*3,
        cost_estimate=pl.CostEstimate(flops=4_000_000_000,bytes_accessed=2_000_000,transcendentals=0),
        name="rotate")(*operands)


def scattered_sum(value, axis):
    count = lax.axis_size(axis)
    parts = lax.all_to_all(value.reshape(count, -1, T), axis, 0, 0, tiled=True)
    return jnp.sum(parts, axis=0)


def gathered(value, axis):
    copies = jnp.broadcast_to(value, (lax.axis_size(axis), *value.shape))
    return lax.all_to_all(copies, axis, split_axis=0, concat_axis=0, tiled=True).reshape(-1, T)


def row_total(value):
    own = scattered_sum(scattered_sum(value, "row_2"), CHIPS)
    return gathered(gathered(own, CHIPS), "row_2")


def moved(value, steps):
    count = lax.axis_size("col")
    first, last = max(0, -steps), min(count, count - steps)
    return lax.ppermute(value, "col", [(source, source + steps) for source in range(first, last)])


def over_slots(terms):
    count = lax.axis_size("col")
    own = jnp.where(jnp.arange(count)[:, None] == lax.axis_index("col"), terms, 0.0)
    parts = [own]
    for step in range(1, count):
        parts.append(lax.ppermute(own, "col", [(i, (i + step) % count) for i in range(count)]))
    return jnp.sum(sum(parts[1:], parts[0]), axis=0)


def steps(matrix):
    place = lax.axis_index("col")
    at_start = place == 0
    at_end = place == lax.axis_size("col") - 1
    ends = jnp.stack([at_start, at_end]).astype(jnp.int32)
    total = row_total(local_gram(matrix))
    top, bottom, right, own_top, own_bottom, own_right, term_0 = rotate(True, ends, total, matrix)
    from_left, from_right = moved(right, 1), moved(bottom, -1)
    pair, cross = local_cross(ends, top, from_left, from_right)
    own_right, own_away, cross = lax.optimization_barrier((own_right, own_bottom, cross))
    own_left = moved(own_right, 1)
    own_from_right = moved(own_away, -1)
    cross = scattered_sum(cross, "row_2")
    cross = gathered(gathered(scattered_sum(cross, CHIPS), CHIPS), "row_2")
    top, bottom, right, term_1 = rotate(False, ends, own_top, own_left, own_from_right, cross, pair)
    from_left = moved(right, 1)
    from_right = moved(bottom, -1)
    lane = jnp.arange(T)[None, :]
    totals = over_slots(jnp.where(lane == 0, term_0, term_1))
    coupling = jnp.sqrt(totals[:STEPS] / (1.0 * lax.axis_size("col") * H))
    rotated = jnp.concatenate(
        [jnp.where(at_start, top, from_left), jnp.where(at_end, top, from_right)], axis=1
    )
    return (rotated, coupling)


def solution(mesh):
    split = Mesh(
        mesh.devices.reshape(8, 2, 2, mesh.shape["col"]), ("row_0", "row_1", "row_2", "col")
    )
    placed = (P(ROW, "col"),)
    return jax.shard_map(
        steps, mesh=split, in_specs=placed, out_specs=(P(ROW, "col"), P()), check_vma=False
    )
```

time: 235 us -> 221 us (0.940)
  starting transfers between devices: 23.5 us -> 49.1 us
  blocking collectives: 71.3 us -> 50.3 us
  waiting for transfers between devices: 48.4 us -> 32.3 us
  local copies, waits for them, and re-layouts: 9.27 us -> 3.63 us
  Pallas kernels: 74.6 us -> 79.3 us
    ppermute x4 -> x13, starting transfers between devices: 14.8 us -> 36.1 us  [the longest x6 22 us: moved(): lax.ppermute(value, 'col', [(source, source + steps) for source in range(...]
    all_to_all x5, blocking collectives: 71.3 us -> 50.3 us  [the longest x4 45.3 us: scattered_sum(): parts = lax.all_to_all(value.reshape(count, -1, T), axis, 0, 0, tiled=True)]
    all_to_all x2 -> x3, waiting for transfers between devices: 26.1 us -> 11.9 us  [gathered(): lax.all_to_all(copies, axis, split_axis=0, concat_axis=0, tiled=True)]
    pallas_call x2 -> x4, Pallas kernels: 74.6 us -> 79.3 us  [the longest x2 74.2 us: rotate(): pl.pallas_call(functools.partial(rotate_kernel, first), out_shape=outs, i...]
    all_to_all x2 -> x3, starting transfers between devices: 8.78 us -> 13 us  [gathered(): lax.all_to_all(copies, axis, split_axis=0, concat_axis=0, tiled=True)]
    slice x4 -> x0, local copies, waits for them, and re-layouts: 2.47 us -> none  [the longest x2 2.38 us: body(): coupling_terms.append(term[0, 0])]
    ppermute x4 -> x13, waiting for transfers between devices: 22.2 us -> 20.4 us  [the longest x6 20.4 us: moved(): lax.ppermute(value, 'col', [(source, source + steps) for source in range(...]
  transfers between devices with their start and end apart: 6 -> 16, of which waited for: 4 -> 7; matrix products, arithmetic and copies ran while one was open for 2% -> 1% of each run, Pallas kernels for 0% -> 0%
where the time goes in v2:
time: 221 us; the launch traced here: 219 us
  Pallas kernels  79.3 us (36%)
  blocking collectives  50.3 us (23%)
  starting transfers between devices  49.1 us (22%)
  waiting for transfers between devices  32.3 us (15%)
  other arithmetic  3.84 us (2%)
  local copies, waits for them, and re-layouts  3.63 us (2%)
    pallas_call x2, Pallas kernels, rotate(): pl.pallas_call(functools.partial(rotate_kernel, first), out_shape=outs, i...  74.2 us
    all_to_all x4, blocking collectives, scattered_sum(): parts = lax.all_to_all(value.reshape(count, -1, T), axis, 0, 0, tiled=True)  45.3 us
    ppermute x6, starting transfers between devices, moved(): lax.ppermute(value, 'col', [(source, source + steps) for source in range(...  22 us
    ppermute x6, waiting for transfers between devices, moved(): lax.ppermute(value, 'col', [(source, source + steps) for source in range(...  20.4 us
    ppermute x7, starting transfers between devices, over_slots(): lax.ppermute(own, 'col', [(i, (i + step) % count) for i in range(count)])  14 us
    all_to_all x3, starting transfers between devices, gathered(): lax.all_to_all(copies, axis, split_axis=0, concat_axis=0, tiled=True)  13 us
    all_to_all x3, waiting for transfers between devices, gathered(): lax.all_to_all(copies, axis, split_axis=0, concat_axis=0, tiled=True)  11.9 us
    all_to_all x1, blocking collectives, gathered(): lax.all_to_all(copies, axis, split_axis=0, concat_axis=0, tiled=True)  5.02 us
  transfers between devices with their start and end apart: 16, of which 7 were waited for; matrix products, arithmetic and copies ran while one was open for 1% of the time, Pallas kernels for 0%

profile of v2, /device:TPU:6, one launch (start us, length us, event | category | flops | bytes accessed | tf_op | source)
XLA Modules:
  0.0 219.3 jit_solution(5057055186186171981)
XLA Ops:
  0.6 2.8 %gram.1 = f32[1280,128]{1,0:T(8,128)} custom-call(f32[256,512]{1,0:T(8,128)} %refs_2_.1), custom_call_target="tpu_custom_call" | custom-call | tf_op jit(solution)/shard_map/gram/pallas_call | solution.py:83
  3.4 5.3 %all_to_all.40 = f32[2,640,128]{2,1,0:T(8,128)S(1)} all-to-all(f32[2,640,128]{2,1,0:T(8,128)} %bitcast.10), channel_id=1, replica_groups=mesh['row_0'=8,'row_1'=2,'row_2'=2,'col'=8] {'row_2'}, dimensions={0} | all-to-all | bytes 1310720 | tf_op jit(solution)/shard_map/all_to_all | solution.py:200
  8.8 21.9 %all_to_all.41 = f32[16,40,128]{2,1,0:T(8,128)S(1)} all-to-all(f32[16,40,128]{2,1,0:T(8,128)S(1)} %bitcast.11), channel_id=1, replica_groups=mesh['row_0'=8,'row_1'=2,'row_2'=2,'col'=8] {'row_0','row_1'}, dimensions={0} | all-to-all | bytes 655360 | tf_op jit(solution)/shard_map/all_to_all | solution.py:200
  30.7 0.7 broadcast_in_dim.34
  31.4 4.8 %all-to-all-start.2 = ((f32[16,40,128]{2,1,0:T(8,128)}), f32[16,40,128]{2,1,0:T(8,128)S(1)}, u32[]{:S(2)}, u32[]{:S(2)}) async-start(f32[16,40,128]{2,1,0:T(8,128)} %broadcast_in_dim.34), calls=%async_computation.2 | async-start | bytes 655360 | tf_op jit(solution)/shard_map/all_to_all | solution.py:206
  36.2 0.6 add_convert_fusion.refs_0_.ends_ref
  36.8 10.8 %all-to-all-done.2 = f32[16,40,128]{2,1,0:T(8,128)S(1)} async-done(((f32[16,40,128]{2,1,0:T(8,128)}), f32[16,40,128]{2,1,0:T(8,128)S(1)}, u32[]{:S(2)}, u32[]{:S(2)}) %all-to-all-start.2) | async-done | bytes 327712 | tf_op jit(solution)/shard_map/all_to_all | solution.py:206
  47.6 5.0 %all_to_all.42 = f32[2,640,128]{2,1,0:T(8,128)} all-to-all(f32[2,640,128]{2,1,0:T(8,128)S(1)} %broadcast_in_dim.35), channel_id=1, replica_groups=mesh['row_0'=8,'row_1'=2,'row_2'=2,'col'=8] {'row_2'}, dimensions={0} | all-to-all | bytes 1310720 | tf_op jit(solution)/shard_map/all_to_all | solution.py:206
  52.6 37.5 %rotate.2 = (f32[256,256]{1,0:T(8,128)}, f32[256,256]{1,0:T(8,128)}, f32[256,256]{1,0:T(8,128)}, f32[384,128]{1,0:T(8,128)}, f32[384,128]{1,0:T(8,128)}, /*index=5*/f32[384,128]{1,0:T(8,128)}, f32[8,128]{1,0:T(8,128)}) custom-call(s32[2]{0:T(128)} %add_convert_fusion.refs_0_.ends_ref, f32[1280,128]{1,0:T(8,128)} %bitcast.13, f32[256,512]{1,0:T(8,128)} %refs_2_.1), custom_call_target="tpu_custom_call" | custom-call | flops 4000000000 | bytes 2000000 | tf_op jit(solution)/shard_map/rotate/pallas_call | solution.py:191
  90.2 4.3 %collective-permute-start = (f32[256,256]{1,0:T(8,128)}, f32[256,256]{1,0:T(8,128)S(1)}, u32[]{:S(2)}, u32[]{:S(2)}) collective-permute-start(f32[256,256]{1,0:T(8,128)} %get-tuple-element.22), channel_id=1, source_target_pairs={{0,1},{1,2},{2,3},{3,4},{4,5},{5,6},{6,7},{8,9},{9,10},{10,11},{11... | collective-permute-start | bytes 786440 | tf_op jit(solution)/shard_map/ppermute | solution.py:217
  94.5 3.0 %collective-permute-start.1 = (f32[256,256]{1,0:T(8,128)}, f32[256,256]{1,0:T(8,128)S(1)}, u32[]{:S(2)}, u32[]{:S(2)}) collective-permute-start(f32[256,256]{1,0:T(8,128)} %get-tuple-element.23), channel_id=1, source_target_pairs={{1,0},{2,1},{3,2},{4,3},{5,4},{6,5},{7,6},{9,8},{10,9},{11,10},{12... | collective-permute-start | bytes 786440 | tf_op jit(solution)/shard_map/ppermute | solution.py:217
  97.5 4.6 %collective-permute-done.from_left_ref = f32[256,256]{1,0:T(8,128)S(1)} collective-permute-done((f32[256,256]{1,0:T(8,128)}, f32[256,256]{1,0:T(8,128)S(1)}, u32[]{:S(2)}, u32[]{:S(2)}) %collective-permute-start) | collective-permute-done | bytes 262176 | tf_op jit(solution)/shard_map/ppermute | solution.py:217
  102.1 0.0 copy-start.1
  102.1 6.6 %collective-permute-done.1.from_right_ref = f32[256,256]{1,0:T(8,128)S(1)} collective-permute-done((f32[256,256]{1,0:T(8,128)}, f32[256,256]{1,0:T(8,128)S(1)}, u32[]{:S(2)}, u32[]{:S(2)}) %collective-permute-start.1) | collective-permute-done | bytes 262176 | tf_op jit(solution)/shard_map/ppermute | solution.py:217
  108.7 0.0 copy-start.2
  108.7 0.0 copy-done.1
  108.7 0.7 copy-done.2
  109.4 2.3 %cross.1 = (f32[256,512]{1,0:T(8,128)}, f32[512,128]{1,0:T(8,128)}) custom-call(s32[2]{0:T(128)} %add_convert_fusion.refs_0_.ends_ref, f32[256,256]{1,0:T(8,128)} %get-tuple-element.21.top_ref, f32[256,256]{1,0:T(8,128)} %copy-done.1, f32[256,256]{1,0:T(8,128)} %copy-done.2), custom_call_target="tpu_custom_call" | custom-call | tf_op jit(solution)/shard_map/cross/pallas_call | solution.py:95
  111.7 5.0 %all_to_all.43 = f32[2,256,128]{2,1,0:T(8,128)S(1)} all-to-all(f32[2,256,128]{2,1,0:T(8,128)} %bitcast.17), channel_id=1, replica_groups=mesh['row_0'=8,'row_1'=2,'row_2'=2,'col'=8] {'row_2'}, dimensions={0} | all-to-all | bytes 524288 | tf_op jit(solution)/shard_map/all_to_all | solution.py:200
  116.7 13.1 %all_to_all.44 = f32[16,16,128]{2,1,0:T(8,128)S(1)} all-to-all(f32[16,16,128]{2,1,0:T(8,128)S(1)} %bitcast.15), channel_id=1, replica_groups=mesh['row_0'=8,'row_1'=2,'row_2'=2,'col'=8] {'row_0','row_1'}, dimensions={0} | all-to-all | bytes 262144 | tf_op jit(solution)/shard_map/all_to_all | solution.py:200
  129.9 0.0 copy-start.5
  129.9 0.0 copy-start.4
  129.9 0.7 broadcast_in_dim.36
  130.5 4.8 %all-to-all-start.6 = ((f32[16,16,128]{2,1,0:T(8,128)}), f32[16,16,128]{2,1,0:T(8,128)S(1)}, u32[]{:S(2)}, u32[]{:S(2)}) async-start(f32[16,16,128]{2,1,0:T(8,128)} %broadcast_in_dim.36), calls=%async_computation.6 | async-start | bytes 262144 | tf_op jit(solution)/shard_map/all_to_all | solution.py:206
  135.3 0.0 copy-done.5
  135.3 4.3 %collective-permute-start.2 = (f32[384,128]{1,0:T(8,128)S(1)}, f32[384,128]{1,0:T(8,128)S(1)}, u32[]{:S(2)}, u32[]{:S(2)}) collective-permute-start(f32[384,128]{1,0:T(8,128)S(1)} %copy-done.5), channel_id=1, source_target_pairs={{0,1},{1,2},{2,3},{3,4},{4,5},{5,6},{6,7},{8,9},{9,10},{10,11},{11... | collective-permute-start | bytes 589832 | tf_op jit(solution)/shard_map/ppermute | solution.py:217
  139.6 0.0 copy-done.4
  139.7 3.0 %collective-permute-start.3 = (f32[384,128]{1,0:T(8,128)S(1)}, f32[384,128]{1,0:T(8,128)S(1)}, u32[]{:S(2)}, u32[]{:S(2)}) collective-permute-start(f32[384,128]{1,0:T(8,128)S(1)} %copy-done.4), channel_id=1, source_target_pairs={{1,0},{2,1},{3,2},{4,3},{5,4},{6,5},{7,6},{9,8},{10,9},{11,10},{12... | collective-permute-start | bytes 589832 | tf_op jit(solution)/shard_map/ppermute | solution.py:217
  142.7 1.2 all-to-all-done.6
  143.9 0.7 broadcast_in_dim.37
  144.6 3.4 %all-to-all-start.7 = ((f32[2,256,128]{2,1,0:T(8,128)}), f32[2,256,128]{2,1,0:T(8,128)S(1)}, u32[]{:S(2)}, u32[]{:S(2)}) async-start(f32[2,256,128]{2,1,0:T(8,128)} %broadcast_in_dim.37), calls=%async_computation.7 | async-start | bytes 524288 | tf_op jit(solution)/shard_map/all_to_all | solution.py:206
  148.0 0.0 collective-permute-done.2.refs_2_
  148.0 0.0 copy-start.6
  148.1 1.8 collective-permute-done.3.refs_3_
  149.9 0.0 copy-start.7
  149.9 0.0 all-to-all-done.7
  149.9 0.0 copy-done.6
  149.9 0.7 copy-done.7
  150.5 0.1 copy-done
  150.6 0.0 copy-start.3
  150.6 36.7 %rotate.3 = (f32[256,256]{1,0:T(8,128)}, f32[256,256]{1,0:T(8,128)}, f32[256,256]{1,0:T(8,128)}, f32[8,128]{1,0:T(8,128)}) custom-call(s32[2]{0:T(128)} %add_convert_fusion.refs_0_.ends_ref, f32[384,128]{1,0:T(8,128)} %get-tuple-element.18.refs_1_, f32[384,128]{1,0:T(8,128)} %copy-done.6, f32[384,128]{1,0:T(8,128)} %copy-done.7, f32[512,128]{1,0:T(8,128)} %bitcast.16, ...), custom_call_target="tpu_custom_call" | custom-call | flops 4000000000 | bytes 2000000 | tf_op jit(solution)/shard_map/rotate/pallas_call | solution.py:191
  187.3 0.0 copy-done.3
  187.3 0.7 select_select_fusion
  188.1 1.3 collective-permute-start.10
  189.4 2.6 %collective-permute-start.11 = (f32[8,128]{1,0:T(8,128)S(1)}, f32[8,128]{1,0:T(8,128)S(1)}, u32[]{:S(2)}, u32[]{:S(2)}) collective-permute-start(f32[8,128]{1,0:T(8,128)S(1)} %select_select_fusion), channel_id=1, source_target_pairs={{0,6},{1,7},{2,0},{3,1},{4,2},{5,3},{6,4},{7,5},{8,14},{9,15},{10,... | collective-permute-start | bytes 12296 | tf_op jit(solution)/shard_map/ppermute | solution.py:225
  192.0 3.0 %collective-permute-start.12 = (f32[8,128]{1,0:T(8,128)S(1)}, f32[8,128]{1,0:T(8,128)S(1)}, u32[]{:S(2)}, u32[]{:S(2)}) collective-permute-start(f32[8,128]{1,0:T(8,128)S(1)} %select_select_fusion), channel_id=1, source_target_pairs={{0,7},{1,0},{2,1},{3,2},{4,3},{5,4},{6,5},{7,6},{8,15},{9,8},{10,9... | collective-permute-start | bytes 12296 | tf_op jit(solution)/shard_map/ppermute | solution.py:225
  195.0 1.4 collective-permute-start.6
  196.5 0.0 collective-permute-start.7
  196.5 0.0 collective-permute-done.10
  196.5 3.1 %collective-permute-start.8 = (f32[8,128]{1,0:T(8,128)S(1)}, f32[8,128]{1,0:T(8,128)S(1)}, u32[]{:S(2)}, u32[]{:S(2)}) collective-permute-start(f32[8,128]{1,0:T(8,128)S(1)} %select_select_fusion), channel_id=1, source_target_pairs={{0,3},{1,4},{2,5},{3,6},{4,7},{5,0},{6,1},{7,2},{8,11},{9,12},{10,... | collective-permute-start | bytes 12296 | tf_op jit(solution)/shard_map/ppermute | solution.py:225
  199.6 0.0 collective-permute-done.11
  199.6 2.6 %collective-permute-start.9 = (f32[8,128]{1,0:T(8,128)S(1)}, f32[8,128]{1,0:T(8,128)S(1)}, u32[]{:S(2)}, u32[]{:S(2)}) collective-permute-start(f32[8,128]{1,0:T(8,128)S(1)} %select_select_fusion), channel_id=1, source_target_pairs={{0,4},{1,5},{2,6},{3,7},{4,0},{5,1},{6,2},{7,3},{8,12},{9,13},{10,... | collective-permute-start | bytes 12296 | tf_op jit(solution)/shard_map/ppermute | solution.py:225
  202.1 0.0 collective-permute-done.12
  202.1 2.7 %collective-permute-start.4 = (f32[256,256]{1,0:T(8,128)}, f32[256,256]{1,0:T(8,128)S(1)}, u32[]{:S(2)}, u32[]{:S(2)}) collective-permute-start(f32[256,256]{1,0:T(8,128)} %get-tuple-element.30), channel_id=1, source_target_pairs={{0,1},{1,2},{2,3},{3,4},{4,5},{5,6},{6,7},{8,9},{9,10},{10,11},{11... | collective-permute-start | bytes 786440 | tf_op jit(solution)/shard_map/ppermute | solution.py:217
  204.9 0.0 collective-permute-done.6
  204.9 4.6 %collective-permute-start.5 = (f32[256,256]{1,0:T(8,128)}, f32[256,256]{1,0:T(8,128)S(1)}, u32[]{:S(2)}, u32[]{:S(2)}) collective-permute-start(f32[256,256]{1,0:T(8,128)} %get-tuple-element.31), channel_id=1, source_target_pairs={{1,0},{2,1},{3,2},{4,3},{5,4},{6,5},{7,6},{9,8},{10,9},{11,10},{12... | collective-permute-start | bytes 786440 | tf_op jit(solution)/shard_map/ppermute | solution.py:217
  209.5 0.0 collective-permute-done.7
  209.5 0.0 collective-permute-done.8
  209.5 0.0 collective-permute-done.9
  209.6 0.5 multiply_sqrt_fusion
  210.1 2.0 collective-permute-done.4
  212.1 5.3 %collective-permute-done.5 = f32[256,256]{1,0:T(8,128)S(1)} collective-permute-done((f32[256,256]{1,0:T(8,128)}, f32[256,256]{1,0:T(8,128)S(1)}, u32[]{:S(2)}, u32[]{:S(2)}) %collective-permute-start.5) | collective-permute-done | bytes 262176 | tf_op jit(solution)/shard_map/ppermute | solution.py:217
  217.5 1.0 broadcast_select_fusion.1
  218.5 0.9 pad_maximum_fusion
  (9 shorter events, 0.2 us)
Async XLA Ops:
  31.4 16.1 %all-to-all-start.2 = ((f32[16,40,128]{2,1,0:T(8,128)}), f32[16,40,128]{2,1,0:T(8,128)S(1)}, u32[]{:S(2)}, u32[]{:S(2)}) async-start(f32[16,40,128]{2,1,0:T(8,128)} %broadcast_in_dim.34), calls=%async_computation.2 | async-start | bytes 655360 | tf_op jit(solution)/shard_map/all_to_all | solution.py:206
  90.2 11.9 %collective-permute-start = (f32[256,256]{1,0:T(8,128)}, f32[256,256]{1,0:T(8,128)S(1)}, u32[]{:S(2)}, u32[]{:S(2)}) collective-permute-start(f32[256,256]{1,0:T(8,128)} %get-tuple-element.22), channel_id=1, source_target_pairs={{0,1},{1,2},{2,3},{3,4},{4,5},{5,6},{6,7},{8,9},{9,10},{10,11},{11... | collective-permute-start | bytes 786440 | tf_op jit(solution)/shard_map/ppermute | solution.py:217
  94.5 14.2 %collective-permute-start.1 = (f32[256,256]{1,0:T(8,128)}, f32[256,256]{1,0:T(8,128)S(1)}, u32[]{:S(2)}, u32[]{:S(2)}) collective-permute-start(f32[256,256]{1,0:T(8,128)} %get-tuple-element.23), channel_id=1, source_target_pairs={{1,0},{2,1},{3,2},{4,3},{5,4},{6,5},{7,6},{9,8},{10,9},{11,10},{12... | collective-permute-start | bytes 786440 | tf_op jit(solution)/shard_map/ppermute | solution.py:217
  102.1 6.6 %copy-start.1 = (f32[256,256]{1,0:T(8,128)}, f32[256,256]{1,0:T(8,128)S(1)}, u32[]{:S(2)}) copy-start(f32[256,256]{1,0:T(8,128)S(1)} %collective-permute-done.from_left_ref) | copy-start | bytes 786436
  108.7 0.7 copy-start.2
  129.9 5.5 %copy-start.5 = (f32[384,128]{1,0:T(8,128)S(1)}, f32[384,128]{1,0:T(8,128)}, u32[]{:S(2)}) copy-start(f32[384,128]{1,0:T(8,128)} %get-tuple-element.25) | copy-start | bytes 589828
  129.9 9.8 %copy-start.4 = (f32[384,128]{1,0:T(8,128)S(1)}, f32[384,128]{1,0:T(8,128)}, u32[]{:S(2)}) copy-start(f32[384,128]{1,0:T(8,128)} %get-tuple-element.26) | copy-start | bytes 589828
  130.5 13.3 %all-to-all-start.6 = ((f32[16,16,128]{2,1,0:T(8,128)}), f32[16,16,128]{2,1,0:T(8,128)S(1)}, u32[]{:S(2)}, u32[]{:S(2)}) async-start(f32[16,16,128]{2,1,0:T(8,128)} %broadcast_in_dim.36), calls=%async_computation.6 | async-start | bytes 262144 | tf_op jit(solution)/shard_map/all_to_all | solution.py:206
  135.3 12.7 %collective-permute-start.2 = (f32[384,128]{1,0:T(8,128)S(1)}, f32[384,128]{1,0:T(8,128)S(1)}, u32[]{:S(2)}, u32[]{:S(2)}) collective-permute-start(f32[384,128]{1,0:T(8,128)S(1)} %copy-done.5), channel_id=1, source_target_pairs={{0,1},{1,2},{2,3},{3,4},{4,5},{5,6},{6,7},{8,9},{9,10},{10,11},{11... | collective-permute-start | bytes 589832 | tf_op jit(solution)/shard_map/ppermute | solution.py:217
  139.7 10.2 %collective-permute-start.3 = (f32[384,128]{1,0:T(8,128)S(1)}, f32[384,128]{1,0:T(8,128)S(1)}, u32[]{:S(2)}, u32[]{:S(2)}) collective-permute-start(f32[384,128]{1,0:T(8,128)S(1)} %copy-done.4), channel_id=1, source_target_pairs={{1,0},{2,1},{3,2},{4,3},{5,4},{6,5},{7,6},{9,8},{10,9},{11,10},{12... | collective-permute-start | bytes 589832 | tf_op jit(solution)/shard_map/ppermute | solution.py:217
  144.6 5.3 %all-to-all-start.7 = ((f32[2,256,128]{2,1,0:T(8,128)}), f32[2,256,128]{2,1,0:T(8,128)S(1)}, u32[]{:S(2)}, u32[]{:S(2)}) async-start(f32[2,256,128]{2,1,0:T(8,128)} %broadcast_in_dim.37), calls=%async_computation.7 | async-start | bytes 524288 | tf_op jit(solution)/shard_map/all_to_all | solution.py:206
  148.0 1.8 copy-start.6
  149.9 0.7 copy-start.7
  149.9 0.8 copy-start
  150.6 36.7 %copy-start.3 = (f32[8,128]{1,0:T(8,128)S(1)}, f32[8,128]{1,0:T(8,128)}, u32[]{:S(2)}) copy-start(f32[8,128]{1,0:T(8,128)} %get-tuple-element.32) | copy-start | bytes 12292
  188.1 8.4 %collective-permute-start.10 = (f32[8,128]{1,0:T(8,128)S(1)}, f32[8,128]{1,0:T(8,128)S(1)}, u32[]{:S(2)}, u32[]{:S(2)}) collective-permute-start(f32[8,128]{1,0:T(8,128)S(1)} %select_select_fusion), channel_id=1, source_target_pairs={{0,5},{1,6},{2,7},{3,0},{4,1},{5,2},{6,3},{7,4},{8,13},{9,14},{10,... | collective-permute-start | bytes 12296 | tf_op jit(solution)/shard_map/ppermute | solution.py:225
  189.4 10.2 %collective-permute-start.11 = (f32[8,128]{1,0:T(8,128)S(1)}, f32[8,128]{1,0:T(8,128)S(1)}, u32[]{:S(2)}, u32[]{:S(2)}) collective-permute-start(f32[8,128]{1,0:T(8,128)S(1)} %select_select_fusion), channel_id=1, source_target_pairs={{0,6},{1,7},{2,0},{3,1},{4,2},{5,3},{6,4},{7,5},{8,14},{9,15},{10,... | collective-permute-start | bytes 12296 | tf_op jit(solution)/shard_map/ppermute | solution.py:225
  192.0 10.1 %collective-permute-start.12 = (f32[8,128]{1,0:T(8,128)S(1)}, f32[8,128]{1,0:T(8,128)S(1)}, u32[]{:S(2)}, u32[]{:S(2)}) collective-permute-start(f32[8,128]{1,0:T(8,128)S(1)} %select_select_fusion), channel_id=1, source_target_pairs={{0,7},{1,0},{2,1},{3,2},{4,3},{5,4},{6,5},{7,6},{8,15},{9,8},{10,9... | collective-permute-start | bytes 12296 | tf_op jit(solution)/shard_map/ppermute | solution.py:225
  195.0 9.9 %collective-permute-start.6 = (f32[8,128]{1,0:T(8,128)S(1)}, f32[8,128]{1,0:T(8,128)S(1)}, u32[]{:S(2)}, u32[]{:S(2)}) collective-permute-start(f32[8,128]{1,0:T(8,128)S(1)} %select_select_fusion), channel_id=1, source_target_pairs={{0,1},{1,2},{2,3},{3,4},{4,5},{5,6},{6,7},{7,0},{8,9},{9,10},{10,1... | collective-permute-start | bytes 12296 | tf_op jit(solution)/shard_map/ppermute | solution.py:225
  196.5 13.1 %collective-permute-start.7 = (f32[8,128]{1,0:T(8,128)S(1)}, f32[8,128]{1,0:T(8,128)S(1)}, u32[]{:S(2)}, u32[]{:S(2)}) collective-permute-start(f32[8,128]{1,0:T(8,128)S(1)} %select_select_fusion), channel_id=1, source_target_pairs={{0,2},{1,3},{2,4},{3,5},{4,6},{5,7},{6,0},{7,1},{8,10},{9,11},{10,... | collective-permute-start | bytes 12296 | tf_op jit(solution)/shard_map/ppermute | solution.py:225
  196.5 13.1 %collective-permute-start.8 = (f32[8,128]{1,0:T(8,128)S(1)}, f32[8,128]{1,0:T(8,128)S(1)}, u32[]{:S(2)}, u32[]{:S(2)}) collective-permute-start(f32[8,128]{1,0:T(8,128)S(1)} %select_select_fusion), channel_id=1, source_target_pairs={{0,3},{1,4},{2,5},{3,6},{4,7},{5,0},{6,1},{7,2},{8,11},{9,12},{10,... | collective-permute-start | bytes 12296 | tf_op jit(solution)/shard_map/ppermute | solution.py:225
  199.6 10.0 %collective-permute-start.9 = (f32[8,128]{1,0:T(8,128)S(1)}, f32[8,128]{1,0:T(8,128)S(1)}, u32[]{:S(2)}, u32[]{:S(2)}) collective-permute-start(f32[8,128]{1,0:T(8,128)S(1)} %select_select_fusion), channel_id=1, source_target_pairs={{0,4},{1,5},{2,6},{3,7},{4,0},{5,1},{6,2},{7,3},{8,12},{9,13},{10,... | collective-permute-start | bytes 12296 | tf_op jit(solution)/shard_map/ppermute | solution.py:225
  202.1 10.0 %collective-permute-start.4 = (f32[256,256]{1,0:T(8,128)}, f32[256,256]{1,0:T(8,128)S(1)}, u32[]{:S(2)}, u32[]{:S(2)}) collective-permute-start(f32[256,256]{1,0:T(8,128)} %get-tuple-element.30), channel_id=1, source_target_pairs={{0,1},{1,2},{2,3},{3,4},{4,5},{5,6},{6,7},{8,9},{9,10},{10,11},{11... | collective-permute-start | bytes 786440 | tf_op jit(solution)/shard_map/ppermute | solution.py:217
  204.9 12.6 %collective-permute-start.5 = (f32[256,256]{1,0:T(8,128)}, f32[256,256]{1,0:T(8,128)S(1)}, u32[]{:S(2)}, u32[]{:S(2)}) collective-permute-start(f32[256,256]{1,0:T(8,128)} %get-tuple-element.31), channel_id=1, source_target_pairs={{1,0},{2,1},{3,2},{4,3},{5,4},{6,5},{7,6},{9,8},{10,9},{11,10},{12... | collective-permute-start | bytes 786440 | tf_op jit(solution)/shard_map/ppermute | solution.py:217

commit v3 on v2

--- a/solution.py
+++ b/solution.py
@@ -8,7 +8,6 @@
 from jax.sharding import Mesh
 from jax.sharding import PartitionSpec as P
 
-STEPS = 2
 ROW = ("row_0", "row_1", "row_2")
 CHIPS = ("row_0", "row_1")
 H = 256
@@ -46,11 +45,14 @@
                     for q in qs:
                         if q==p:
                             if j==7: continue
-                            m=jnp.where(sub>j,C[a][q][j]*rinv,0.0)
+                            cm=jnp.where(sub>j,C[a][q][j],0.0)
+                            for k in range(j+1,8):
+                                C[a][q][k]=C[a][q][k]-(cm*rows[k-j-1])*rinv
+                            m=cm*rinv
                         else:
                             m=C[a][q][j]*rinv
-                        for k in range(j+1,8):
-                            C[a][q][k]=C[a][q][k]-m*rows[k-j-1]
+                            for k in range(j+1,8):
+                                C[a][q][k]=C[a][q][k]-m*rows[k-j-1]
                         A[q]=A[q]-m*ra; I[q]=I[q]-m*ri
             for a in range(n):
                 s=jnp.sqrt(rd[a])
@@ -94,80 +96,138 @@
 def local_cross(ends,top,from_left,from_right):
     return pl.pallas_call(cross_kernel,out_shape=[jax.ShapeDtypeStruct((256,512),F32),jax.ShapeDtypeStruct((4*T,T),F32)],
         in_specs=[SM,VM,VM,VM],out_specs=[VM]*2,name="cross")(ends,top,from_left,from_right)
-def diagonals(A,sub,lane):
-    eye=sub==lane
-    down=[jnp.sum(jnp.where(eye,A[tile((i,i))],0.0),axis=1,keepdims=True) for i in (0,1)]
-    along=[jnp.sum(jnp.where(eye,A[tile((i,i))],0.0),axis=0,keepdims=True) for i in (2,3)]
-    return down,along
+def spread_leaves(d_ref,u_ref,i_ref,count):
+    us,is_=leaves([[d_ref[a,8*q:8*q+8,:] for q in range(T//8)] for a in range(count)])
+    for a in range(count):
+        for q in range(T//8):
+            u_ref[a,8*q:8*q+8,:]=us[a][q]
+            i_ref[a,8*q:8*q+8,:]=is_[a][q]
+def early_kernel(ends_ref,own_ref,own_left_ref,up_ref,inv_ref,d_ref,u_ref,i_ref):
+    g=jnp.where(ends_ref[0]==1,own_ref[...],own_left_ref[...])
+    d_ref[0]=g[:T]
+    up_ref[T:2*T,:]=g[T:2*T]
+    inv_ref[T:2*T,:]=g[2*T:]
+    def stage(t,c):
+        spread_leaves(d_ref,u_ref,i_ref,1)
+        @pl.when(t==0)
+        def _():
+            up_ref[:T,:]=u_ref[0]
+            inv_ref[:T,:]=i_ref[0]
+            u01=dot(i_ref[0],up_ref[T:2*T,:],1,0)
+            up_ref[T:2*T,:]=u01
+            d_ref[0]=inv_ref[T:2*T,:]-dot(u01,u01,0,0)
+        @pl.when(t==1)
+        def _():
+            up_ref[2*T:,:]=u_ref[0]
+            inv_ref[2*T:,:]=i_ref[0]
+            inv_ref[T:2*T,:]=-dot(i_ref[0],dot(up_ref[T:2*T,:],inv_ref[:T,:],0,0),1,0)
+        return c
+    lax.fori_loop(0,2,stage,0)
+def early(*operands):
+    own=jax.ShapeDtypeStruct((3*T,T),F32)
+    return pl.pallas_call(early_kernel,out_shape=[own]*2,in_specs=[SM,VM,VM],out_specs=[VM]*2,
+        scratch_shapes=[pltpu.VMEM((1,T,T),F32)]*3,
+        cost_estimate=pl.CostEstimate(flops=500_000_000,bytes_accessed=1_000_000,transcendentals=0),
+        name="early")(*operands)
+def coupling_sum(A,down,along):
+    cpl=jnp.zeros((1,T),F32)
+    for i in (0,1):
+        for j in (2,3):
+            c=A[tile((i,j))]
+            cpl=cpl+jnp.sum(c*c/(down[i]*along[j-2]),axis=0,keepdims=True)
+    return jnp.broadcast_to(jnp.sum(cpl,axis=1,keepdims=True),(8,T))
 def rotate_kernel(first,*refs):
     if first:
         ends_ref,g_ref,pair_ref,top_ref,bottom_ref,right_ref,own_top_ref,own_bottom_ref,own_right_ref,cpl_ref=refs[:10]
         refs=refs[10:]
     else:
-        ends_ref,own_ref,own_left_ref,own_from_right_ref,g_ref,pair_ref,top_ref,bottom_ref,right_ref,cpl_ref=refs[:10]
-        refs=refs[10:]
+        ends_ref,own_ref,own_from_right_ref,up_ref,inv_ref,g_ref,pair_ref,top_ref,bottom_ref,right_ref,cpl_ref=refs[:11]
+        refs=refs[11:]
     A,U,V,W,RT,d_ref,u_ref,i_ref=refs
     sub=lax.broadcasted_iota(jnp.int32,(T,T),0); lane=lax.broadcasted_iota(jnp.int32,(T,T),1)
+    eye=sub==lane
+    U[...]=jnp.zeros_like(U); V[...]=jnp.zeros_like(V)
+    def along_of(n):
+        return jnp.sum(jnp.where(eye,A[tile((n,n))],0.0),axis=0,keepdims=True)
+    def down_of(row):
+        return jnp.sum(jnp.where(eye,row,0.0),axis=1,keepdims=True)
+    def next_d2(t):
+        lo,hi=t*T,(t+1)*T
+        bcol=dot(U[:hi,lo:],U[lo:hi,lo:],1,1)
+        if t:
+            vcol=dot(W[:lo,:lo],bcol[:lo],1,0)
+            V[:lo,lo:hi]=vcol
+            d_ref[1]=bcol[lo:]-dot(vcol,vcol,0,0)
+        else:
+            d_ref[1]=bcol
+    def inner_part(s):
+        sl,sh=s*T,(s+1)*T
+        V[sl:sh,sl:sh]=u_ref[1]
+        sinv=i_ref[1]
+        W[sl:sh,sl:sh]=sinv
+        if s:
+            t1=dot(V[:sl,sl:sh],W[:sl,:sl],0,0)
+            W[sl:sh,:sl]=-dot(sinv,t1,1,0)
+            W[:sl,sl:sh]=jnp.zeros((sl,T),F32)
+    def outer_part(t):
+        lo,hi=t*T,(t+1)*T
+        U[lo:hi,lo:hi]=u_ref[0]
+        if t<3:
+            U[lo:hi,hi:]=dot(i_ref[0],A[lo:hi,hi:],1,0)
+            d_ref[0]=A[hi:hi+T,hi:hi+T]-dot(U[lo:hi,hi:hi+T],U[lo:hi,hi:hi+T],0,0)
+    def trailing(t):
+        lo,hi=t*T,(t+1)*T
+        for i in range(t+1,4):
+            a,b=i*T,(i+1)*T
+            A[a:b,a:]=A[a:b,a:]-dot(U[lo:hi,a:b],U[lo:hi,a:],0,0)
+    def turn_row(s):
+        sl,sh=s*T,(s+1)*T
+        RT[sl:sh,:]=dot(W[sl:sh,:sh],U[:sh,:],1,0)
     if first:
         for n,ij in enumerate(TOP+CROSS+BOTTOM):
             A[tile(ij)]=g_ref[n*T:(n+1)*T,:]
+        d_ref[0]=A[:T,:T]
+        d_ref[1]=jnp.where(eye,1.0,0.0).astype(F32)
+        down=[down_of(A[tile((n,n))]) for n in (0,1)]
+        skip=0
     else:
-        own=own_ref[...]
-        own_top=jnp.where(ends_ref[0]==1,own,own_left_ref[...])
-        own_bottom=jnp.where(ends_ref[1]==1,own,own_from_right_ref[...])
+        own_bottom=jnp.where(ends_ref[1]==1,own_ref[...],own_from_right_ref[...])
         for n in range(3):
-            A[tile(TOP[n])]=own_top[n*T:(n+1)*T]
             A[tile(BOTTOM[n])]=own_bottom[n*T:(n+1)*T]
+            U[tile(TOP[n])]=up_ref[n*T:(n+1)*T,:]
         for n,ij in enumerate(CROSS):
             A[tile(ij)]=g_ref[n*T:(n+1)*T,:]
-    U[...]=jnp.zeros_like(U); V[...]=jnp.zeros_like(V)
-    d_ref[0]=A[:T,:T]
-    d_ref[1]=jnp.where(sub==lane,1.0,0.0).astype(F32)
-    down,along=diagonals(A,sub,lane)
-    cpl=jnp.zeros((1,T),F32)
-    for i in (0,1):
-        for j in (2,3):
-            c=A[tile((i,j))]
-            cpl=cpl+jnp.sum(c*c/(down[i]*along[j-2]),axis=0,keepdims=True)
-    cpl_ref[...]=jnp.broadcast_to(jnp.sum(cpl,axis=1,keepdims=True),(8,T))
-    def branch(t):
-        lo,hi=t*T,(t+1)*T
-        if t>=1:
-            s=t-1; sl,sh=s*T,t*T
-            V[sl:sh,sl:sh]=u_ref[1]
-            sinv=i_ref[1]
-            W[sl:sh,sl:sh]=sinv
-            if s:
-                t1=dot(V[:sl,sl:sh],W[:sl,:sl],0,0)
-                W[sl:sh,:sl]=-dot(sinv,t1,1,0)
-                W[:sl,sl:sh]=jnp.zeros((sl,T),F32)
+        sq=[jnp.sum(up_ref[n*T:(n+1)*T,:]*up_ref[n*T:(n+1)*T,:],axis=0,keepdims=True) for n in range(3)]
+        down=[down_of(sq[0]),down_of(sq[1]+sq[2])]
+        skip=2
+    cpl_ref[...]=coupling_sum(A,down,[along_of(2),along_of(3)])
+    if not first:
+        U[:T,H:]=dot(inv_ref[:T,:],A[:T,H:],1,0)
+        U[T:H,H:]=dot(inv_ref[T:2*T,:],A[:T,H:],1,0)+dot(inv_ref[2*T:,:],A[T:H,H:],1,0)
+        for a in (H,H+T):
+            A[a:a+T,a:]=A[a:a+T,a:]-dot(U[:H,a:a+T],U[:H,a:],0,0)
+        d_ref[0]=A[H:H+T,H:H+T]
+        next_d2(0)
+    def branch(k):
+        s=k-1 if first else k
+        t=k+skip
+        if s>=0:
+            inner_part(s)
         if t<4:
-            U[lo:hi,lo:hi]=u_ref[0]
-            linv=i_ref[0]
-            if t<3:
-                U[lo:hi,hi:]=dot(linv,A[lo:hi,hi:],1,0)
-                d_ref[0]=A[hi:hi+T,hi:hi+T]-dot(U[lo:hi,hi:hi+T],U[lo:hi,hi:hi+T],0,0)
-            bcol=dot(U[:hi,lo:],U[lo:hi,lo:],1,1)
-            if t:
-                vcol=dot(W[:lo,:lo],bcol[:lo],1,0)
-                V[:lo,lo:hi]=vcol
-                d_ref[1]=bcol[lo:]-dot(vcol,vcol,0,0)
-            else:
-                d_ref[1]=bcol
-            for i in range(t+1,4):
-                a,b=i*T,(i+1)*T
-                A[a:b,a:]=A[a:b,a:]-dot(U[lo:hi,a:b],U[lo:hi,a:],0,0)
-        if t>=1:
-            RT[sl:sh,:]=dot(W[sl:sh,:sh],U[:sh,:],1,0)
+            outer_part(t)
+        if s+1<4:
+            next_d2(s+1)
+        if t<4:
+            trailing(t)
+        if s>=0:
+            turn_row(s)
+    stages=5 if first else 4
     def stage(t,c):
-        us,is_=leaves([[d_ref[a,8*q:8*q+8,:] for q in range(T//8)] for a in range(2)])
-        for a in range(2):
-            for q in range(T//8):
-                u_ref[a,8*q:8*q+8,:]=us[a][q]; i_ref[a,8*q:8*q+8,:]=is_[a][q]
-        for k in range(5):
+        spread_leaves(d_ref,u_ref,i_ref,2)
+        for k in range(stages):
             pl.when(t==k)(functools.partial(branch,k))
         return c
-    lax.fori_loop(0,5,stage,0)
+    lax.fori_loop(0,stages,stage,0)
     turned=dot(pair_ref[...],RT[...],1,1)
     top,bottom=turned[:,:H],turned[:,H:]
     top_ref[...]=top
@@ -218,12 +278,8 @@
 
 
 def over_slots(terms):
-    count = lax.axis_size("col")
-    own = jnp.where(jnp.arange(count)[:, None] == lax.axis_index("col"), terms, 0.0)
-    parts = [own]
-    for step in range(1, count):
-        parts.append(lax.ppermute(own, "col", [(i, (i + step) % count) for i in range(count)]))
-    return jnp.sum(sum(parts[1:], parts[0]), axis=0)
+    copies = jnp.broadcast_to(terms, (lax.axis_size("col"), *terms.shape))
+    return jnp.sum(lax.all_to_all(copies, "col", split_axis=0, concat_axis=0, tiled=True), axis=0)
 
 
 def steps(matrix):
@@ -233,19 +289,21 @@
     ends = jnp.stack([at_start, at_end]).astype(jnp.int32)
     total = row_total(local_gram(matrix))
     top, bottom, right, own_top, own_bottom, own_right, term_0 = rotate(True, ends, total, matrix)
-    from_left, from_right = moved(right, 1), moved(bottom, -1)
-    pair, cross = local_cross(ends, top, from_left, from_right)
-    own_right, own_away, cross = lax.optimization_barrier((own_right, own_bottom, cross))
-    own_left = moved(own_right, 1)
-    own_from_right = moved(own_away, -1)
-    cross = scattered_sum(cross, "row_2")
-    cross = gathered(gathered(scattered_sum(cross, CHIPS), CHIPS), "row_2")
-    top, bottom, right, term_1 = rotate(False, ends, own_top, own_left, own_from_right, cross, pair)
     from_left = moved(right, 1)
     from_right = moved(bottom, -1)
-    lane = jnp.arange(T)[None, :]
-    totals = over_slots(jnp.where(lane == 0, term_0, term_1))
-    coupling = jnp.sqrt(totals[:STEPS] / (1.0 * lax.axis_size("col") * H))
+    own_left = moved(own_right, 1)
+    own_from_right = moved(own_bottom, -1)
+    pair, cross = local_cross(ends, top, from_left, from_right)
+    cross = scattered_sum(cross, ROW)
+    cross = gathered(cross, ROW)
+    up, inverse = early(ends, own_top, own_left)
+    top, bottom, right, term_1 = rotate(
+        False, ends, own_top, own_from_right, up, inverse, cross, pair
+    )
+    from_left = moved(right, 1)
+    from_right = moved(bottom, -1)
+    totals = over_slots(jnp.stack([term_0[0, 0], term_1[0, 0]]))
+    coupling = jnp.sqrt(totals / (1.0 * lax.axis_size("col") * H))
     rotated = jnp.concatenate(
         [jnp.where(at_start, top, from_left), jnp.where(at_end, top, from_right)], axis=1
     )
@@ -257,6 +315,4 @@
         mesh.devices.reshape(8, 2, 2, mesh.shape["col"]), ("row_0", "row_1", "row_2", "col")
     )
     placed = (P(ROW, "col"),)
-    return jax.shard_map(
-        steps, mesh=split, in_specs=placed, out_specs=(P(ROW, "col"), P()), check_vma=False
-    )
+    return jax.shard_map(steps, mesh=split, in_specs=placed, out_specs=(P(ROW, "col"), P()), check_vma=False)

time: 221 us -> 216 us (0.977)
  starting transfers between devices: 49.1 us -> 31 us
  blocking collectives: 50.3 us -> 61.8 us
  waiting for transfers between devices: 32.3 us -> 25.6 us
  Pallas kernels: 79.3 us -> 83.7 us
  local copies, waits for them, and re-layouts: 3.63 us -> 6.09 us
    ppermute x7 -> x0, starting transfers between devices: 14 us -> none  [over_slots(): lax.ppermute(own, 'col', [(i, (i + step) % count) for i in range(count)])]
    all_to_all x0 -> x1, blocking collectives: none -> 12.2 us  [over_slots(): lax.all_to_all(copies, 'col', split_axis=0, concat_axis=0, tiled=True)]
    pallas_call x0 -> x1, Pallas kernels: none -> 11 us  [early(): pl.pallas_call(early_kernel, out_shape=[own] * 2, in_specs=[SM, VM, VM],...]
    pallas_call x2, Pallas kernels: 74.2 us -> 67.7 us  [rotate(): pl.pallas_call(functools.partial(rotate_kernel, first), out_shape=outs, i...]
    ppermute x6, waiting for transfers between devices: 20.4 us -> 14.8 us  [moved(): lax.ppermute(value, 'col', [(source, source + steps) for source in range(...]
    all_to_all x3 -> x2, starting transfers between devices: 13 us -> 8.98 us  [gathered(): lax.all_to_all(copies, axis, split_axis=0, concat_axis=0, tiled=True)]
    slice x0 -> x2, local copies, waits for them, and re-layouts: none -> 2.39 us  [steps(): totals = over_slots(jnp.stack([term_0[0, 0], term_1[0, 0]]))]
    all_to_all x3 -> x2, waiting for transfers between devices: 11.9 us -> 10.8 us  [gathered(): lax.all_to_all(copies, axis, split_axis=0, concat_axis=0, tiled=True)]
  transfers between devices with their start and end apart: 16 -> 8, of which waited for: 7 -> 4; matrix products, arithmetic and copies ran while one was open for 1% -> 2% of each run, Pallas kernels for 0% -> 5%
where the time goes in v3:
time: 216 us; the launch traced here: 213 us
  Pallas kernels  83.7 us (39%)
  blocking collectives  61.8 us (29%)
  starting transfers between devices  31 us (14%)
  waiting for transfers between devices  25.6 us (12%)
  local copies, waits for them, and re-layouts  6.09 us (3%)
  other arithmetic  4.43 us (2%)
    pallas_call x2, Pallas kernels, rotate(): pl.pallas_call(functools.partial(rotate_kernel, first), out_shape=outs, i...  67.7 us
    all_to_all x3, blocking collectives, scattered_sum(): parts = lax.all_to_all(value.reshape(count, -1, T), axis, 0, 0, tiled=True)  44.5 us
    ppermute x6, starting transfers between devices, moved(): lax.ppermute(value, 'col', [(source, source + steps) for source in range(...  22 us
    ppermute x6, waiting for transfers between devices, moved(): lax.ppermute(value, 'col', [(source, source + steps) for source in range(...  14.8 us
    all_to_all x1, blocking collectives, over_slots(): lax.all_to_all(copies, 'col', split_axis=0, concat_axis=0, tiled=True)  12.2 us
    pallas_call x1, Pallas kernels, early(): pl.pallas_call(early_kernel, out_shape=[own] * 2, in_specs=[SM, VM, VM],...  11 us
    all_to_all x2, waiting for transfers between devices, gathered(): lax.all_to_all(copies, axis, split_axis=0, concat_axis=0, tiled=True)  10.8 us
    all_to_all x2, starting transfers between devices, gathered(): lax.all_to_all(copies, axis, split_axis=0, concat_axis=0, tiled=True)  8.98 us
  transfers between devices with their start and end apart: 8, of which 4 were waited for; matrix products, arithmetic and copies ran while one was open for 2% of the time, Pallas kernels for 5%

profile of v3, /device:TPU:6, one launch (start us, length us, event | category | flops | bytes accessed | tf_op | source)
XLA Modules:
  0.0 213.3 jit_solution(6269926247523749489)
XLA Ops:
  0.6 2.8 %gram.1 = f32[1280,128]{1,0:T(8,128)} custom-call(f32[256,512]{1,0:T(8,128)} %refs_2_.1), custom_call_target="tpu_custom_call" | custom-call | tf_op jit(solution)/shard_map/gram/pallas_call | solution.py:85
  3.4 5.3 %all_to_all.36 = f32[2,640,128]{2,1,0:T(8,128)S(1)} all-to-all(f32[2,640,128]{2,1,0:T(8,128)} %bitcast.10), channel_id=1, replica_groups=mesh['row_0'=8,'row_1'=2,'row_2'=2,'col'=8] {'row_2'}, dimensions={0} | all-to-all | bytes 1310720 | tf_op jit(solution)/shard_map/all_to_all | solution.py:260
  8.8 21.9 %all_to_all.37 = f32[16,40,128]{2,1,0:T(8,128)S(1)} all-to-all(f32[16,40,128]{2,1,0:T(8,128)S(1)} %bitcast.11), channel_id=1, replica_groups=mesh['row_0'=8,'row_1'=2,'row_2'=2,'col'=8] {'row_0','row_1'}, dimensions={0} | all-to-all | bytes 655360 | tf_op jit(solution)/shard_map/all_to_all | solution.py:260
  30.7 0.7 broadcast_in_dim.12
  31.4 4.8 %all-to-all-start.2 = ((f32[16,40,128]{2,1,0:T(8,128)}), f32[16,40,128]{2,1,0:T(8,128)S(1)}, u32[]{:S(2)}, u32[]{:S(2)}) async-start(f32[16,40,128]{2,1,0:T(8,128)} %broadcast_in_dim.12), calls=%async_computation.2 | async-start | bytes 655360 | tf_op jit(solution)/shard_map/all_to_all | solution.py:266
  36.2 0.6 add_convert_fusion.refs_0_.ends_ref
  36.8 10.8 %all-to-all-done.2 = f32[16,40,128]{2,1,0:T(8,128)S(1)} async-done(((f32[16,40,128]{2,1,0:T(8,128)}), f32[16,40,128]{2,1,0:T(8,128)S(1)}, u32[]{:S(2)}, u32[]{:S(2)}) %all-to-all-start.2) | async-done | bytes 327712 | tf_op jit(solution)/shard_map/all_to_all | solution.py:266
  47.6 5.0 %all_to_all.38 = f32[2,640,128]{2,1,0:T(8,128)} all-to-all(f32[2,640,128]{2,1,0:T(8,128)S(1)} %broadcast_in_dim.13), channel_id=1, replica_groups=mesh['row_0'=8,'row_1'=2,'row_2'=2,'col'=8] {'row_2'}, dimensions={0} | all-to-all | bytes 1310720 | tf_op jit(solution)/shard_map/all_to_all | solution.py:266
  52.6 36.5 %rotate.2 = (f32[256,256]{1,0:T(8,128)}, f32[256,256]{1,0:T(8,128)}, f32[256,256]{1,0:T(8,128)}, f32[384,128]{1,0:T(8,128)}, f32[384,128]{1,0:T(8,128)}, /*index=5*/f32[384,128]{1,0:T(8,128)}, f32[8,128]{1,0:T(8,128)}) custom-call(s32[2]{0:T(128)} %add_convert_fusion.refs_0_.ends_ref, f32[1280,128]{1,0:T(8,128)} %bitcast.13, f32[256,512]{1,0:T(8,128)} %refs_2_.1), custom_call_target="tpu_custom_call" | custom-call | flops 4000000000 | bytes 2000000 | tf_op jit(solution)/shard_map/rotate/pallas_call | solution.py:251
  89.1 4.3 %collective-permute-start.2 = (f32[256,256]{1,0:T(8,128)}, f32[256,256]{1,0:T(8,128)S(1)}, u32[]{:S(2)}, u32[]{:S(2)}) collective-permute-start(f32[256,256]{1,0:T(8,128)} %get-tuple-element.23), channel_id=1, source_target_pairs={{0,1},{1,2},{2,3},{3,4},{4,5},{5,6},{6,7},{8,9},{9,10},{10,11},{11... | collective-permute-start | bytes 786440 | tf_op jit(solution)/shard_map/ppermute | solution.py:277
  93.5 3.0 %collective-permute-start.3 = (f32[256,256]{1,0:T(8,128)}, f32[256,256]{1,0:T(8,128)S(1)}, u32[]{:S(2)}, u32[]{:S(2)}) collective-permute-start(f32[256,256]{1,0:T(8,128)} %get-tuple-element.24), channel_id=1, source_target_pairs={{1,0},{2,1},{3,2},{4,3},{5,4},{6,5},{7,6},{9,8},{10,9},{11,10},{12... | collective-permute-start | bytes 786440 | tf_op jit(solution)/shard_map/ppermute | solution.py:277
  96.5 4.6 %collective-permute-done.2.from_left_ref = f32[256,256]{1,0:T(8,128)S(1)} collective-permute-done((f32[256,256]{1,0:T(8,128)}, f32[256,256]{1,0:T(8,128)S(1)}, u32[]{:S(2)}, u32[]{:S(2)}) %collective-permute-start.2) | collective-permute-done | bytes 262176 | tf_op jit(solution)/shard_map/ppermute | solution.py:277
  101.1 0.0 copy-start.1
  101.1 6.6 %collective-permute-done.3.from_right_ref = f32[256,256]{1,0:T(8,128)S(1)} collective-permute-done((f32[256,256]{1,0:T(8,128)}, f32[256,256]{1,0:T(8,128)S(1)}, u32[]{:S(2)}, u32[]{:S(2)}) %collective-permute-start.3) | collective-permute-done | bytes 262176 | tf_op jit(solution)/shard_map/ppermute | solution.py:277
  107.7 0.0 copy-start.2
  107.7 0.0 copy-done.1
  107.7 0.7 copy-done.2
  108.4 2.3 %cross.1 = (f32[256,512]{1,0:T(8,128)}, f32[512,128]{1,0:T(8,128)}) custom-call(s32[2]{0:T(128)} %add_convert_fusion.refs_0_.ends_ref, f32[256,256]{1,0:T(8,128)} %get-tuple-element.22.top_ref, f32[256,256]{1,0:T(8,128)} %copy-done.1, f32[256,256]{1,0:T(8,128)} %copy-done.2), custom_call_target="tpu_custom_call" | custom-call | tf_op jit(solution)/shard_map/cross/pallas_call | solution.py:97
  110.7 17.3 %all_to_all.39 = f32[32,16,128]{2,1,0:T(8,128)S(1)} all-to-all(f32[32,16,128]{2,1,0:T(8,128)} %bitcast.15), channel_id=1, replica_groups=mesh['row_0'=8,'row_1'=2,'row_2'=2,'col'=8] {'row_0','row_1','row_2'}, dimensions={0} | all-to-all | bytes 524288 | tf_op jit(solution)/shard_map/all_to_all | solution.py:260
  128.1 0.7 broadcast_in_dim.14
  128.8 0.0 copy-start.4
  128.8 0.0 copy-start.3
  128.8 4.2 %all-to-all-start.5 = ((f32[32,16,128]{2,1,0:T(8,128)}), f32[32,16,128]{2,1,0:T(8,128)S(1)}, u32[]{:S(2)}, u32[]{:S(2)}) async-start(f32[32,16,128]{2,1,0:T(8,128)} %broadcast_in_dim.14), calls=%async_computation.5 | async-start | bytes 524288 | tf_op jit(solution)/shard_map/all_to_all | solution.py:266
  133.0 0.0 copy-done.4
  133.0 4.3 %collective-permute-start.1 = (f32[384,128]{1,0:T(8,128)S(1)}, f32[384,128]{1,0:T(8,128)S(1)}, u32[]{:S(2)}, u32[]{:S(2)}) collective-permute-start(f32[384,128]{1,0:T(8,128)S(1)} %copy-done.4), channel_id=1, source_target_pairs={{0,1},{1,2},{2,3},{3,4},{4,5},{5,6},{6,7},{8,9},{9,10},{10,11},{11... | collective-permute-start | bytes 589832 | tf_op jit(solution)/shard_map/ppermute | solution.py:277
  137.4 0.0 copy-done.3
  137.4 3.0 %collective-permute-start = (f32[384,128]{1,0:T(8,128)S(1)}, f32[384,128]{1,0:T(8,128)S(1)}, u32[]{:S(2)}, u32[]{:S(2)}) collective-permute-start(f32[384,128]{1,0:T(8,128)S(1)} %copy-done.3), channel_id=1, source_target_pairs={{1,0},{2,1},{3,2},{4,3},{5,4},{6,5},{7,6},{9,8},{10,9},{11,10},{12... | collective-permute-start | bytes 589832 | tf_op jit(solution)/shard_map/ppermute | solution.py:277
  140.4 1.2 slice.6
  141.6 3.6 %collective-permute-done.1.own_left_ref = f32[384,128]{1,0:T(8,128)S(1)} collective-permute-done((f32[384,128]{1,0:T(8,128)S(1)}, f32[384,128]{1,0:T(8,128)S(1)}, u32[]{:S(2)}, u32[]{:S(2)}) %collective-permute-start.1) | collective-permute-done | bytes 196640 | tf_op jit(solution)/shard_map/ppermute | solution.py:277
  145.2 0.0 copy-start.6
  145.2 0.7 copy-done.6
  145.9 11.0 %early.1 = (f32[384,128]{1,0:T(8,128)}, f32[384,128]{1,0:T(8,128)}) custom-call(s32[2]{0:T(128)} %add_convert_fusion.refs_0_.ends_ref, f32[384,128]{1,0:T(8,128)} %get-tuple-element.17.own_ref.refs_1_, f32[384,128]{1,0:T(8,128)} %copy-done.6), custom_call_target="tpu_custom_call" | custom-call | flops 500000000 | bytes 1000000 | tf_op jit(solution)/shard_map/early/pallas_call | solution.py:128
  156.8 0.0 collective-permute-done.refs_2_
  156.8 0.0 copy-start.5
  156.9 0.0 all-to-all-done.5
  156.9 0.0 copy-start
  156.9 0.7 copy-done.5
  157.5 0.1 copy-done
  157.6 31.1 %rotate.3 = (f32[256,256]{1,0:T(8,128)}, f32[256,256]{1,0:T(8,128)}, f32[256,256]{1,0:T(8,128)}, f32[8,128]{1,0:T(8,128)}) custom-call(s32[2]{0:T(128)} %add_convert_fusion.refs_0_.ends_ref, f32[384,128]{1,0:T(8,128)} %get-tuple-element.17.own_ref.refs_1_, f32[384,128]{1,0:T(8,128)} %copy-done.5, f32[384,128]{1,0:T(8,128)} %get-tuple-element.20.refs_3_, ...), custom_call_target="tpu_custom_call" | custom-call | flops 4000000000 | bytes 2000000 | tf_op jit(solution)/shard_map/rotate/pallas_call | solution.py:251
  188.8 1.2 slice.7
  190.0 5.4 %collective-permute-start.4 = (f32[256,256]{1,0:T(8,128)}, f32[256,256]{1,0:T(8,128)S(1)}, u32[]{:S(2)}, u32[]{:S(2)}) collective-permute-start(f32[256,256]{1,0:T(8,128)} %get-tuple-element.28), channel_id=1, source_target_pairs={{0,1},{1,2},{2,3},{3,4},{4,5},{5,6},{6,7},{8,9},{9,10},{10,11},{11... | collective-permute-start | bytes 786440 | tf_op jit(solution)/shard_map/ppermute | solution.py:277
  195.4 2.0 collective-permute-start.5
  197.3 1.3 pad_maximum_fusion.1
  198.7 12.2 %all_to_all.40 = f32[8,1,2]{2,1,0:T(1,128)S(1)} all-to-all(f32[8,1,2]{2,1,0:T(1,128)S(1)} %broadcast_in_dim.15), channel_id=1, replica_groups=mesh['row_0'=8,'row_1'=2,'row_2'=2,'col'=8] {'col'}, dimensions={0} | all-to-all | bytes 128 | tf_op jit(solution)/shard_map/all_to_all | solution.py:282
  210.9 0.5 multiply_sqrt_fusion
  211.5 0.0 collective-permute-done.4
  211.5 0.0 collective-permute-done.5
  211.5 1.0 broadcast_select_fusion.1
  212.5 0.9 pad_maximum_fusion
  (6 shorter events, 0.2 us)
Async XLA Ops:
  31.4 16.1 %all-to-all-start.2 = ((f32[16,40,128]{2,1,0:T(8,128)}), f32[16,40,128]{2,1,0:T(8,128)S(1)}, u32[]{:S(2)}, u32[]{:S(2)}) async-start(f32[16,40,128]{2,1,0:T(8,128)} %broadcast_in_dim.12), calls=%async_computation.2 | async-start | bytes 655360 | tf_op jit(solution)/shard_map/all_to_all | solution.py:266
  89.1 11.9 %collective-permute-start.2 = (f32[256,256]{1,0:T(8,128)}, f32[256,256]{1,0:T(8,128)S(1)}, u32[]{:S(2)}, u32[]{:S(2)}) collective-permute-start(f32[256,256]{1,0:T(8,128)} %get-tuple-element.23), channel_id=1, source_target_pairs={{0,1},{1,2},{2,3},{3,4},{4,5},{5,6},{6,7},{8,9},{9,10},{10,11},{11... | collective-permute-start | bytes 786440 | tf_op jit(solution)/shard_map/ppermute | solution.py:277
  93.5 14.2 %collective-permute-start.3 = (f32[256,256]{1,0:T(8,128)}, f32[256,256]{1,0:T(8,128)S(1)}, u32[]{:S(2)}, u32[]{:S(2)}) collective-permute-start(f32[256,256]{1,0:T(8,128)} %get-tuple-element.24), channel_id=1, source_target_pairs={{1,0},{2,1},{3,2},{4,3},{5,4},{6,5},{7,6},{9,8},{10,9},{11,10},{12... | collective-permute-start | bytes 786440 | tf_op jit(solution)/shard_map/ppermute | solution.py:277
  101.1 6.6 %copy-start.1 = (f32[256,256]{1,0:T(8,128)}, f32[256,256]{1,0:T(8,128)S(1)}, u32[]{:S(2)}) copy-start(f32[256,256]{1,0:T(8,128)S(1)} %collective-permute-done.2.from_left_ref) | copy-start | bytes 786436
  107.7 0.7 copy-start.2
  128.8 4.2 %copy-start.4 = (f32[384,128]{1,0:T(8,128)S(1)}, f32[384,128]{1,0:T(8,128)}, u32[]{:S(2)}) copy-start(f32[384,128]{1,0:T(8,128)} %get-tuple-element.19) | copy-start | bytes 589828
  128.8 8.6 %copy-start.3 = (f32[384,128]{1,0:T(8,128)S(1)}, f32[384,128]{1,0:T(8,128)}, u32[]{:S(2)}) copy-start(f32[384,128]{1,0:T(8,128)} %get-tuple-element.18) | copy-start | bytes 589828
  128.8 28.1 %all-to-all-start.5 = ((f32[32,16,128]{2,1,0:T(8,128)}), f32[32,16,128]{2,1,0:T(8,128)S(1)}, u32[]{:S(2)}, u32[]{:S(2)}) async-start(f32[32,16,128]{2,1,0:T(8,128)} %broadcast_in_dim.14), calls=%async_computation.5 | async-start | bytes 524288 | tf_op jit(solution)/shard_map/all_to_all | solution.py:266
  133.0 12.2 %collective-permute-start.1 = (f32[384,128]{1,0:T(8,128)S(1)}, f32[384,128]{1,0:T(8,128)S(1)}, u32[]{:S(2)}, u32[]{:S(2)}) collective-permute-start(f32[384,128]{1,0:T(8,128)S(1)} %copy-done.4), channel_id=1, source_target_pairs={{0,1},{1,2},{2,3},{3,4},{4,5},{5,6},{6,7},{8,9},{9,10},{10,11},{11... | collective-permute-start | bytes 589832 | tf_op jit(solution)/shard_map/ppermute | solution.py:277
  137.4 19.5 %collective-permute-start = (f32[384,128]{1,0:T(8,128)S(1)}, f32[384,128]{1,0:T(8,128)S(1)}, u32[]{:S(2)}, u32[]{:S(2)}) collective-permute-start(f32[384,128]{1,0:T(8,128)S(1)} %copy-done.3), channel_id=1, source_target_pairs={{1,0},{2,1},{3,2},{4,3},{5,4},{6,5},{7,6},{9,8},{10,9},{11,10},{12... | collective-permute-start | bytes 589832 | tf_op jit(solution)/shard_map/ppermute | solution.py:277
  145.2 0.7 copy-start.6
  156.8 0.7 copy-start.5
  156.9 0.8 copy-start
  190.0 21.5 %collective-permute-start.4 = (f32[256,256]{1,0:T(8,128)}, f32[256,256]{1,0:T(8,128)S(1)}, u32[]{:S(2)}, u32[]{:S(2)}) collective-permute-start(f32[256,256]{1,0:T(8,128)} %get-tuple-element.28), channel_id=1, source_target_pairs={{0,1},{1,2},{2,3},{3,4},{4,5},{5,6},{6,7},{8,9},{9,10},{10,11},{11... | collective-permute-start | bytes 786440 | tf_op jit(solution)/shard_map/ppermute | solution.py:277
  195.4 16.1 %collective-permute-start.5 = (f32[256,256]{1,0:T(8,128)}, f32[256,256]{1,0:T(8,128)S(1)}, u32[]{:S(2)}, u32[]{:S(2)}) collective-permute-start(f32[256,256]{1,0:T(8,128)} %get-tuple-element.29), channel_id=1, source_target_pairs={{1,0},{2,1},{3,2},{4,3},{5,4},{6,5},{7,6},{9,8},{10,9},{11,10},{12... | collective-permute-start | bytes 786440 | tf_op jit(solution)/shard_map/ppermute | solution.py:277

commit v4 on v3

--- a/solution.py
+++ b/solution.py
@@ -8,6 +8,7 @@
 from jax.sharding import Mesh
 from jax.sharding import PartitionSpec as P
 
+STEPS = 2
 ROW = ("row_0", "row_1", "row_2")
 CHIPS = ("row_0", "row_1")
 H = 256
@@ -74,15 +75,26 @@
 def tile(ij):
     i,j=ij
     return slice(i*T,(i+1)*T),slice(j*T,(j+1)*T)
-def gram_kernel(pair_ref,g_ref):
+def gram_kernel(ends_ref,pair_ref,keep_ref,give_ref,g_ref):
     where={ij:n for n,ij in enumerate(TOP+CROSS+BOTTOM)}
     for i in range(4):
         rows=dot(pair_ref[:,i*T:(i+1)*T],pair_ref[:,i*T:],0,0)
         for j in range(i,4):
             n=where[(i,j)]
             g_ref[n*T:(n+1)*T,:]=rows[:,(j-i)*T:(j-i+1)*T]
-def local_gram(pair):
-    return pl.pallas_call(gram_kernel,out_shape=jax.ShapeDtypeStruct((10*T,T),F32),in_specs=[VM],out_specs=VM,name="gram")(pair)
+    core=ends_ref[2]
+    keep_ref[...]=g_ref[pl.ds(pl.multiple_of(core*(5*T),T),5*T),:]
+    give_ref[...]=g_ref[pl.ds(pl.multiple_of((1-core)*(5*T),T),5*T),:]
+def local_gram(ends,pair):
+    half=jax.ShapeDtypeStruct((5*T,T),F32)
+    return pl.pallas_call(gram_kernel,out_shape=[half]*2,in_specs=[SM,VM],out_specs=[VM]*2,
+        scratch_shapes=[pltpu.VMEM((10*T,T),F32)],name="gram")(ends,pair)
+def place_kernel(ends_ref,own_ref,from_left_ref,from_right_ref,o_ref):
+    own=own_ref[...]
+    o_ref[:,:H]=jnp.where(ends_ref[0]==1,own,from_left_ref[...])
+    o_ref[:,H:]=jnp.where(ends_ref[1]==1,own,from_right_ref[...])
+def placed_blocks(*operands):
+    return pl.pallas_call(place_kernel,out_shape=jax.ShapeDtypeStruct((256,512),F32),in_specs=[SM]+[VM]*3,out_specs=VM,name="place")(*operands)
 def cross_kernel(ends_ref,top_ref,from_left_ref,from_right_ref,pair_ref,c_ref):
     own=top_ref[...]
     top=jnp.where(ends_ref[0]==1,own,from_left_ref[...])
@@ -138,11 +150,11 @@
     return jnp.broadcast_to(jnp.sum(cpl,axis=1,keepdims=True),(8,T))
 def rotate_kernel(first,*refs):
     if first:
-        ends_ref,g_ref,pair_ref,top_ref,bottom_ref,right_ref,own_top_ref,own_bottom_ref,own_right_ref,cpl_ref=refs[:10]
-        refs=refs[10:]
+        ends_ref,half_ref,rest_ref,pair_ref,top_ref,bottom_ref,right_ref,own_top_ref,own_bottom_ref,own_right_ref,cpl_ref=refs[:11]
+        refs=refs[11:]
     else:
-        ends_ref,own_ref,own_from_right_ref,up_ref,inv_ref,g_ref,pair_ref,top_ref,bottom_ref,right_ref,cpl_ref=refs[:11]
-        refs=refs[11:]
+        ends_ref,own_ref,own_from_right_ref,up_ref,inv_ref,g_ref,pair_ref,term_ref,top_ref,bottom_ref,right_ref,cpl_ref=refs[:12]
+        refs=refs[12:]
     A,U,V,W,RT,d_ref,u_ref,i_ref=refs
     sub=lax.broadcasted_iota(jnp.int32,(T,T),0); lane=lax.broadcasted_iota(jnp.int32,(T,T),1)
     eye=sub==lane
@@ -185,7 +197,8 @@
         RT[sl:sh,:]=dot(W[sl:sh,:sh],U[:sh,:],1,0)
     if first:
         for n,ij in enumerate(TOP+CROSS+BOTTOM):
-            A[tile(ij)]=g_ref[n*T:(n+1)*T,:]
+            m=(n%5)*T
+            A[tile(ij)]=jnp.where(ends_ref[2]==n//5,half_ref[m:m+T,:],rest_ref[m:m+T,:])
         d_ref[0]=A[:T,:T]
         d_ref[1]=jnp.where(eye,1.0,0.0).astype(F32)
         down=[down_of(A[tile((n,n))]) for n in (0,1)]
@@ -200,7 +213,11 @@
         sq=[jnp.sum(up_ref[n*T:(n+1)*T,:]*up_ref[n*T:(n+1)*T,:],axis=0,keepdims=True) for n in range(3)]
         down=[down_of(sq[0]),down_of(sq[1]+sq[2])]
         skip=2
-    cpl_ref[...]=coupling_sum(A,down,[along_of(2),along_of(3)])
+    term=coupling_sum(A,down,[along_of(2),along_of(3)])
+    if first:
+        cpl_ref[...]=term
+    else:
+        cpl_ref[...]=jnp.where(lane[:8]==0,term_ref[...],term)
     if not first:
         U[:T,H:]=dot(inv_ref[:T,:],A[:T,H:],1,0)
         U[T:H,H:]=dot(inv_ref[T:2*T,:],A[:T,H:],1,0)+dot(inv_ref[2*T:,:],A[T:H,H:],1,0)
@@ -266,9 +283,13 @@
     return lax.all_to_all(copies, axis, split_axis=0, concat_axis=0, tiled=True).reshape(-1, T)
 
 
-def row_total(value):
-    own = scattered_sum(scattered_sum(value, "row_2"), CHIPS)
-    return gathered(gathered(own, CHIPS), "row_2")
+def swapped(value):
+    return lax.ppermute(value, "row_2", [(0, 1), (1, 0)])
+
+
+def row_halves(keep, give):
+    half = gathered(scattered_sum(keep + swapped(give), CHIPS), CHIPS)
+    return half, swapped(half)
 
 
 def moved(value, steps):
@@ -277,18 +298,15 @@
     return lax.ppermute(value, "col", [(source, source + steps) for source in range(first, last)])
 
 
-def over_slots(terms):
-    copies = jnp.broadcast_to(terms, (lax.axis_size("col"), *terms.shape))
-    return jnp.sum(lax.all_to_all(copies, "col", split_axis=0, concat_axis=0, tiled=True), axis=0)
-
-
 def steps(matrix):
     place = lax.axis_index("col")
     at_start = place == 0
     at_end = place == lax.axis_size("col") - 1
-    ends = jnp.stack([at_start, at_end]).astype(jnp.int32)
-    total = row_total(local_gram(matrix))
-    top, bottom, right, own_top, own_bottom, own_right, term_0 = rotate(True, ends, total, matrix)
+    ends = jnp.stack([at_start, at_end, lax.axis_index("row_2")]).astype(jnp.int32)
+    half, rest = row_halves(*local_gram(ends, matrix))
+    top, bottom, right, own_top, own_bottom, own_right, term_0 = rotate(
+        True, ends, half, rest, matrix
+    )
     from_left = moved(right, 1)
     from_right = moved(bottom, -1)
     own_left = moved(own_right, 1)
@@ -297,16 +315,15 @@
     cross = scattered_sum(cross, ROW)
     cross = gathered(cross, ROW)
     up, inverse = early(ends, own_top, own_left)
-    top, bottom, right, term_1 = rotate(
-        False, ends, own_top, own_from_right, up, inverse, cross, pair
+    top, bottom, right, terms = rotate(
+        False, ends, own_top, own_from_right, up, inverse, cross, pair, term_0
     )
+    terms = lax.all_to_all(terms, "col", split_axis=0, concat_axis=0, tiled=True)
     from_left = moved(right, 1)
     from_right = moved(bottom, -1)
-    totals = over_slots(jnp.stack([term_0[0, 0], term_1[0, 0]]))
+    totals = jnp.sum(terms, axis=0)[:STEPS]
     coupling = jnp.sqrt(totals / (1.0 * lax.axis_size("col") * H))
-    rotated = jnp.concatenate(
-        [jnp.where(at_start, top, from_left), jnp.where(at_end, top, from_right)], axis=1
-    )
+    rotated = placed_blocks(ends, top, from_left, from_right)
     return (rotated, coupling)
 
 

time: 216 us -> 209 us (0.968)
  waiting for transfers between devices: 25.6 us -> 19.5 us
  blocking collectives: 61.8 us -> 67.2 us
  starting transfers between devices: 31 us -> 26.4 us
    all_to_all x1, blocking collectives: 5.02 us -> 15.9 us  [gathered(): lax.all_to_all(copies, axis, split_axis=0, concat_axis=0, tiled=True)]
    all_to_all x2 -> x1, waiting for transfers between devices: 10.8 us -> 0.01 us  [gathered(): lax.all_to_all(copies, axis, split_axis=0, concat_axis=0, tiled=True)]
    all_to_all x3 -> x2, blocking collectives: 44.5 us -> 39.1 us  [scattered_sum(): parts = lax.all_to_all(value.reshape(count, -1, T), axis, 0, 0, tiled=True)]
    all_to_all x2 -> x1, starting transfers between devices: 8.98 us -> 4.21 us  [gathered(): lax.all_to_all(copies, axis, split_axis=0, concat_axis=0, tiled=True)]
    ppermute x0 -> x2, waiting for transfers between devices: none -> 3.46 us  [swapped(): return lax.ppermute(value, 'row_2', [(0, 1), (1, 0)])]
    slice x2 -> x0, local copies, waits for them, and re-layouts: 2.39 us -> none  [steps(): totals = over_slots(jnp.stack([term_0[0, 0], term_1[0, 0]]))]
    pallas_call x1 -> x2, Pallas kernels: 2.78 us -> 4.75 us  [the longest x1 2.79 us: local_gram(): pl.pallas_call(gram_kernel, out_shape=[half] * 2, in_specs=[SM, VM], out_...]
  transfers between devices with their start and end apart: 8 -> 9, of which waited for: 4 -> 5; matrix products, arithmetic and copies ran while one was open for 2% -> 0% of each run, Pallas kernels for 5% -> 5%
where the time goes in v4:
time: 209 us; the launch traced here: 206 us
  Pallas kernels  85.7 us (41%)
  blocking collectives  67.2 us (32%)
  starting transfers between devices  26.4 us (13%)
  waiting for transfers between devices  19.5 us (9%)
  local copies, waits for them, and re-layouts  4.45 us (2%)
  other arithmetic  2.3 us (1%)
    pallas_call x2, Pallas kernels, rotate(): pl.pallas_call(functools.partial(rotate_kernel, first), out_shape=outs, i...  67.7 us
    all_to_all x2, blocking collectives, scattered_sum(): parts = lax.all_to_all(value.reshape(count, -1, T), axis, 0, 0, tiled=True)  39.1 us
    ppermute x6, starting transfers between devices, moved(): lax.ppermute(value, 'col', [(source, source + steps) for source in range(...  22.2 us
    ppermute x6, waiting for transfers between devices, moved(): lax.ppermute(value, 'col', [(source, source + steps) for source in range(...  16 us
    all_to_all x1, blocking collectives, gathered(): lax.all_to_all(copies, axis, split_axis=0, concat_axis=0, tiled=True)  15.9 us
    all_to_all x1, blocking collectives, steps(): lax.all_to_all(terms, 'col', split_axis=0, concat_axis=0, tiled=True)  12.3 us
    pallas_call x1, Pallas kernels, early(): pl.pallas_call(early_kernel, out_shape=[own] * 2, in_specs=[SM, VM, VM],...  11 us
    all_to_all x1, starting transfers between devices, gathered(): lax.all_to_all(copies, axis, split_axis=0, concat_axis=0, tiled=True)  4.21 us
  transfers between devices with their start and end apart: 9, of which 5 were waited for; matrix products, arithmetic and copies ran while one was open for 0% of the time, Pallas kernels for 5%

profile of v4, /device:TPU:6, one launch (start us, length us, event | category | flops | bytes accessed | tf_op | source)
XLA Modules:
  0.0 206.3 jit_solution(16230522905793944942)
XLA Ops:
  0.6 0.7 pad_add_fusion.ends_ref.refs_0_
  1.3 2.8 %gram.1 = (f32[640,128]{1,0:T(8,128)}, f32[640,128]{1,0:T(8,128)}) custom-call(s32[3]{0:T(128)} %pad_add_fusion.ends_ref.refs_0_, f32[256,512]{1,0:T(8,128)} %refs_3_.1), custom_call_target="tpu_custom_call" | custom-call | tf_op jit(solution)/shard_map/gram/pallas_call | solution.py:90
  4.1 0.0 collective-permute-start
  4.1 1.8 collective-permute-done
  5.9 1.0 add.3
  7.0 21.9 %all_to_all.29 = f32[16,40,128]{2,1,0:T(8,128)S(1)} all-to-all(f32[16,40,128]{2,1,0:T(8,128)S(1)} %bitcast.10), channel_id=1, replica_groups=mesh['row_0'=8,'row_1'=2,'row_2'=2,'col'=8] {'row_0','row_1'}, dimensions={0} | all-to-all | bytes 655360 | tf_op jit(solution)/shard_map/all_to_all | solution.py:277
  28.9 15.9 %all_to_all.30 = f32[16,40,128]{2,1,0:T(8,128)S(1)} all-to-all(f32[16,40,128]{2,1,0:T(8,128)S(1)} %broadcast_in_dim.6), channel_id=1, replica_groups=mesh['row_0'=8,'row_1'=2,'row_2'=2,'col'=8] {'row_0','row_1'}, dimensions={0} | all-to-all | bytes 655360 | tf_op jit(solution)/shard_map/all_to_all | solution.py:283
  44.8 0.0 copy-start
  44.8 0.0 collective-permute-start.1
  44.8 1.6 collective-permute-done.1.refs_2_
  46.5 0.0 copy-done
  46.5 0.0 copy-start.7
  46.5 0.7 copy-done.7
  47.2 36.6 %rotate.2 = (f32[256,256]{1,0:T(8,128)}, f32[256,256]{1,0:T(8,128)}, f32[256,256]{1,0:T(8,128)}, f32[384,128]{1,0:T(8,128)}, f32[384,128]{1,0:T(8,128)}, /*index=5*/f32[384,128]{1,0:T(8,128)}, f32[8,128]{1,0:T(8,128)}) custom-call(s32[3]{0:T(128)} %pad_add_fusion.ends_ref.refs_0_, f32[640,128]{1,0:T(8,128)} %bitcast.12, f32[640,128]{1,0:T(8,128)} %copy-done.7, ...), custom_call_target="tpu_custom_call" | custom-call | flops 4000000000 | bytes 2000000 | tf_op jit(solution)/shard_map/rotate/pallas_call | solution.py:268
  83.8 4.3 %collective-permute-start.4 = (f32[256,256]{1,0:T(8,128)}, f32[256,256]{1,0:T(8,128)S(1)}, u32[]{:S(2)}, u32[]{:S(2)}) collective-permute-start(f32[256,256]{1,0:T(8,128)} %get-tuple-element.27), channel_id=1, source_target_pairs={{0,1},{1,2},{2,3},{3,4},{4,5},{5,6},{6,7},{8,9},{9,10},{10,11},{11... | collective-permute-start | bytes 786440 | tf_op jit(solution)/shard_map/ppermute | solution.py:298
  88.1 3.0 %collective-permute-start.5 = (f32[256,256]{1,0:T(8,128)}, f32[256,256]{1,0:T(8,128)S(1)}, u32[]{:S(2)}, u32[]{:S(2)}) collective-permute-start(f32[256,256]{1,0:T(8,128)} %get-tuple-element.28), channel_id=1, source_target_pairs={{1,0},{2,1},{3,2},{4,3},{5,4},{6,5},{7,6},{9,8},{10,9},{11,10},{12... | collective-permute-start | bytes 786440 | tf_op jit(solution)/shard_map/ppermute | solution.py:298
  91.1 4.6 %collective-permute-done.4.from_left_ref = f32[256,256]{1,0:T(8,128)S(1)} collective-permute-done((f32[256,256]{1,0:T(8,128)}, f32[256,256]{1,0:T(8,128)S(1)}, u32[]{:S(2)}, u32[]{:S(2)}) %collective-permute-start.4) | collective-permute-done | bytes 262176 | tf_op jit(solution)/shard_map/ppermute | solution.py:298
  95.7 0.0 copy-start.4
  95.7 6.6 %collective-permute-done.5.from_right_ref = f32[256,256]{1,0:T(8,128)S(1)} collective-permute-done((f32[256,256]{1,0:T(8,128)}, f32[256,256]{1,0:T(8,128)S(1)}, u32[]{:S(2)}, u32[]{:S(2)}) %collective-permute-start.5) | collective-permute-done | bytes 262176 | tf_op jit(solution)/shard_map/ppermute | solution.py:298
  102.4 0.0 copy-start.5
  102.4 0.0 copy-done.4
  102.4 0.7 copy-done.5
  103.1 2.3 %cross.1 = (f32[256,512]{1,0:T(8,128)}, f32[512,128]{1,0:T(8,128)}) custom-call(s32[3]{0:T(128)} %pad_add_fusion.ends_ref.refs_0_, f32[256,256]{1,0:T(8,128)} %get-tuple-element.26.top_ref, f32[256,256]{1,0:T(8,128)} %copy-done.4, f32[256,256]{1,0:T(8,128)} %copy-done.5), custom_call_target="tpu_custom_call" | custom-call | tf_op jit(solution)/shard_map/cross/pallas_call | solution.py:109
  105.3 17.2 %all_to_all.31 = f32[32,16,128]{2,1,0:T(8,128)S(1)} all-to-all(f32[32,16,128]{2,1,0:T(8,128)} %bitcast.14), channel_id=1, replica_groups=mesh['row_0'=8,'row_1'=2,'row_2'=2,'col'=8] {'row_0','row_1','row_2'}, dimensions={0} | all-to-all | bytes 524288 | tf_op jit(solution)/shard_map/all_to_all | solution.py:277
  122.6 0.7 broadcast_in_dim.7
  123.3 0.0 copy-start.9
  123.3 0.0 copy-start.8
  123.3 4.2 %all-to-all-start.3 = ((f32[32,16,128]{2,1,0:T(8,128)}), f32[32,16,128]{2,1,0:T(8,128)S(1)}, u32[]{:S(2)}, u32[]{:S(2)}) async-start(f32[32,16,128]{2,1,0:T(8,128)} %broadcast_in_dim.7), calls=%async_computation.3 | async-start | bytes 524288 | tf_op jit(solution)/shard_map/all_to_all | solution.py:283
  127.5 0.0 copy-done.9
  127.5 4.3 %collective-permute-start.3 = (f32[384,128]{1,0:T(8,128)S(1)}, f32[384,128]{1,0:T(8,128)S(1)}, u32[]{:S(2)}, u32[]{:S(2)}) collective-permute-start(f32[384,128]{1,0:T(8,128)S(1)} %copy-done.9), channel_id=1, source_target_pairs={{0,1},{1,2},{2,3},{3,4},{4,5},{5,6},{6,7},{8,9},{9,10},{10,11},{11... | collective-permute-start | bytes 589832 | tf_op jit(solution)/shard_map/ppermute | solution.py:298
  131.9 0.0 copy-done.8
  131.9 3.0 %collective-permute-start.2 = (f32[384,128]{1,0:T(8,128)S(1)}, f32[384,128]{1,0:T(8,128)S(1)}, u32[]{:S(2)}, u32[]{:S(2)}) collective-permute-start(f32[384,128]{1,0:T(8,128)S(1)} %copy-done.8), channel_id=1, source_target_pairs={{1,0},{2,1},{3,2},{4,3},{5,4},{6,5},{7,6},{9,8},{10,9},{11,10},{12... | collective-permute-start | bytes 589832 | tf_op jit(solution)/shard_map/ppermute | solution.py:298
  134.9 4.8 %collective-permute-done.3.own_left_ref = f32[384,128]{1,0:T(8,128)S(1)} collective-permute-done((f32[384,128]{1,0:T(8,128)S(1)}, f32[384,128]{1,0:T(8,128)S(1)}, u32[]{:S(2)}, u32[]{:S(2)}) %collective-permute-start.3) | collective-permute-done | bytes 196640 | tf_op jit(solution)/shard_map/ppermute | solution.py:298
  139.7 0.0 copy-start.11
  139.7 0.7 copy-done.11
  140.4 11.0 %early.1 = (f32[384,128]{1,0:T(8,128)}, f32[384,128]{1,0:T(8,128)}) custom-call(s32[3]{0:T(128)} %pad_add_fusion.ends_ref.refs_0_, f32[384,128]{1,0:T(8,128)} %get-tuple-element.21.own_ref.refs_1_, f32[384,128]{1,0:T(8,128)} %copy-done.11), custom_call_target="tpu_custom_call" | custom-call | flops 500000000 | bytes 1000000 | tf_op jit(solution)/shard_map/early/pallas_call | solution.py:140
  151.3 0.0 collective-permute-done.2.refs_2_
  151.3 0.0 copy-start.10
  151.3 0.0 all-to-all-done.3
  151.4 0.0 copy-start.3
  151.4 0.7 copy-done.10
  152.0 0.1 copy-done.3
  152.1 31.1 %rotate.3 = (f32[256,256]{1,0:T(8,128)}, f32[256,256]{1,0:T(8,128)}, f32[256,256]{1,0:T(8,128)}, f32[8,128]{1,0:T(8,128)}) custom-call(s32[3]{0:T(128)} %pad_add_fusion.ends_ref.refs_0_, f32[384,128]{1,0:T(8,128)} %get-tuple-element.21.own_ref.refs_1_, f32[384,128]{1,0:T(8,128)} %copy-done.10, f32[384,128]{1,0:T(8,128)} %get-tuple-element.24.refs_3_, ...), custom_call_target="tpu_custom_call" | custom-call | flops 4000000000 | bytes 2000000 | tf_op jit(solution)/shard_map/rotate/pallas_call | solution.py:268
  183.2 0.0 copy-start.6
  183.2 5.5 %collective-permute-start.6 = (f32[256,256]{1,0:T(8,128)}, f32[256,256]{1,0:T(8,128)S(1)}, u32[]{:S(2)}, u32[]{:S(2)}) collective-permute-start(f32[256,256]{1,0:T(8,128)} %get-tuple-element.33), channel_id=1, source_target_pairs={{0,1},{1,2},{2,3},{3,4},{4,5},{5,6},{6,7},{8,9},{9,10},{10,11},{11... | collective-permute-start | bytes 786440 | tf_op jit(solution)/shard_map/ppermute | solution.py:298
  188.8 1.9 collective-permute-start.7
  190.7 0.0 copy-done.6
  190.8 12.3 %all_to_all.32 = f32[8,1,128]{2,1,0:T(1,128)S(1)} all-to-all(f32[8,1,128]{2,1,0:T(1,128)S(1)} %bitcast.15), channel_id=1, replica_groups=mesh['row_0'=8,'row_1'=2,'row_2'=2,'col'=8] {'col'}, dimensions={0} | all-to-all | bytes 8192 | tf_op jit(solution)/shard_map/all_to_all | solution.py:321
  203.0 0.5 multiply_sqrt_fusion
  203.6 0.0 collective-permute-done.6.from_left_ref
  203.6 0.0 copy-start.1
  203.6 0.0 collective-permute-done.7.from_right_ref
  203.6 0.0 copy-start.2
  203.6 0.7 copy-done.1
  204.3 0.1 copy-done.2
  204.4 2.0 place.1
  (4 shorter events, 0.1 us)
Async XLA Ops:
  4.1 1.8 collective-permute-start
  44.8 1.6 copy-start
  44.8 1.6 collective-permute-start.1
  46.5 0.7 copy-start.7
  83.8 11.9 %collective-permute-start.4 = (f32[256,256]{1,0:T(8,128)}, f32[256,256]{1,0:T(8,128)S(1)}, u32[]{:S(2)}, u32[]{:S(2)}) collective-permute-start(f32[256,256]{1,0:T(8,128)} %get-tuple-element.27), channel_id=1, source_target_pairs={{0,1},{1,2},{2,3},{3,4},{4,5},{5,6},{6,7},{8,9},{9,10},{10,11},{11... | collective-permute-start | bytes 786440 | tf_op jit(solution)/shard_map/ppermute | solution.py:298
  88.1 14.2 %collective-permute-start.5 = (f32[256,256]{1,0:T(8,128)}, f32[256,256]{1,0:T(8,128)S(1)}, u32[]{:S(2)}, u32[]{:S(2)}) collective-permute-start(f32[256,256]{1,0:T(8,128)} %get-tuple-element.28), channel_id=1, source_target_pairs={{1,0},{2,1},{3,2},{4,3},{5,4},{6,5},{7,6},{9,8},{10,9},{11,10},{12... | collective-permute-start | bytes 786440 | tf_op jit(solution)/shard_map/ppermute | solution.py:298
  95.7 6.6 %copy-start.4 = (f32[256,256]{1,0:T(8,128)}, f32[256,256]{1,0:T(8,128)S(1)}, u32[]{:S(2)}) copy-start(f32[256,256]{1,0:T(8,128)S(1)} %collective-permute-done.4.from_left_ref) | copy-start | bytes 786436
  102.4 0.7 copy-start.5
  123.3 4.2 %copy-start.9 = (f32[384,128]{1,0:T(8,128)S(1)}, f32[384,128]{1,0:T(8,128)}, u32[]{:S(2)}) copy-start(f32[384,128]{1,0:T(8,128)} %get-tuple-element.23) | copy-start | bytes 589828
  123.3 8.6 %copy-start.8 = (f32[384,128]{1,0:T(8,128)S(1)}, f32[384,128]{1,0:T(8,128)}, u32[]{:S(2)}) copy-start(f32[384,128]{1,0:T(8,128)} %get-tuple-element.22) | copy-start | bytes 589828
  123.3 28.0 %all-to-all-start.3 = ((f32[32,16,128]{2,1,0:T(8,128)}), f32[32,16,128]{2,1,0:T(8,128)S(1)}, u32[]{:S(2)}, u32[]{:S(2)}) async-start(f32[32,16,128]{2,1,0:T(8,128)} %broadcast_in_dim.7), calls=%async_computation.3 | async-start | bytes 524288 | tf_op jit(solution)/shard_map/all_to_all | solution.py:283
  127.5 12.2 %collective-permute-start.3 = (f32[384,128]{1,0:T(8,128)S(1)}, f32[384,128]{1,0:T(8,128)S(1)}, u32[]{:S(2)}, u32[]{:S(2)}) collective-permute-start(f32[384,128]{1,0:T(8,128)S(1)} %copy-done.9), channel_id=1, source_target_pairs={{0,1},{1,2},{2,3},{3,4},{4,5},{5,6},{6,7},{8,9},{9,10},{10,11},{11... | collective-permute-start | bytes 589832 | tf_op jit(solution)/shard_map/ppermute | solution.py:298
  131.9 19.5 %collective-permute-start.2 = (f32[384,128]{1,0:T(8,128)S(1)}, f32[384,128]{1,0:T(8,128)S(1)}, u32[]{:S(2)}, u32[]{:S(2)}) collective-permute-start(f32[384,128]{1,0:T(8,128)S(1)} %copy-done.8), channel_id=1, source_target_pairs={{1,0},{2,1},{3,2},{4,3},{5,4},{6,5},{7,6},{9,8},{10,9},{11,10},{12... | collective-permute-start | bytes 589832 | tf_op jit(solution)/shard_map/ppermute | solution.py:298
  139.7 0.7 copy-start.11
  151.3 0.7 copy-start.10
  151.4 0.8 copy-start.3
  183.2 7.5 %copy-start.6 = (f32[8,128]{1,0:T(8,128)S(1)}, f32[8,128]{1,0:T(8,128)}, u32[]{:S(2)}) copy-start(f32[8,128]{1,0:T(8,128)} %get-tuple-element.35) | copy-start | bytes 12292
  183.2 20.3 %collective-permute-start.6 = (f32[256,256]{1,0:T(8,128)}, f32[256,256]{1,0:T(8,128)S(1)}, u32[]{:S(2)}, u32[]{:S(2)}) collective-permute-start(f32[256,256]{1,0:T(8,128)} %get-tuple-element.33), channel_id=1, source_target_pairs={{0,1},{1,2},{2,3},{3,4},{4,5},{5,6},{6,7},{8,9},{9,10},{10,11},{11... | collective-permute-start | bytes 786440 | tf_op jit(solution)/shard_map/ppermute | solution.py:298
  188.8 14.8 %collective-permute-start.7 = (f32[256,256]{1,0:T(8,128)}, f32[256,256]{1,0:T(8,128)S(1)}, u32[]{:S(2)}, u32[]{:S(2)}) collective-permute-start(f32[256,256]{1,0:T(8,128)} %get-tuple-element.34), channel_id=1, source_target_pairs={{1,0},{2,1},{3,2},{4,3},{5,4},{6,5},{7,6},{9,8},{10,9},{11,10},{12... | collective-permute-start | bytes 786440 | tf_op jit(solution)/shard_map/ppermute | solution.py:298
  203.6 0.7 copy-start.1
  203.6 0.8 copy-start.2

commit v5 on v4

--- a/solution.py
+++ b/solution.py
@@ -88,13 +88,7 @@
 def local_gram(ends,pair):
     half=jax.ShapeDtypeStruct((5*T,T),F32)
     return pl.pallas_call(gram_kernel,out_shape=[half]*2,in_specs=[SM,VM],out_specs=[VM]*2,
-        scratch_shapes=[pltpu.VMEM((10*T,T),F32)],name="gram")(ends,pair)
-def place_kernel(ends_ref,own_ref,from_left_ref,from_right_ref,o_ref):
-    own=own_ref[...]
-    o_ref[:,:H]=jnp.where(ends_ref[0]==1,own,from_left_ref[...])
-    o_ref[:,H:]=jnp.where(ends_ref[1]==1,own,from_right_ref[...])
-def placed_blocks(*operands):
-    return pl.pallas_call(place_kernel,out_shape=jax.ShapeDtypeStruct((256,512),F32),in_specs=[SM]+[VM]*3,out_specs=VM,name="place")(*operands)
+        scratch_shapes=[pltpu.VMEM((10*T,T),F32)],compiler_params=pltpu.CompilerParams(vmem_limit_bytes=16 * 2**20),name="gram")(ends,pair)
 def cross_kernel(ends_ref,top_ref,from_left_ref,from_right_ref,pair_ref,c_ref):
     own=top_ref[...]
     top=jnp.where(ends_ref[0]==1,own,from_left_ref[...])
@@ -107,7 +101,7 @@
         c_ref[(2*i+1)*T:(2*i+2)*T,:]=rows[:,T:]
 def local_cross(ends,top,from_left,from_right):
     return pl.pallas_call(cross_kernel,out_shape=[jax.ShapeDtypeStruct((256,512),F32),jax.ShapeDtypeStruct((4*T,T),F32)],
-        in_specs=[SM,VM,VM,VM],out_specs=[VM]*2,name="cross")(ends,top,from_left,from_right)
+        in_specs=[SM,VM,VM,VM],out_specs=[VM]*2,compiler_params=pltpu.CompilerParams(vmem_limit_bytes=16 * 2**20),name="cross")(ends,top,from_left,from_right)
 def spread_leaves(d_ref,u_ref,i_ref,count):
     us,is_=leaves([[d_ref[a,8*q:8*q+8,:] for q in range(T//8)] for a in range(count)])
     for a in range(count):
@@ -140,7 +134,7 @@
     return pl.pallas_call(early_kernel,out_shape=[own]*2,in_specs=[SM,VM,VM],out_specs=[VM]*2,
         scratch_shapes=[pltpu.VMEM((1,T,T),F32)]*3,
         cost_estimate=pl.CostEstimate(flops=500_000_000,bytes_accessed=1_000_000,transcendentals=0),
-        name="early")(*operands)
+        compiler_params=pltpu.CompilerParams(vmem_limit_bytes=16 * 2**20),name="early")(*operands)
 def coupling_sum(A,down,along):
     cpl=jnp.zeros((1,T),F32)
     for i in (0,1):
@@ -269,7 +263,7 @@
         in_specs=[SM]+[VM]*(len(operands)-1),out_specs=[VM]*len(outs),
         scratch_shapes=[pltpu.VMEM((N,N),F32)]*5+[pltpu.VMEM((2,T,T),F32)]*3,
         cost_estimate=pl.CostEstimate(flops=4_000_000_000,bytes_accessed=2_000_000,transcendentals=0),
-        name="rotate")(*operands)
+        compiler_params=pltpu.CompilerParams(vmem_limit_bytes=32 * 2**20),name="rotate")(*operands)
 
 
 def scattered_sum(value, axis):
@@ -323,7 +317,9 @@
     from_right = moved(bottom, -1)
     totals = jnp.sum(terms, axis=0)[:STEPS]
     coupling = jnp.sqrt(totals / (1.0 * lax.axis_size("col") * H))
-    rotated = placed_blocks(ends, top, from_left, from_right)
+    rotated = jnp.concatenate(
+        [jnp.where(at_start, top, from_left), jnp.where(at_end, top, from_right)], axis=1
+    )
     return (rotated, coupling)
 
 

time: 209 us -> 195 us (0.933)
  Pallas kernels: 85.7 us -> 76.7 us
  local copies, waits for them, and re-layouts: 4.45 us -> 1.79 us
    pallas_call x2, Pallas kernels: 67.7 us -> 64.5 us  [rotate(): pl.pallas_call(functools.partial(rotate_kernel, first), out_shape=outs, i...]
    unnamed x24 -> x4, local copies, waits for them, and re-layouts: 3.69 us -> 1.05 us
where the time goes in v5:
time: 195 us; the launch traced here: 193 us
  Pallas kernels  76.7 us (39%)
  blocking collectives  66.5 us (34%)
  starting transfers between devices  26.3 us (13%)
  waiting for transfers between devices  19.1 us (10%)
    pallas_call x2, Pallas kernels, rotate(): pl.pallas_call(functools.partial(rotate_kernel, first), out_shape=outs, i...  64.5 us
    all_to_all x2, blocking collectives, scattered_sum(): parts = lax.all_to_all(value.reshape(count, -1, T), axis, 0, 0, tiled=True)  38.2 us
    ppermute x6, starting transfers between devices, moved(): lax.ppermute(value, 'col', [(source, source + steps) for source in range(...  22.1 us
    all_to_all x1, blocking collectives, gathered(): lax.all_to_all(copies, axis, split_axis=0, concat_axis=0, tiled=True)  16 us
    ppermute x6, waiting for transfers between devices, moved(): lax.ppermute(value, 'col', [(source, source + steps) for source in range(...  15.8 us
    all_to_all x1, blocking collectives, steps(): lax.all_to_all(terms, 'col', split_axis=0, concat_axis=0, tiled=True)  12.3 us
    pallas_call x1, Pallas kernels, early(): pl.pallas_call(early_kernel, out_shape=[own] * 2, in_specs=[SM, VM, VM],...  9.74 us
    all_to_all x1, starting transfers between devices, gathered(): lax.all_to_all(copies, axis, split_axis=0, concat_axis=0, tiled=True)  4.1 us
  transfers between devices with their start and end apart: 9, of which 5 were waited for; matrix products, arithmetic and copies ran while one was open for 0% of the time, Pallas kernels for 5%

profile of v5, /device:TPU:6, one launch (start us, length us, event | category | flops | bytes accessed | tf_op | source)
XLA Modules:
  0.0 192.7 jit_solution(15850779161414210843)
XLA Ops:
  0.6 0.1 pad_add_fusion.ends_ref.refs_0_
  0.7 0.0 copy-start
  0.7 1.0 copy-done
  1.8 1.5 gram.1
  3.3 0.1 collective-permute-start
  3.4 1.6 collective-permute-done
  5.0 21.9 %all_to_all.29 = f32[16,40,128]{2,1,0:T(8,128)S(1)} all-to-all(f32[16,40,128]{2,1,0:T(8,128)S(1)} %bitcast.15), channel_id=1, replica_groups=mesh['row_0'=8,'row_1'=2,'row_2'=2,'col'=8] {'row_0','row_1'}, dimensions={0} | all-to-all | bytes 655360 | tf_op jit(solution)/shard_map/all_to_all | solution.py:271
  26.9 0.0 copy-start.1
  27.0 16.0 %all_to_all.30 = f32[16,40,128]{2,1,0:T(8,128)S(1)} all-to-all(f32[16,40,128]{2,1,0:T(8,128)S(1)} %broadcast_in_dim.6), channel_id=1, replica_groups=mesh['row_0'=8,'row_1'=2,'row_2'=2,'col'=8] {'row_0','row_1'}, dimensions={0} | all-to-all | bytes 655360 | tf_op jit(solution)/shard_map/all_to_all | solution.py:277
  43.0 0.0 collective-permute-start.1
  43.0 1.6 collective-permute-done.1.refs_2_
  44.6 0.0 copy-done.1
  44.7 35.1 %rotate.2 = (f32[256,256]{1,0:T(8,128)S(1)}, f32[256,256]{1,0:T(8,128)S(1)}, f32[256,256]{1,0:T(8,128)S(1)}, f32[384,128]{1,0:T(8,128)S(1)}, f32[384,128]{1,0:T(...) custom-call(s32[3]{0:T(128)S(1)} %pad_add_fusion.ends_ref.refs_0_, f32[640,128]{1,0:T(8,128)S(1)} %bitcast.11, ...), custom_call_target="tpu_custom_call" | custom-call | flops 4000000000 | bytes 2000000 | tf_op jit(solution)/shard_map/rotate/pallas_call | solution.py:262
  79.8 4.3 %collective-permute-start.4 = (f32[256,256]{1,0:T(8,128)S(1)}, f32[256,256]{1,0:T(8,128)S(1)}, u32[]{:S(2)}, u32[]{:S(2)}) collective-permute-start(f32[256,256]{1,0:T(8,128)S(1)} %get-tuple-element.27), channel_id=1, source_target_pairs={{0,1},{1,2},{2,3},{3,4},{4,5},{5,6},{6,7},{8,9},{9,10},{10,11},{11... | collective-permute-start | bytes 786440 | tf_op jit(solution)/shard_map/ppermute | solution.py:292
  84.1 3.0 %collective-permute-start.5 = (f32[256,256]{1,0:T(8,128)S(1)}, f32[256,256]{1,0:T(8,128)S(1)}, u32[]{:S(2)}, u32[]{:S(2)}) collective-permute-start(f32[256,256]{1,0:T(8,128)S(1)} %get-tuple-element.28), channel_id=1, source_target_pairs={{1,0},{2,1},{3,2},{4,3},{5,4},{6,5},{7,6},{9,8},{10,9},{11,10},{12... | collective-permute-start | bytes 786440 | tf_op jit(solution)/shard_map/ppermute | solution.py:292
  87.2 4.4 %collective-permute-done.4.from_left_ref = f32[256,256]{1,0:T(8,128)S(1)} collective-permute-done((f32[256,256]{1,0:T(8,128)S(1)}, f32[256,256]{1,0:T(8,128)S(1)}, u32[]{:S(2)}, u32[]{:S(2)}) %collective-permute-start.4) | collective-permute-done | bytes 262176 | tf_op jit(solution)/shard_map/ppermute | solution.py:292
  91.6 6.6 %collective-permute-done.5.from_right_ref = f32[256,256]{1,0:T(8,128)S(1)} collective-permute-done((f32[256,256]{1,0:T(8,128)S(1)}, f32[256,256]{1,0:T(8,128)S(1)}, u32[]{:S(2)}, u32[]{:S(2)}) %collective-permute-start.5) | collective-permute-done | bytes 262176 | tf_op jit(solution)/shard_map/ppermute | solution.py:292
  98.2 1.0 cross.1
  99.2 16.3 %all_to_all.31 = f32[32,16,128]{2,1,0:T(8,128)S(1)} all-to-all(f32[32,16,128]{2,1,0:T(8,128)S(1)} %bitcast.13), channel_id=1, replica_groups=mesh['row_0'=8,'row_1'=2,'row_2'=2,'col'=8] {'row_0','row_1','row_2'}, dimensions={0} | all-to-all | bytes 524288 | tf_op jit(solution)/shard_map/all_to_all | solution.py:271
  115.5 0.7 broadcast_in_dim.7
  116.2 4.1 %all-to-all-start.3 = ((f32[32,16,128]{2,1,0:T(8,128)}), f32[32,16,128]{2,1,0:T(8,128)S(1)}, u32[]{:S(2)}, u32[]{:S(2)}) async-start(f32[32,16,128]{2,1,0:T(8,128)} %broadcast_in_dim.7), calls=%async_computation.3 | async-start | bytes 524288 | tf_op jit(solution)/shard_map/all_to_all | solution.py:277
  120.4 4.3 %collective-permute-start.3 = (f32[384,128]{1,0:T(8,128)S(1)}, f32[384,128]{1,0:T(8,128)S(1)}, u32[]{:S(2)}, u32[]{:S(2)}) collective-permute-start(f32[384,128]{1,0:T(8,128)S(1)} %get-tuple-element.23), channel_id=1, source_target_pairs={{0,1},{1,2},{2,3},{3,4},{4,5},{5,6},{6,7},{8,9},{9,10},{10,11},{11... | collective-permute-start | bytes 589832 | tf_op jit(solution)/shard_map/ppermute | solution.py:292
  124.7 3.0 %collective-permute-start.2 = (f32[384,128]{1,0:T(8,128)S(1)}, f32[384,128]{1,0:T(8,128)S(1)}, u32[]{:S(2)}, u32[]{:S(2)}) collective-permute-start(f32[384,128]{1,0:T(8,128)S(1)} %get-tuple-element.22), channel_id=1, source_target_pairs={{1,0},{2,1},{3,2},{4,3},{5,4},{6,5},{7,6},{9,8},{10,9},{11,10},{12... | collective-permute-start | bytes 589832 | tf_op jit(solution)/shard_map/ppermute | solution.py:292
  127.7 4.8 %collective-permute-done.3.own_left_ref = f32[384,128]{1,0:T(8,128)S(1)} collective-permute-done((f32[384,128]{1,0:T(8,128)S(1)}, f32[384,128]{1,0:T(8,128)S(1)}, u32[]{:S(2)}, u32[]{:S(2)}) %collective-permute-start.3) | collective-permute-done | bytes 196640 | tf_op jit(solution)/shard_map/ppermute | solution.py:292
  132.5 9.7 %early.1 = (f32[384,128]{1,0:T(8,128)S(1)}, f32[384,128]{1,0:T(8,128)S(1)}) custom-call(s32[3]{0:T(128)S(1)} %pad_add_fusion.ends_ref.refs_0_, f32[384,128]{1,0:T(8,128)S(1)} %get-tuple-element.21.own_ref.refs_1_, f32[384,128]{1,0:T(8,128)S(1)} %collective-permute-done.3.own_left_ref), custom_call_target="tpu_custom_call" | custom-call | flops 500000000 | bytes 1000000 | tf_op jit(solution)/shard_map/early/pallas_call | solution.py:134
  142.3 0.0 collective-permute-done.2.refs_2_
  142.3 0.0 all-to-all-done.3
  142.3 29.3 %rotate.3 = (f32[256,256]{1,0:T(8,128)S(1)}, f32[256,256]{1,0:T(8,128)S(1)}, f32[256,256]{1,0:T(8,128)S(1)}, f32[8,128]{1,0:T(8,128)S(1)}) custom-call(s32[3]{0:T(128)S(1)} %pad_add_fusion.ends_ref.refs_0_, f32[384,128]{1,0:T(8,128)S(1)} %get-tuple-element.21.own_ref.refs_1_, f32[384,128]{1,0:T(8,128)S(1)} %collective-permute-done.2.refs_2_, ...), custom_call_target="tpu_custom_call" | custom-call | flops 4000000000 | bytes 2000000 | tf_op jit(solution)/shard_map/rotate/pallas_call | solution.py:262
  171.6 5.4 %collective-permute-start.6 = (f32[256,256]{1,0:T(8,128)S(1)}, f32[256,256]{1,0:T(8,128)S(1)}, u32[]{:S(2)}, u32[]{:S(2)}) collective-permute-start(f32[256,256]{1,0:T(8,128)S(1)} %get-tuple-element.33), channel_id=1, source_target_pairs={{0,1},{1,2},{2,3},{3,4},{4,5},{5,6},{6,7},{8,9},{9,10},{10,11},{11... | collective-permute-start | bytes 786440 | tf_op jit(solution)/shard_map/ppermute | solution.py:292
  177.1 1.9 %collective-permute-start.7 = (f32[256,256]{1,0:T(8,128)S(1)}, f32[256,256]{1,0:T(8,128)S(1)}, u32[]{:S(2)}, u32[]{:S(2)}) collective-permute-start(f32[256,256]{1,0:T(8,128)S(1)} %get-tuple-element.34), channel_id=1, source_target_pairs={{1,0},{2,1},{3,2},{4,3},{5,4},{6,5},{7,6},{9,8},{10,9},{11,10},{12... | collective-permute-start | bytes 786440 | tf_op jit(solution)/shard_map/ppermute | solution.py:292
  179.0 12.3 %all_to_all.32 = f32[8,1,128]{2,1,0:T(1,128)S(1)} all-to-all(f32[8,1,128]{2,1,0:T(1,128)S(1)} %bitcast.14), channel_id=1, replica_groups=mesh['row_0'=8,'row_1'=2,'row_2'=2,'col'=8] {'col'}, dimensions={0} | all-to-all | bytes 8192 | tf_op jit(solution)/shard_map/all_to_all | solution.py:315
  191.3 0.5 multiply_sqrt_fusion
  191.8 0.0 collective-permute-done.6
  191.8 0.0 collective-permute-done.7
  191.8 0.1 broadcast_select_fusion.1
  191.9 0.9 pad_maximum_fusion
  (5 shorter events, 0.1 us)
Async XLA Ops:
  0.7 1.0 copy-start
  3.3 1.7 collective-permute-start
  26.9 17.7 %copy-start.1 = (f32[256,512]{1,0:T(8,128)S(1)}, f32[256,512]{1,0:T(8,128)}, u32[]{:S(2)}) copy-start(f32[256,512]{1,0:T(8,128)} %refs_3_.1) | copy-start | bytes 1572868
  43.0 1.6 collective-permute-start.1
  79.8 11.7 %collective-permute-start.4 = (f32[256,256]{1,0:T(8,128)S(1)}, f32[256,256]{1,0:T(8,128)S(1)}, u32[]{:S(2)}, u32[]{:S(2)}) collective-permute-start(f32[256,256]{1,0:T(8,128)S(1)} %get-tuple-element.27), channel_id=1, source_target_pairs={{0,1},{1,2},{2,3},{3,4},{4,5},{5,6},{6,7},{8,9},{9,10},{10,11},{11... | collective-permute-start | bytes 786440 | tf_op jit(solution)/shard_map/ppermute | solution.py:292
  84.1 14.0 %collective-permute-start.5 = (f32[256,256]{1,0:T(8,128)S(1)}, f32[256,256]{1,0:T(8,128)S(1)}, u32[]{:S(2)}, u32[]{:S(2)}) collective-permute-start(f32[256,256]{1,0:T(8,128)S(1)} %get-tuple-element.28), channel_id=1, source_target_pairs={{1,0},{2,1},{3,2},{4,3},{5,4},{6,5},{7,6},{9,8},{10,9},{11,10},{12... | collective-permute-start | bytes 786440 | tf_op jit(solution)/shard_map/ppermute | solution.py:292
  116.2 26.0 %all-to-all-start.3 = ((f32[32,16,128]{2,1,0:T(8,128)}), f32[32,16,128]{2,1,0:T(8,128)S(1)}, u32[]{:S(2)}, u32[]{:S(2)}) async-start(f32[32,16,128]{2,1,0:T(8,128)} %broadcast_in_dim.7), calls=%async_computation.3 | async-start | bytes 524288 | tf_op jit(solution)/shard_map/all_to_all | solution.py:277
  120.4 12.2 %collective-permute-start.3 = (f32[384,128]{1,0:T(8,128)S(1)}, f32[384,128]{1,0:T(8,128)S(1)}, u32[]{:S(2)}, u32[]{:S(2)}) collective-permute-start(f32[384,128]{1,0:T(8,128)S(1)} %get-tuple-element.23), channel_id=1, source_target_pairs={{0,1},{1,2},{2,3},{3,4},{4,5},{5,6},{6,7},{8,9},{9,10},{10,11},{11... | collective-permute-start | bytes 589832 | tf_op jit(solution)/shard_map/ppermute | solution.py:292
  124.7 17.6 %collective-permute-start.2 = (f32[384,128]{1,0:T(8,128)S(1)}, f32[384,128]{1,0:T(8,128)S(1)}, u32[]{:S(2)}, u32[]{:S(2)}) collective-permute-start(f32[384,128]{1,0:T(8,128)S(1)} %get-tuple-element.22), channel_id=1, source_target_pairs={{1,0},{2,1},{3,2},{4,3},{5,4},{6,5},{7,6},{9,8},{10,9},{11,10},{12... | collective-permute-start | bytes 589832 | tf_op jit(solution)/shard_map/ppermute | solution.py:292
  171.6 20.2 %collective-permute-start.6 = (f32[256,256]{1,0:T(8,128)S(1)}, f32[256,256]{1,0:T(8,128)S(1)}, u32[]{:S(2)}, u32[]{:S(2)}) collective-permute-start(f32[256,256]{1,0:T(8,128)S(1)} %get-tuple-element.33), channel_id=1, source_target_pairs={{0,1},{1,2},{2,3},{3,4},{4,5},{5,6},{6,7},{8,9},{9,10},{10,11},{11... | collective-permute-start | bytes 786440 | tf_op jit(solution)/shard_map/ppermute | solution.py:292
  177.1 14.8 %collective-permute-start.7 = (f32[256,256]{1,0:T(8,128)S(1)}, f32[256,256]{1,0:T(8,128)S(1)}, u32[]{:S(2)}, u32[]{:S(2)}) collective-permute-start(f32[256,256]{1,0:T(8,128)S(1)} %get-tuple-element.34), channel_id=1, source_target_pairs={{1,0},{2,1},{3,2},{4,3},{5,4},{6,5},{7,6},{9,8},{10,9},{11,10},{12... | collective-permute-start | bytes 786440 | tf_op jit(solution)/shard_map/ppermute | solution.py:292

commit v6 on v5

--- a/solution.py
+++ b/solution.py
@@ -89,27 +89,32 @@
     half=jax.ShapeDtypeStruct((5*T,T),F32)
     return pl.pallas_call(gram_kernel,out_shape=[half]*2,in_specs=[SM,VM],out_specs=[VM]*2,
         scratch_shapes=[pltpu.VMEM((10*T,T),F32)],compiler_params=pltpu.CompilerParams(vmem_limit_bytes=16 * 2**20),name="gram")(ends,pair)
-def cross_kernel(ends_ref,top_ref,from_left_ref,from_right_ref,pair_ref,c_ref):
-    own=top_ref[...]
-    top=jnp.where(ends_ref[0]==1,own,from_left_ref[...])
-    bottom=jnp.where(ends_ref[1]==1,own,from_right_ref[...])
+def cross_kernel(ends_ref,keep_ref,far_ref,edge_ref,pair_ref,hold_ref,give_ref):
+    edge=edge_ref[...]
+    top=jnp.where(ends_ref[1]==1,edge,keep_ref[...])
+    bottom=jnp.where(ends_ref[3]==1,edge,far_ref[...])
     pair_ref[:,:H]=top
     pair_ref[:,H:]=bottom
-    for i in range(2):
-        rows=dot(top[:,i*T:(i+1)*T],bottom,0,0)
-        c_ref[2*i*T:(2*i+1)*T,:]=rows[:,:T]
-        c_ref[(2*i+1)*T:(2*i+2)*T,:]=rows[:,T:]
-def local_cross(ends,top,from_left,from_right):
-    return pl.pallas_call(cross_kernel,out_shape=[jax.ShapeDtypeStruct((256,512),F32),jax.ShapeDtypeStruct((4*T,T),F32)],
-        in_specs=[SM,VM,VM,VM],out_specs=[VM]*2,compiler_params=pltpu.CompilerParams(vmem_limit_bytes=16 * 2**20),name="cross")(ends,top,from_left,from_right)
+    low=ends_ref[2]==0
+    upper=dot(top[:,:T],bottom,0,0)
+    lower=dot(top[:,T:],bottom,0,0)
+    hold=jnp.where(low,upper,lower)
+    give=jnp.where(low,lower,upper)
+    for j in range(2):
+        hold_ref[j*T:(j+1)*T,:]=hold[:,j*T:(j+1)*T]
+        give_ref[j*T:(j+1)*T,:]=give[:,j*T:(j+1)*T]
+def local_cross(*operands):
+    half=jax.ShapeDtypeStruct((2*T,T),F32)
+    return pl.pallas_call(cross_kernel,out_shape=[jax.ShapeDtypeStruct((256,512),F32),half,half],
+        in_specs=[SM,VM,VM,VM],out_specs=[VM]*3,compiler_params=pltpu.CompilerParams(vmem_limit_bytes=16 * 2**20),name="cross")(*operands)
 def spread_leaves(d_ref,u_ref,i_ref,count):
     us,is_=leaves([[d_ref[a,8*q:8*q+8,:] for q in range(T//8)] for a in range(count)])
     for a in range(count):
         for q in range(T//8):
             u_ref[a,8*q:8*q+8,:]=us[a][q]
             i_ref[a,8*q:8*q+8,:]=is_[a][q]
-def early_kernel(ends_ref,own_ref,own_left_ref,up_ref,inv_ref,d_ref,u_ref,i_ref):
-    g=jnp.where(ends_ref[0]==1,own_ref[...],own_left_ref[...])
+def early_kernel(ends_ref,own_keep_ref,own_edge_ref,up_ref,inv_ref,d_ref,u_ref,i_ref):
+    g=jnp.where(ends_ref[1]==1,own_edge_ref[...],own_keep_ref[...])
     d_ref[0]=g[:T]
     up_ref[T:2*T,:]=g[T:2*T]
     inv_ref[T:2*T,:]=g[2*T:]
@@ -144,11 +149,11 @@
     return jnp.broadcast_to(jnp.sum(cpl,axis=1,keepdims=True),(8,T))
 def rotate_kernel(first,*refs):
     if first:
-        ends_ref,half_ref,rest_ref,pair_ref,top_ref,bottom_ref,right_ref,own_top_ref,own_bottom_ref,own_right_ref,cpl_ref=refs[:11]
+        ends_ref,half_ref,rest_ref,pair_ref,top_ref,bottom_ref,pick_ref,own_top_ref,own_bottom_ref,own_pick_ref,cpl_ref=refs[:11]
         refs=refs[11:]
     else:
-        ends_ref,own_ref,own_from_right_ref,up_ref,inv_ref,g_ref,pair_ref,term_ref,top_ref,bottom_ref,right_ref,cpl_ref=refs[:12]
-        refs=refs[12:]
+        ends_ref,own_edge_ref,own_far_ref,up_ref,inv_ref,half_ref,rest_ref,pair_ref,term_ref,top_ref,bottom_ref,pick_ref,cpl_ref=refs[:13]
+        refs=refs[13:]
     A,U,V,W,RT,d_ref,u_ref,i_ref=refs
     sub=lax.broadcasted_iota(jnp.int32,(T,T),0); lane=lax.broadcasted_iota(jnp.int32,(T,T),1)
     eye=sub==lane
@@ -198,12 +203,13 @@
         down=[down_of(A[tile((n,n))]) for n in (0,1)]
         skip=0
     else:
-        own_bottom=jnp.where(ends_ref[1]==1,own_ref[...],own_from_right_ref[...])
+        own_bottom=jnp.where(ends_ref[3]==1,own_edge_ref[...],own_far_ref[...])
         for n in range(3):
             A[tile(BOTTOM[n])]=own_bottom[n*T:(n+1)*T]
             U[tile(TOP[n])]=up_ref[n*T:(n+1)*T,:]
         for n,ij in enumerate(CROSS):
-            A[tile(ij)]=g_ref[n*T:(n+1)*T,:]
+            m=(n%2)*T
+            A[tile(ij)]=jnp.where(ends_ref[2]==n//2,half_ref[m:m+T,:],rest_ref[m:m+T,:])
         sq=[jnp.sum(up_ref[n*T:(n+1)*T,:]*up_ref[n*T:(n+1)*T,:],axis=0,keepdims=True) for n in range(3)]
         down=[down_of(sq[0]),down_of(sq[1]+sq[2])]
         skip=2
@@ -243,8 +249,8 @@
     top,bottom=turned[:,:H],turned[:,H:]
     top_ref[...]=top
     bottom_ref[...]=bottom
-    at_start=ends_ref[0]==1
-    right_ref[...]=jnp.where(at_start,bottom,top)
+    swap=ends_ref[0 if first else 1]==1
+    pick_ref[...]=jnp.where(swap,bottom,top)
     if first:
         def packed(ref,lo):
             a=dot(V[lo:lo+T,lo:],V[lo:lo+H,lo:],1,1)
@@ -254,7 +260,7 @@
             ref[2*T:,:]=b
         packed(own_top_ref,0)
         packed(own_bottom_ref,H)
-        own_right_ref[...]=jnp.where(at_start,own_bottom_ref[...],own_top_ref[...])
+        own_pick_ref[...]=jnp.where(swap,own_bottom_ref[...],own_top_ref[...])
 def rotate(first,*operands):
     block=jax.ShapeDtypeStruct((256,H),F32)
     own=jax.ShapeDtypeStruct((3*T,T),F32)
@@ -286,39 +292,46 @@
     return half, swapped(half)
 
 
-def moved(value, steps):
+def moved(value, steps, sources):
     count = lax.axis_size("col")
-    first, last = max(0, -steps), min(count, count - steps)
-    return lax.ppermute(value, "col", [(source, source + steps) for source in range(first, last)])
+    return lax.ppermute(value, "col", [(i % count, (i + steps) % count) for i in sources])
+
+
+def carried(value, links):
+    return lax.ppermute(value, "col", links)
 
 
 def steps(matrix):
     place = lax.axis_index("col")
-    at_start = place == 0
-    at_end = place == lax.axis_size("col") - 1
-    ends = jnp.stack([at_start, at_end, lax.axis_index("row_2")]).astype(jnp.int32)
+    count = lax.axis_size("col")
+    last = count - 1
+    ends = jnp.stack(
+        [place == 0, place == last, lax.axis_index("row_2"), place == last - 1]
+    ).astype(jnp.int32)
     half, rest = row_halves(*local_gram(ends, matrix))
-    top, bottom, right, own_top, own_bottom, own_right, term_0 = rotate(
+    top, bottom, keep, own_top, own_bottom, own_keep, term_0 = rotate(
         True, ends, half, rest, matrix
     )
-    from_left = moved(right, 1)
-    from_right = moved(bottom, -1)
-    own_left = moved(own_right, 1)
-    own_from_right = moved(own_bottom, -1)
-    pair, cross = local_cross(ends, top, from_left, from_right)
-    cross = scattered_sum(cross, ROW)
-    cross = gathered(cross, ROW)
-    up, inverse = early(ends, own_top, own_left)
-    top, bottom, right, terms = rotate(
-        False, ends, own_top, own_from_right, up, inverse, cross, pair, term_0
-    )
+    edges = [(last, last - 1), (0, last)]
+    far = moved(bottom, -2, range(1, count))
+    edge = carried(top, edges)
+    own_far = moved(own_bottom, -2, range(1, count))
+    own_edge = carried(own_top, edges)
+    pair, hold, give = local_cross(ends, keep, far, edge)
+    cross = scattered_sum(hold + swapped(give), CHIPS)
+    cross = gathered(cross, CHIPS)
+    cross_rest = swapped(cross)
+    up, inverse = early(ends, own_keep, own_edge)
+    top, bottom, pick, terms = rotate(
+        False, ends, own_edge, own_far, up, inverse, cross, cross_rest, pair, term_0
+    )
+    far = moved(pick, 2, [*range(last - 1), last])
+    edge = carried(top, [(last - 1, last), (last, 0)])
     terms = lax.all_to_all(terms, "col", split_axis=0, concat_axis=0, tiled=True)
-    from_left = moved(right, 1)
-    from_right = moved(bottom, -1)
     totals = jnp.sum(terms, axis=0)[:STEPS]
-    coupling = jnp.sqrt(totals / (1.0 * lax.axis_size("col") * H))
+    coupling = jnp.sqrt(totals / (1.0 * count * H))
     rotated = jnp.concatenate(
-        [jnp.where(at_start, top, from_left), jnp.where(at_end, top, from_right)], axis=1
+        [jnp.where(place == 0, edge, far), jnp.where(place == last, edge, bottom)], axis=1
     )
     return (rotated, coupling)
 
@@ -328,4 +341,6 @@
         mesh.devices.reshape(8, 2, 2, mesh.shape["col"]), ("row_0", "row_1", "row_2", "col")
     )
     placed = (P(ROW, "col"),)
-    return jax.shard_map(steps, mesh=split, in_specs=placed, out_specs=(P(ROW, "col"), P()), check_vma=False)
+    return jax.shard_map(
+        steps, mesh=split, in_specs=placed, out_specs=(P(ROW, "col"), P()), check_vma=False
+    )

time: 195 us -> 189 us (0.969)
  starting transfers between devices: 26.3 us -> 20.6 us
  blocking collectives: 66.5 us -> 69.3 us
  waiting for transfers between devices: 19.1 us -> 16.4 us
    ppermute x6, starting transfers between devices: 22.1 us -> 15.7 us  [the longest x3 13.7 us: moved(): lax.ppermute(value, 'col', [(i % count, (i + steps) % count) for i in sou...]
    all_to_all x1, blocking collectives: 12.3 us -> 18.4 us  [steps(): lax.all_to_all(terms, 'col', split_axis=0, concat_axis=0, tiled=True)]
    ppermute x6, waiting for transfers between devices: 15.8 us -> 10.8 us  [the longest x3 10.8 us: moved(): lax.ppermute(value, 'col', [(i % count, (i + steps) % count) for i in sou...]
    all_to_all x2, blocking collectives: 38.2 us -> 34.9 us  [scattered_sum(): parts = lax.all_to_all(value.reshape(count, -1, T), axis, 0, 0, tiled=True)]
    ppermute x2 -> x4, waiting for transfers between devices: 3.24 us -> 4.58 us  [swapped(): return lax.ppermute(value, 'row_2', [(0, 1), (1, 0)])]
  transfers between devices with their start and end apart: 9 -> 11, of which waited for: 5 -> 5; matrix products, arithmetic and copies ran while one was open for 0% -> 0% of each run, Pallas kernels for 5% -> 5%
where the time goes in v6:
time: 189 us; the launch traced here: 187 us
  Pallas kernels  76.7 us (41%)
  blocking collectives  69.3 us (37%)
  starting transfers between devices  20.6 us (11%)
  waiting for transfers between devices  16.4 us (9%)
    pallas_call x2, Pallas kernels, rotate(): pl.pallas_call(functools.partial(rotate_kernel, first), out_shape=outs, i...  64.5 us
    all_to_all x2, blocking collectives, scattered_sum(): parts = lax.all_to_all(value.reshape(count, -1, T), axis, 0, 0, tiled=True)  34.9 us
    all_to_all x1, blocking collectives, steps(): lax.all_to_all(terms, 'col', split_axis=0, concat_axis=0, tiled=True)  18.4 us
    all_to_all x1, blocking collectives, gathered(): lax.all_to_all(copies, axis, split_axis=0, concat_axis=0, tiled=True)  16 us
    ppermute x3, starting transfers between devices, moved(): lax.ppermute(value, 'col', [(i % count, (i + steps) % count) for i in sou...  13.7 us
    ppermute x3, waiting for transfers between devices, moved(): lax.ppermute(value, 'col', [(i % count, (i + steps) % count) for i in sou...  10.8 us
    pallas_call x1, Pallas kernels, early(): pl.pallas_call(early_kernel, out_shape=[own] * 2, in_specs=[SM, VM, VM],...  9.74 us
    all_to_all x1, starting transfers between devices, gathered(): lax.all_to_all(copies, axis, split_axis=0, concat_axis=0, tiled=True)  4.77 us
  transfers between devices with their start and end apart: 11, of which 5 were waited for; matrix products, arithmetic and copies ran while one was open for 0% of the time, Pallas kernels for 5%

profile of v6, /device:TPU:6, one launch (start us, length us, event | category | flops | bytes accessed | tf_op | source)
XLA Modules:
  0.0 187.2 jit_solution(13315602087752066725)
XLA Ops:
  0.6 0.1 pad_add_fusion.ends_ref.refs_0_
  0.7 0.0 copy-start
  0.7 1.0 copy-done
  1.8 1.5 gram.1
  3.3 0.1 collective-permute-start
  3.4 1.6 collective-permute-done
  5.0 21.9 %all_to_all.29 = f32[16,40,128]{2,1,0:T(8,128)S(1)} all-to-all(f32[16,40,128]{2,1,0:T(8,128)S(1)} %bitcast.16), channel_id=1, replica_groups=mesh['row_0'=8,'row_1'=2,'row_2'=2,'col'=8] {'row_0','row_1'}, dimensions={0} | all-to-all | bytes 655360 | tf_op jit(solution)/shard_map/all_to_all | solution.py:277
  26.9 0.0 copy-start.1
  27.0 16.0 %all_to_all.30 = f32[16,40,128]{2,1,0:T(8,128)S(1)} all-to-all(f32[16,40,128]{2,1,0:T(8,128)S(1)} %broadcast_in_dim.6), channel_id=1, replica_groups=mesh['row_0'=8,'row_1'=2,'row_2'=2,'col'=8] {'row_0','row_1'}, dimensions={0} | all-to-all | bytes 655360 | tf_op jit(solution)/shard_map/all_to_all | solution.py:283
  43.0 0.0 collective-permute-start.1
  43.0 1.6 collective-permute-done.1.refs_2_
  44.7 0.0 copy-done.1
  44.7 35.2 %rotate.2 = (f32[256,256]{1,0:T(8,128)S(1)}, f32[256,256]{1,0:T(8,128)S(1)}, f32[256,256]{1,0:T(8,128)S(1)}, f32[384,128]{1,0:T(8,128)S(1)}, f32[384,128]{1,0:T(...) custom-call(s32[4]{0:T(128)S(1)} %pad_add_fusion.ends_ref.refs_0_, f32[640,128]{1,0:T(8,128)S(1)} %bitcast.12, ...), custom_call_target="tpu_custom_call" | custom-call | flops 4000000000 | bytes 2000000 | tf_op jit(solution)/shard_map/rotate/pallas_call | solution.py:268
  79.8 4.9 %collective-permute-start.4 = (f32[256,256]{1,0:T(8,128)S(1)}, f32[256,256]{1,0:T(8,128)S(1)}, u32[]{:S(2)}, u32[]{:S(2)}) collective-permute-start(f32[256,256]{1,0:T(8,128)S(1)} %get-tuple-element.28), channel_id=1, source_target_pairs={{1,7},{2,0},{3,1},{4,2},{5,3},{6,4},{7,5},{9,15},{10,8},{11,9},{12... | collective-permute-start | bytes 786440 | tf_op jit(solution)/shard_map/ppermute | solution.py:297
  84.7 0.7 collective-permute-start.5
  85.4 10.8 %collective-permute-done.4.far_ref = f32[256,256]{1,0:T(8,128)S(1)} collective-permute-done((f32[256,256]{1,0:T(8,128)S(1)}, f32[256,256]{1,0:T(8,128)S(1)}, u32[]{:S(2)}, u32[]{:S(2)}) %collective-permute-start.4) | collective-permute-done | bytes 262176 | tf_op jit(solution)/shard_map/ppermute | solution.py:297
  96.2 0.0 collective-permute-done.5.edge_ref
  96.2 1.0 cross.1
  97.2 0.1 collective-permute-start.6
  97.3 1.3 collective-permute-done.6
  98.7 13.0 %all_to_all.31 = f32[16,16,128]{2,1,0:T(8,128)S(1)} all-to-all(f32[16,16,128]{2,1,0:T(8,128)S(1)} %bitcast.17), channel_id=1, replica_groups=mesh['row_0'=8,'row_1'=2,'row_2'=2,'col'=8] {'row_0','row_1'}, dimensions={0} | all-to-all | bytes 262144 | tf_op jit(solution)/shard_map/all_to_all | solution.py:277
  111.7 0.7 broadcast_in_dim.7
  112.4 4.8 %all-to-all-start.3 = ((f32[16,16,128]{2,1,0:T(8,128)}), f32[16,16,128]{2,1,0:T(8,128)S(1)}, u32[]{:S(2)}, u32[]{:S(2)}) async-start(f32[16,16,128]{2,1,0:T(8,128)} %broadcast_in_dim.7), calls=%async_computation.3 | async-start | bytes 262144 | tf_op jit(solution)/shard_map/all_to_all | solution.py:283
  117.1 0.7 collective-permute-start.2
  117.8 6.8 %collective-permute-start.3 = (f32[384,128]{1,0:T(8,128)S(1)}, f32[384,128]{1,0:T(8,128)S(1)}, u32[]{:S(2)}, u32[]{:S(2)}) collective-permute-start(f32[384,128]{1,0:T(8,128)S(1)} %get-tuple-element.23), channel_id=1, source_target_pairs={{1,7},{2,0},{3,1},{4,2},{5,3},{6,4},{7,5},{9,15},{10,8},{11,9},{12... | collective-permute-start | bytes 589832 | tf_op jit(solution)/shard_map/ppermute | solution.py:297
  124.6 1.0 all-to-all-done.3
  125.6 0.0 collective-permute-start.7
  125.6 0.0 collective-permute-done.2.own_edge_ref.refs_1_
  125.6 9.7 %early.1 = (f32[384,128]{1,0:T(8,128)S(1)}, f32[384,128]{1,0:T(8,128)S(1)}) custom-call(s32[4]{0:T(128)S(1)} %pad_add_fusion.ends_ref.refs_0_, f32[384,128]{1,0:T(8,128)S(1)} %get-tuple-element.24.own_keep_ref, f32[384,128]{1,0:T(8,128)S(1)} %collective-permute-done.2.own_edge_ref.refs_1_), custom_call_target="tpu_custom_call" | custom-call | flops 500000000 | bytes 1000000 | tf_op jit(solution)/shard_map/early/pallas_call | solution.py:139
  135.4 0.0 collective-permute-done.3.refs_2_
  135.4 0.0 collective-permute-done.7.refs_6_
  135.4 29.4 %rotate.3 = (f32[256,256]{1,0:T(8,128)S(1)}, f32[256,256]{1,0:T(8,128)S(1)}, f32[256,256]{1,0:T(8,128)S(1)}, f32[8,128]{1,0:T(8,128)S(1)}) custom-call(s32[4]{0:T(128)S(1)} %pad_add_fusion.ends_ref.refs_0_, f32[384,128]{1,0:T(8,128)S(1)} %collective-permute-done.2.own_edge_ref.refs_1_, f32[384,128]{1,0:T(8,128)S(1)} %collective-permute-done.3.refs_2_, ...), custom_call_target="tpu_custom_call" | custom-call | flops 4000000000 | bytes 2000000 | tf_op jit(solution)/shard_map/rotate/pallas_call | solution.py:268
  164.8 0.7 collective-permute-start.8
  165.4 1.9 %collective-permute-start.9 = (f32[256,256]{1,0:T(8,128)S(1)}, f32[256,256]{1,0:T(8,128)S(1)}, u32[]{:S(2)}, u32[]{:S(2)}) collective-permute-start(f32[256,256]{1,0:T(8,128)S(1)} %get-tuple-element.35), channel_id=1, source_target_pairs={{0,2},{1,3},{2,4},{3,5},{4,6},{5,7},{7,1},{8,10},{9,11},{10,12},{1... | collective-permute-start | bytes 786440 | tf_op jit(solution)/shard_map/ppermute | solution.py:297
  167.4 18.4 %all_to_all.32 = f32[8,1,128]{2,1,0:T(1,128)S(1)} all-to-all(f32[8,1,128]{2,1,0:T(1,128)S(1)} %bitcast.15), channel_id=1, replica_groups=mesh['row_0'=8,'row_1'=2,'row_2'=2,'col'=8] {'col'}, dimensions={0} | all-to-all | bytes 8192 | tf_op jit(solution)/shard_map/all_to_all | solution.py:330
  185.8 0.5 multiply_sqrt_fusion
  186.3 0.0 collective-permute-done.8
  186.3 0.0 collective-permute-done.9
  186.3 0.1 broadcast_select_fusion.1
  186.4 0.9 pad_maximum_fusion
  (6 shorter events, 0.1 us)
Async XLA Ops:
  0.7 1.0 copy-start
  3.3 1.7 collective-permute-start
  26.9 17.7 %copy-start.1 = (f32[256,512]{1,0:T(8,128)S(1)}, f32[256,512]{1,0:T(8,128)}, u32[]{:S(2)}) copy-start(f32[256,512]{1,0:T(8,128)} %refs_3_.1) | copy-start | bytes 1572868
  43.0 1.6 collective-permute-start.1
  79.8 16.4 %collective-permute-start.4 = (f32[256,256]{1,0:T(8,128)S(1)}, f32[256,256]{1,0:T(8,128)S(1)}, u32[]{:S(2)}, u32[]{:S(2)}) collective-permute-start(f32[256,256]{1,0:T(8,128)S(1)} %get-tuple-element.28), channel_id=1, source_target_pairs={{1,7},{2,0},{3,1},{4,2},{5,3},{6,4},{7,5},{9,15},{10,8},{11,9},{12... | collective-permute-start | bytes 786440 | tf_op jit(solution)/shard_map/ppermute | solution.py:297
  84.7 11.5 %collective-permute-start.5 = (f32[256,256]{1,0:T(8,128)S(1)}, f32[256,256]{1,0:T(8,128)S(1)}, u32[]{:S(2)}, u32[]{:S(2)}) collective-permute-start(f32[256,256]{1,0:T(8,128)S(1)} %get-tuple-element.29), channel_id=1, source_target_pairs={{7,6},{0,7},{15,14},{8,15},{23,22},{16,23},{31,30},{24,31},{39,38}... | collective-permute-start | bytes 786440 | tf_op jit(solution)/shard_map/ppermute | solution.py:301
  97.2 1.4 collective-permute-start.6
  112.4 13.2 %all-to-all-start.3 = ((f32[16,16,128]{2,1,0:T(8,128)}), f32[16,16,128]{2,1,0:T(8,128)S(1)}, u32[]{:S(2)}, u32[]{:S(2)}) async-start(f32[16,16,128]{2,1,0:T(8,128)} %broadcast_in_dim.7), calls=%async_computation.3 | async-start | bytes 262144 | tf_op jit(solution)/shard_map/all_to_all | solution.py:283
  117.1 8.5 %collective-permute-start.2 = (f32[384,128]{1,0:T(8,128)S(1)}, f32[384,128]{1,0:T(8,128)S(1)}, u32[]{:S(2)}, u32[]{:S(2)}) collective-permute-start(f32[384,128]{1,0:T(8,128)S(1)} %get-tuple-element.22), channel_id=1, source_target_pairs={{7,6},{0,7},{15,14},{8,15},{23,22},{16,23},{31,30},{24,31},{39,38}... | collective-permute-start | bytes 589832 | tf_op jit(solution)/shard_map/ppermute | solution.py:301
  117.8 17.6 %collective-permute-start.3 = (f32[384,128]{1,0:T(8,128)S(1)}, f32[384,128]{1,0:T(8,128)S(1)}, u32[]{:S(2)}, u32[]{:S(2)}) collective-permute-start(f32[384,128]{1,0:T(8,128)S(1)} %get-tuple-element.23), channel_id=1, source_target_pairs={{1,7},{2,0},{3,1},{4,2},{5,3},{6,4},{7,5},{9,15},{10,8},{11,9},{12... | collective-permute-start | bytes 589832 | tf_op jit(solution)/shard_map/ppermute | solution.py:297
  125.6 9.8 %collective-permute-start.7 = (f32[256,128]{1,0:T(8,128)S(1)}, f32[256,128]{1,0:T(8,128)S(1)}, u32[]{:S(2)}, u32[]{:S(2)}) collective-permute-start(f32[256,128]{1,0:T(8,128)S(1)} %bitcast.13), channel_id=1, source_target_pairs={{0,8},{8,0},{1,9},{9,1},{2,10},{10,2},{3,11},{11,3},{4,12},{12,4},... | collective-permute-start | bytes 393224 | tf_op jit(solution)/shard_map/ppermute | solution.py:287
  164.8 21.5 %collective-permute-start.8 = (f32[256,256]{1,0:T(8,128)S(1)}, f32[256,256]{1,0:T(8,128)S(1)}, u32[]{:S(2)}, u32[]{:S(2)}) collective-permute-start(f32[256,256]{1,0:T(8,128)S(1)} %get-tuple-element.34), channel_id=1, source_target_pairs={{6,7},{7,0},{14,15},{15,8},{22,23},{23,16},{30,31},{31,24},{38,39}... | collective-permute-start | bytes 786440 | tf_op jit(solution)/shard_map/ppermute | solution.py:301
  165.4 20.9 %collective-permute-start.9 = (f32[256,256]{1,0:T(8,128)S(1)}, f32[256,256]{1,0:T(8,128)S(1)}, u32[]{:S(2)}, u32[]{:S(2)}) collective-permute-start(f32[256,256]{1,0:T(8,128)S(1)} %get-tuple-element.35), channel_id=1, source_target_pairs={{0,2},{1,3},{2,4},{3,5},{4,6},{5,7},{7,1},{8,10},{9,11},{10,12},{1... | collective-permute-start | bytes 786440 | tf_op jit(solution)/shard_map/ppermute | solution.py:297
